TPU v7x, 256 devices: a whole 4x4x8 slice. The times are simulated.
256 devices in a mesh: patch: 16 (over x_hi, z), depth: 16 (over y, x_lo, core).
Axes of the slice: x: 4 (x_hi: 2, x_lo: 2; x = x_hi * 2 + x_lo), y: 4, z: 8, core: 2. Of those that a mesh axis runs over, the one named last changes fastest.
Arguments:
- slabs: bfloat16 [16, 32, 16, 32, 384], P('patch', 'depth'), may hold values from -12 to 12, as said below
- kernel: bfloat16 [3, 3, 3, 384, 384], P(None, None, None, None, 'patch'), may hold values from -0.0625 to 0.0625
- gain: float32 [384], replicated, may hold values from 0.25 to 1.75
- shift: float32 [384], replicated, may hold values from -3 to 3
Outputs:
- activated: bfloat16 [16, 32, 16, 32, 384], P('patch', 'depth')
Inputs may be any that keep to these rules, and one draw needn't show every extreme that they name: `slabs`: feature values of order one.
All inputs are finite; a program needn't handle non-finite values.
Results may differ from a plain program's by a relative error of at most 0.001.
Values may be sent and summed in bfloat16 or wider, within the bound.
No kernel may reach another device: no remote copies, remote signals or barrier semaphores. Data moves between devices by JAX's collectives and lax.ppermute only.
A program may use at most 384 MiB of HBM per device.

v0:
```python
import jax
import jax.numpy as jnp
from jax import lax
from jax.sharding import PartitionSpec as P


def with_halo(cells, sides, width):
    for axis, dim in sides:
        count = lax.axis_size(axis)
        ends = count - 1
        head = lax.slice_in_dim(cells, 0, width, axis=dim)
        tail = lax.slice_in_dim(cells, cells.shape[dim] - width, cells.shape[dim], axis=dim)
        cells = jnp.concatenate(
            [
                lax.ppermute(tail, axis, [(i, (i + 1) % count) for i in range(ends)]),
                cells,
                lax.ppermute(head, axis, [((i + 1) % count, i) for i in range(ends)]),
            ],
            axis=dim,
        )
    return cells


def conv_taps(volume, weights):
    planes = volume.shape[1] - 2
    height = volume.shape[2]
    width = volume.shape[3]
    padded = jnp.pad(volume, ((0, 0), (0, 0), (1, 1), (1, 1), (0, 0)))
    total = jnp.zeros((volume.shape[0], planes, height, width, weights.shape[4]), jnp.float32)
    for tap_a in range(3):
        for tap_b in range(3):
            for tap_e in range(3):
                window = padded[
                    :, tap_a : tap_a + planes, tap_b : tap_b + height, tap_e : tap_e + width, :
                ]
                total = total + jnp.einsum(
                    "pzhwc,co->pzhwo",
                    window,
                    weights[tap_a, tap_b, tap_e],
                    preferred_element_type=jnp.float32,
                )
    return total


def normalize(conv_out, gain_part, shift_part):
    sums = jnp.sum(conv_out, axis=(1, 2, 3))
    squares = jnp.sum(conv_out * conv_out, axis=(1, 2, 3))
    sums, squares = lax.psum((sums, squares), "depth")
    cells = conv_out.shape[1] * lax.axis_size("depth") * conv_out.shape[2] * conv_out.shape[3]
    mean = sums / cells
    variance = squares / cells - mean * mean
    scaled = gain_part / jnp.sqrt(variance + 1e-05)
    normed = (conv_out - mean[:, None, None, None, :]) * scaled[:, None, None, None, :] + shift_part
    return jnp.where(normed >= 0, normed, 0.01 * normed).astype(jnp.bfloat16)


def local(slabs, kernel, gain, shift):
    faced = with_halo(slabs, (("depth", 1),), 1)
    conv_out = conv_taps(faced, lax.all_gather(kernel, "patch", axis=4, tiled=True))
    return normalize(conv_out, gain, shift)


def solution(mesh):
    in_specs = (P("patch", "depth", None, None, None), P(None, None, None, None, "patch"), P(), P())
    out_specs = P("patch", "depth", None, None, None)
    return jax.shard_map(local, mesh=mesh, in_specs=in_specs, out_specs=out_specs, check_vma=False)
```

profile of v0, /device:TPU:1, one launch (start us, length us, event | category | flops | bytes accessed | tf_op | source)
XLA Modules:
  0.0 240.8 jit_solution(6454747968138920003)
XLA Ops:
  8.5 4.5 %collective-permute-start = (bf16[1,1,16,32,384]{4,3,2,1,0:T(8,128)(2,1)S(1)}, bf16[1,1,16,32,384]{4,3,2,1,0:T(8,128)(2,1)S(1)}, u32[]{:S(2)}, u32[]{:S(2)}) collective-permute-start(bf16[1,1,16,32,384]{4,3,2,1,0:T(8,128)(2,1)S(1)} %get-tuple-element.11), channel_id=1, source_target_pairs={{0,1},{1,2},{2,3},{3,4},{4,5},{5,6},{6,7},{7,8},{8,9},{9,10},{10,1... | collective-permute-start | bytes 1179656 | tf_op jit(solution)/shard_map/ppermute | solution.py:15
  13.0 2.0 collective-permute-start.1
  14.9 2.7 %collective-permute-done = bf16[1,1,16,32,384]{4,3,2,1,0:T(8,128)(2,1)S(1)} collective-permute-done((bf16[1,1,16,32,384]{4,3,2,1,0:T(8,128)(2,1)S(1)}, bf16[1,1,16,32,384]{4,3,2,1,0:T(8,128)(2,1)S(1)}, u32[]{:S(2)}, u32[]{:S(2)}) %collective-permute-start) | collective-permute-done | bytes 393248 | tf_op jit(solution)/shard_map/ppermute | solution.py:15
  17.7 5.9 %collective-permute-done.1 = bf16[1,1,16,32,384]{4,3,2,1,0:T(8,128)(2,1)S(1)} collective-permute-done((bf16[1,1,16,32,384]{4,3,2,1,0:T(8,128)(2,1)S(1)}, bf16[1,1,16,32,384]{4,3,2,1,0:T(8,128)(2,1)S(1)}, u32[]{:S(2)}, u32[]{:S(2)}) %collective-permute-start.1) | collective-permute-done | bytes 393248 | tf_op jit(solution)/shard_map/ppermute | solution.py:17
  26.1 119.1 %all-gather.2.cloned.1.call-done = bf16[3,3,3,384,384]{3,4,2,1,0:T(8,128)(2,1)} async-done(((bf16[3,3,3,384,24]{3,4,2,1,0:T(8,128)(2,1)}), bf16[3,3,3,384,384]{3,4,2,1,0:T(8,128)(2,1)}) %all-gather.2.cloned.1.call-update) | async-done | bytes 7962640 | tf_op jit(solution)/shard_map/all_gather | solution.py:59
  145.2 1.9 fusion.12
  147.1 2.1 fusion.32
  151.4 1.8 fusion.10
  153.9 1.9 fusion.16
  155.8 1.8 fusion.17
  159.4 1.8 fusion.19
  161.3 1.8 fusion.20
  164.9 1.8 fusion.22
  168.5 1.9 fusion.24
  170.4 1.8 fusion.25
  172.2 1.9 fusion.26
  175.9 1.9 fusion.28
  179.5 2.0 fusion.30
  183.3 1.8 fusion.36
  186.9 1.8 fusion.38
  188.7 1.8 fusion.39
  190.5 13.1 %fusion.43 = (f32[384]{0:T(512)S(1)}, f32[384]{0:T(512)S(1)}, f32[2,16,32,384]{3,2,1,0:T(8,128)}) fusion(bf16[3,3,3,384,384]{3,4,2,1,0:T(8,128)(2,1)} %all-gather.2.cloned.1.call-done, bf16[1,4,18,34,384]{4,3,2,1,0:T(8,128)(2,1)S(1)} %select_maximum_fusion, f32[2,16,32,384]{3,2,1,0:T(8,128)S(1)} %fusion.8, f32[2,16,32,384]{3,2,1,0:T(8,128)S(1)} %fusion.9, ...), kind=kOutput, calls=%fused_computation.105 | convolution fusion | flops 313392384 | bytes 43551744 | tf_op jit(solution)/shard_map/pzhwc,co->pzhwo/dot_general | solution.py:36
  203.7 27.6 %all-reduce.1 = (f32[1,384]{1,0:T(1,128)S(1)}, f32[1,384]{1,0:T(1,128)S(1)}) all-reduce(f32[1,384]{1,0:T(1,128)S(1)} %reduce_sum.23, f32[1,384]{1,0:T(1,128)S(1)} %reduce_sum.25), channel_id=1, replica_groups=mesh['patch'=16,'depth'=16] {'depth'}, use_global_device_ids=true, to_apply=%region_1.2 | all-reduce | flops 768 | bytes 6144 | tf_op jit(solution)/shard_map/psum | solution.py:48
  231.3 2.6 %fusion.7 = bf16[1,2,16,32,384]{4,3,2,1,0:T(8,128)(2,1)} fusion(f32[2,16,32,384]{3,2,1,0:T(8,128)} %get-tuple-element.13, f32[384]{0:T(512)S(1)} %copy-done.4, f32[384]{0:T(512)S(1)} %get-tuple-element.8, f32[384]{0:T(512)S(1)} %get-tuple-element.7), kind=kLoop, calls=%fused_computation.16 | loop fusion | flops 2752512 | bytes 2363904 | tf_op jit(solution)/shard_map/convert_element_type | solution.py:54
  (27 shorter events, 19.9 us)
Async XLA Ops:
  6.5 17.8 %copy-start = (bf16[1,2,16,32,384]{4,3,2,1,0:T(8,128)(2,1)S(1)}, bf16[1,2,16,32,384]{4,3,2,1,0:T(8,128)(2,1)}, u32[]{:S(2)}) copy-start(bf16[1,2,16,32,384]{4,3,2,1,0:T(8,128)(2,1)} %param.4) | copy-start | bytes 2359300
  6.5 138.6 %all-gather.2.cloned.1.call-start = ((), (), s32[]{:S(2)}) async-start(), calls=%async_computation | async-start | bytes 8460288 | tf_op jit(solution)/shard_map/all_gather | solution.py:59
  8.5 9.2 %collective-permute-start = (bf16[1,1,16,32,384]{4,3,2,1,0:T(8,128)(2,1)S(1)}, bf16[1,1,16,32,384]{4,3,2,1,0:T(8,128)(2,1)S(1)}, u32[]{:S(2)}, u32[]{:S(2)}) collective-permute-start(bf16[1,1,16,32,384]{4,3,2,1,0:T(8,128)(2,1)S(1)} %get-tuple-element.11), channel_id=1, source_target_pairs={{0,1},{1,2},{2,3},{3,4},{4,5},{5,6},{6,7},{7,8},{8,9},{9,10},{10,1... | collective-permute-start | bytes 1179656 | tf_op jit(solution)/shard_map/ppermute | solution.py:15
  13.0 10.6 %collective-permute-start.1 = (bf16[1,1,16,32,384]{4,3,2,1,0:T(8,128)(2,1)S(1)}, bf16[1,1,16,32,384]{4,3,2,1,0:T(8,128)(2,1)S(1)}, u32[]{:S(2)}, u32[]{:S(2)}) collective-permute-start(bf16[1,1,16,32,384]{4,3,2,1,0:T(8,128)(2,1)S(1)} %get-tuple-element.12), channel_id=1, source_target_pairs={{1,0},{2,1},{3,2},{4,3},{5,4},{6,5},{7,6},{8,7},{9,8},{10,9},{11,1... | collective-permute-start | bytes 1179656 | tf_op jit(solution)/shard_map/ppermute | solution.py:17
  23.6 0.7 copy-start.2
  145.2 5.6 %copy-start.1 = (bf16[3,3,3,384,384]{3,4,2,1,0:T(8,128)(2,1)S(1)}, bf16[3,3,3,384,384]{3,4,2,1,0:T(8,128)(2,1)}, u32[]{:S(2)}) copy-start(bf16[3,3,3,384,384]{3,4,2,1,0:T(8,128)(2,1)} %all-gather.2.cloned.1.call-done) | copy-start | bytes 23887876
  190.5 40.8 %copy-start.3 = (f32[384]{0:T(512)S(1)}, f32[384]{0:T(512)}, u32[]{:S(2)}) copy-start(f32[384]{0:T(512)} %param.6) | copy-start | bytes 4612
  190.5 40.8 %copy-start.4 = (f32[384]{0:T(512)S(1)}, f32[384]{0:T(512)}, u32[]{:S(2)}) copy-start(f32[384]{0:T(512)} %param.7) | copy-start | bytes 4612
Sparse Core Ops, SparseCore 0:
  10.1 135.0 all-gather.1
where the time goes:
time: 241 us
  waiting for transfers between devices  128 us (53%)
  matrix products  58.4 us (24%)
  blocking collectives  27.6 us (11%)
  between operations  13.5 us (6%)
  starting transfers between devices  6.47 us (3%)
  other arithmetic  4.43 us (2%)
    all_gather x1, waiting for transfers between devices, local(): lax.all_gather(kernel, 'patch', axis=4, tiled=True)  119 us
    dot_general x27, matrix products, conv_taps(): jnp.einsum('pzhwc,co->pzhwo', window, weights[tap_a, tap_b, tap_e], prefe...  58.4 us
    psum x1, blocking collectives, normalize(): sums, squares = lax.psum((sums, squares), 'depth')  27.6 us
    ppermute x1, waiting for transfers between devices, with_halo(): lax.ppermute(head, axis, [((i + 1) % count, i) for i in range(ends)])  5.92 us
  transfers between devices with their start and end apart: 3, of which 3 were waited for; matrix products, arithmetic and copies ran while one was open for 1% of the time, Pallas kernels for 0%

commit v1 on v0

v1 whole, which is shorter than its diff:
```python
import functools

import jax
import jax.numpy as jnp
from jax import lax
from jax.experimental import pallas as pl
from jax.experimental.pallas import tpu as pltpu
from jax.sharding import Mesh, PartitionSpec as P

AXES = ("xh", "z", "y", "xl", "c")
SIZES = (2, 8, 4, 2, 2)
CHIPS = ("y", "xl")
DEPTH = ("y", "xl", "c")
SWAP = [(0, 1), (1, 0)]
EPS = 1e-05


def shift_rows(plane, by, width):
    rows = plane.shape[0]
    moved = pltpu.roll(plane, by % rows, 0)
    w = lax.broadcasted_iota(jnp.int32, plane.shape, 0) % width
    edge = 0 if by == 1 else width - 1
    return jnp.where(w == edge, 0.0, moved)


def widen_kernel(x_ref, o_ref, *, width):
    x = x_ref[0]
    rows, chans = x.shape
    zero = jnp.zeros((width, 3 * chans), o_ref.dtype)
    o_ref[0, 0:width, :] = zero
    o_ref[0, width + rows : 2 * width + rows, :] = zero
    wide = x.astype(jnp.float32)
    o_ref[0, width : width + rows, 0:chans] = shift_rows(wide, 1, width).astype(o_ref.dtype)
    o_ref[0, width : width + rows, chans : 2 * chans] = x
    o_ref[0, width : width + rows, 2 * chans : 3 * chans] = shift_rows(wide, -1, width).astype(o_ref.dtype)


def widen(planes, width):
    count, rows, chans = planes.shape
    return pl.pallas_call(
        functools.partial(widen_kernel, width=width),
        grid=(count,),
        in_specs=[pl.BlockSpec((1, rows, chans), lambda i: (i, 0, 0))],
        out_specs=pl.BlockSpec((1, rows + 2 * width, 3 * chans), lambda i: (i, 0, 0)),
        out_shape=jax.ShapeDtypeStruct((count, rows + 2 * width, 3 * chans), planes.dtype),
        compiler_params=pltpu.CompilerParams(vmem_limit_bytes=32 << 20),
        cost_estimate=pl.CostEstimate(flops=0, bytes_accessed=12_000_000, transcendentals=0),
    )(planes)


def conv_kernel(core_ref, x_ref, w_ref, send_ref, keep_ref, stats_ref, acc_ref, *, rows, width):
    del core_ref
    j, a = pl.program_id(0), pl.program_id(1)
    lhs = jnp.concatenate([x_ref[0, b * width : b * width + rows, :] for b in range(3)], axis=1)
    rhs = jnp.concatenate([w_ref[0, t] for t in range(9)], axis=1)
    part = lax.dot_general(lhs, rhs, (((1,), (1,)), ((), ())), preferred_element_type=jnp.float32)

    @pl.when(a == 0)
    def _():
        acc_ref[...] = part

    @pl.when(a == 1)
    def _():
        acc_ref[...] += part

    @pl.when((j == 0) & (a == 0))
    def _():
        stats_ref[...] = jnp.zeros_like(stats_ref)

    @pl.when(a == 2)
    def _():
        total = acc_ref[...] + part
        stats_ref[0:1, :] += jnp.sum(total, axis=0, keepdims=True)
        stats_ref[1:2, :] += jnp.sum(total * total, axis=0, keepdims=True)

        @pl.when(j < 2)
        def _():
            send_ref[0] = total

        @pl.when(j >= 2)
        def _():
            keep_ref[0] = total


def conv(core, wide, weights, rows, width):
    outs = weights.shape[2]
    part = jax.ShapeDtypeStruct((2, rows, outs), jnp.float32)
    spec = pltpu.PrefetchScalarGridSpec(
        num_scalar_prefetch=1,
        grid=(4, 3),
        in_specs=[
            pl.BlockSpec((1, wide.shape[1], wide.shape[2]), lambda j, a, core: ((j + 2 * (1 - core[0])) % 4 + a, 0, 0)),
            pl.BlockSpec((1, 9, outs, weights.shape[3]), lambda j, a, core: (a, 0, 0, 0)),
        ],
        out_specs=[
            pl.BlockSpec((1, rows, outs), lambda j, a, core: (jnp.minimum(j, 1), 0, 0)),
            pl.BlockSpec((1, rows, outs), lambda j, a, core: (jnp.maximum(j - 2, 0), 0, 0)),
            pl.BlockSpec((8, outs), lambda j, a, core: (0, 0)),
        ],
        scratch_shapes=[pltpu.VMEM((rows, outs), jnp.float32)],
    )
    return pl.pallas_call(
        functools.partial(conv_kernel, rows=rows, width=width),
        grid_spec=spec,
        out_shape=[part, part, jax.ShapeDtypeStruct((8, outs), jnp.float32)],
        compiler_params=pltpu.CompilerParams(vmem_limit_bytes=40 << 20),
        cost_estimate=pl.CostEstimate(flops=8 * 10**9, bytes_accessed=16_000_000, transcendentals=0),
    )(core, wide, weights)


def norm_kernel(core_ref, keep_ref, recv_ref, sums_ref, gain_ref, shift_ref, o_ref, *, cells):
    first = core_ref[0] == 0
    outs = keep_ref.shape[2]
    keep, recv = keep_ref[0], recv_ref[0]
    for half in range(2):
        mean = sums_ref[half, 0:1, :] / cells
        variance = sums_ref[half, 1:2, :] / cells - mean * mean
        scale = gain_ref[half] / jnp.sqrt(variance + EPS)
        conv_out = jnp.where(first, keep, recv) if half == 0 else jnp.where(first, recv, keep)
        normed = (conv_out - mean) * scale + shift_ref[half]
        active = jnp.where(normed >= 0, normed, 0.01 * normed).astype(o_ref.dtype)
        o_ref[0, :, half * outs : (half + 1) * outs] = active


def normalize(core, keep, recv, sums, gain, shift, cells):
    planes, rows, outs = keep.shape
    tile = 256
    spec = pltpu.PrefetchScalarGridSpec(
        num_scalar_prefetch=1,
        grid=(planes, rows // tile),
        in_specs=[
            pl.BlockSpec((1, tile, outs), lambda i, j, core: (i, j, 0)),
            pl.BlockSpec((1, tile, outs), lambda i, j, core: (i, j, 0)),
            pl.BlockSpec((2, 2, outs), lambda i, j, core: (0, 0, 0)),
            pl.BlockSpec((2, 1, outs), lambda i, j, core: (0, 0, 0)),
            pl.BlockSpec((2, 1, outs), lambda i, j, core: (0, 0, 0)),
        ],
        out_specs=pl.BlockSpec((1, tile, 2 * outs), lambda i, j, core: (i, j, 0)),
    )
    return pl.pallas_call(
        functools.partial(norm_kernel, cells=cells),
        grid_spec=spec,
        out_shape=jax.ShapeDtypeStruct((planes, rows, 2 * outs), jnp.bfloat16),
        compiler_params=pltpu.CompilerParams(vmem_limit_bytes=32 << 20),
        cost_estimate=pl.CostEstimate(flops=4_000_000, bytes_accessed=3_000_000, transcendentals=0),
    )(core, keep, recv, sums, gain, shift)


def chip_planes(slab, core):
    other = lax.ppermute(slab, "c", SWAP)
    inner = jnp.where(core == 0, jnp.concatenate([slab, other]), jnp.concatenate([other, slab]))
    chips = SIZES[2] * SIZES[3]
    before = lax.ppermute(inner[3:], CHIPS, [(i, i + 1) for i in range(chips - 1)])
    after = lax.ppermute(inner[:1], CHIPS, [(i + 1, i) for i in range(chips - 1)])
    return jnp.concatenate([before, inner, after])


def x_exchange(shard, core):
    pairs = []
    for xl in range(2):
        low, high = (0 + xl) * 2 + 1, (2 + 1 - xl) * 2
        pairs += [(low, high), (high, low)]
    other = lax.ppermute(shard, ("xh", "xl", "c"), pairs)
    return jnp.where(core == lax.axis_index("xh"), shard, other)


def local(slabs, kernel, gain, shift):
    core = lax.axis_index("c")
    core_arg = core.reshape(1).astype(jnp.int32)
    _, planes, height, width, chans = slabs.shape
    rows = height * width
    outs = chans // 2

    shard = jnp.transpose(kernel, (0, 1, 2, 4, 3)).reshape(27, kernel.shape[4], chans)
    half = lax.all_gather(x_exchange(shard, core), "z", axis=1, tiled=True)
    weights = half.reshape(3, 9, outs, chans)

    wide = widen(chip_planes(slabs[0].reshape(planes, rows, chans), core), width)
    send, keep, stats = conv(core_arg, wide, weights, rows, width)

    recv = lax.ppermute(send, "c", SWAP)
    mine = stats[:2].reshape(1, 2 * outs)
    group = SIZES[2] * SIZES[3] * SIZES[4]
    everyone = lax.all_to_all(jnp.broadcast_to(mine, (group, 2 * outs)), DEPTH, 0, 0)
    sums = jnp.sum(everyone.reshape(group // 2, 2, 2, outs), axis=0)
    cells = planes * rows * group
    out = normalize(
        core_arg, keep, recv, sums, gain.reshape(2, 1, outs), shift.reshape(2, 1, outs), cells
    )
    return out.reshape(slabs.shape)


def solution(mesh):
    fine = Mesh(mesh.devices.reshape(SIZES), AXES)
    x_spec = P(("xh", "z"), DEPTH, None, None, None)
    in_specs = (x_spec, P(None, None, None, None, ("xh", "z")), P(), P())
    return jax.shard_map(local, mesh=fine, in_specs=in_specs, out_specs=x_spec, check_vma=False)
```

time: 241 us -> 121 us (0.50)
  waiting for transfers between devices: 128 us -> 59.3 us
  matrix products: 58.4 us -> 0 us
  blocking collectives: 27.6 us -> 0 us
  Pallas kernels: 0 us -> 18.2 us
  local copies, waits for them, and re-layouts: 1.96 us -> 11.3 us
  starting transfers between devices: 6.47 us -> 15.2 us
    all_gather x1, waiting for transfers between devices: 119 us -> 25.8 us  [local(): half = lax.all_gather(x_exchange(shard, core), 'z', axis=1, tiled=True)]
    dot_general x27 -> x0, matrix products: 58.4 us -> none  [conv_taps(): jnp.einsum('pzhwc,co->pzhwo', window, weights[tap_a, tap_b, tap_e], prefe...]
    psum x1 -> x0, blocking collectives: 27.6 us -> none  [normalize(): sums, squares = lax.psum((sums, squares), 'depth')]
    ppermute x2 -> x5, waiting for transfers between devices: 8.66 us -> 27.9 us  [the longest x1 11.8 us: chip_planes(): lax.ppermute(inner[:1], CHIPS, [(i + 1, i) for i in range(chips - 1)])]
    pallas_call x0 -> x3, Pallas kernels: none -> 18.2 us  [the longest x1 14.7 us: conv(): pl.pallas_call(functools.partial(conv_kernel, rows=rows, width=width), gr...]
    unnamed x10 -> x12, local copies, waits for them, and re-layouts: 0.76 us -> 8.47 us
    all_to_all x0 -> x1, waiting for transfers between devices: none -> 5.62 us  [local(): lax.all_to_all(jnp.broadcast_to(mine, (group, 2 * outs)), DEPTH, 0, 0)]
    all_to_all x0 -> x1, starting transfers between devices: none -> 5.31 us  [local(): lax.all_to_all(jnp.broadcast_to(mine, (group, 2 * outs)), DEPTH, 0, 0)]
  transfers between devices with their start and end apart: 3 -> 7, of which waited for: 3 -> 6; matrix products, arithmetic and copies ran while one was open for 1% -> 1% of each run, Pallas kernels for 0% -> 1%
where the time goes in v1:
time: 121 us; the launch traced here: 120 us
  waiting for transfers between devices  59.3 us (49%)
  Pallas kernels  18.2 us (15%)
  starting transfers between devices  15.2 us (13%)
  between operations  13.5 us (11%)
  local copies, waits for them, and re-layouts  11.3 us (9%)
  other arithmetic  2.57 us (2%)
    all_gather x1, waiting for transfers between devices, local(): half = lax.all_gather(x_exchange(shard, core), 'z', axis=1, tiled=True)  25.8 us
    pallas_call x1, Pallas kernels, conv(): pl.pallas_call(functools.partial(conv_kernel, rows=rows, width=width), gr...  14.7 us
    ppermute x1, waiting for transfers between devices, chip_planes(): lax.ppermute(inner[:1], CHIPS, [(i + 1, i) for i in range(chips - 1)])  11.8 us
    unnamed x12, local copies, waits for them, and re-layouts  8.47 us
    ppermute x1, waiting for transfers between devices, chip_planes(): lax.ppermute(inner[3:], CHIPS, [(i, i + 1) for i in range(chips - 1)])  7.03 us
    ppermute x1, waiting for transfers between devices, x_exchange(): other = lax.ppermute(shard, ('xh', 'xl', 'c'), pairs)  6.77 us
    ppermute x1, starting transfers between devices, x_exchange(): other = lax.ppermute(shard, ('xh', 'xl', 'c'), pairs)  5.9 us
    all_to_all x1, waiting for transfers between devices, local(): lax.all_to_all(jnp.broadcast_to(mine, (group, 2 * outs)), DEPTH, 0, 0)  5.62 us
  transfers between devices with their start and end apart: 7, of which 6 were waited for; matrix products, arithmetic and copies ran while one was open for 1% of the time, Pallas kernels for 1%

profile of v1, /device:TPU:1, one launch (start us, length us, event | category | flops | bytes accessed | tf_op | source)
XLA Modules:
  0.0 120.1 jit_solution(12637461955174161997)
XLA Ops:
  6.5 5.9 %collective-permute-start.3 = (bf16[27,24,384]{2,1,0:T(8,128)(2,1)}, bf16[27,24,384]{2,1,0:T(8,128)(2,1)S(1)}, u32[]{:S(2)}, u32[]{:S(2)}) collective-permute-start(bf16[27,24,384]{2,1,0:T(8,128)(2,1)} %bitcast.11), channel_id=1, source_target_pairs={{1,130},{130,1},{3,128},{128,3},{5,134},{134,5},{7,132},{132,7},{9... | collective-permute-start | bytes 1493000 | tf_op jit(solution)/shard_map/ppermute | solution.py:163
  12.5 6.8 %collective-permute-done.3 = bf16[27,24,384]{2,1,0:T(8,128)(2,1)S(1)} collective-permute-done((bf16[27,24,384]{2,1,0:T(8,128)(2,1)}, bf16[27,24,384]{2,1,0:T(8,128)(2,1)S(1)}, u32[]{:S(2)}, u32[]{:S(2)}) %collective-permute-start.3) | collective-permute-done | bytes 497696 | tf_op jit(solution)/shard_map/ppermute | solution.py:163
  19.2 1.9 %broadcast_select_fusion = bf16[27,24,384]{2,1,0:T(8,128)(2,1)} fusion(bf16[27,24,384]{2,1,0:T(8,128)(2,1)S(1)} %collective-permute-done.3, pred[]{:T(512)S(6)} %eq.7, bf16[3,3,3,384,24]{3,4,2,1,0:T(8,128)(2,1)} %param.5), kind=kLoop, calls=%fused_computation.2 | loop fusion | flops 248832 | bytes 1492993 | tf_op jit(solution)/shard_map/jit(_where)/select_n | solution.py:164
  21.1 0.1 collective-permute-start
  21.2 2.3 %collective-permute-done = bf16[2,512,384]{2,1,0:T(8,128)(2,1)S(1)} collective-permute-done((bf16[2,512,384]{2,1,0:T(8,128)(2,1)S(1)}, bf16[2,512,384]{2,1,0:T(8,128)(2,1)S(1)}, u32[]{:S(2)}, u32[]{:S(2)}) %collective-permute-start) | collective-permute-done | bytes 786464 | tf_op jit(solution)/shard_map/ppermute | solution.py:150
  23.5 0.3 maximum_select_fusion
  23.9 1.9 %collective-permute-start.1 = (bf16[1,512,384]{2,1,0:T(8,128)(2,1)S(1)}, bf16[1,512,384]{2,1,0:T(8,128)(2,1)S(1)}, u32[]{:S(2)}, u32[]{:S(2)}) collective-permute-start(bf16[1,512,384]{2,1,0:T(8,128)(2,1)S(1)} %get-tuple-element.11), channel_id=1, source_target_pairs={{0,2},{2,4},{4,6},{6,8},{8,10},{10,12},{12,14},{1,3},{3,5},{5,7},{... | collective-permute-start | bytes 1179656 | tf_op jit(solution)/shard_map/ppermute | solution.py:153
  25.8 1.3 %collective-permute-start.2 = (bf16[1,512,384]{2,1,0:T(8,128)(2,1)S(1)}, bf16[1,512,384]{2,1,0:T(8,128)(2,1)S(1)}, u32[]{:S(2)}, u32[]{:S(2)}) collective-permute-start(bf16[1,512,384]{2,1,0:T(8,128)(2,1)S(1)} %get-tuple-element.12), channel_id=1, source_target_pairs={{2,0},{4,2},{6,4},{8,6},{10,8},{12,10},{14,12},{3,1},{5,3},{7,5},{... | collective-permute-start | bytes 1179656 | tf_op jit(solution)/shard_map/ppermute | solution.py:154
  27.1 7.0 %collective-permute-done.1 = bf16[1,512,384]{2,1,0:T(8,128)(2,1)S(1)} collective-permute-done((bf16[1,512,384]{2,1,0:T(8,128)(2,1)S(1)}, bf16[1,512,384]{2,1,0:T(8,128)(2,1)S(1)}, u32[]{:S(2)}, u32[]{:S(2)}) %collective-permute-start.1) | collective-permute-done | bytes 393248 | tf_op jit(solution)/shard_map/ppermute | solution.py:153
  34.1 11.8 %collective-permute-done.2 = bf16[1,512,384]{2,1,0:T(8,128)(2,1)S(1)} collective-permute-done((bf16[1,512,384]{2,1,0:T(8,128)(2,1)S(1)}, bf16[1,512,384]{2,1,0:T(8,128)(2,1)S(1)}, u32[]{:S(2)}, u32[]{:S(2)}) %collective-permute-start.2) | collective-permute-done | bytes 393248 | tf_op jit(solution)/shard_map/ppermute | solution.py:154
  45.9 0.3 pad_maximum_fusion.x_ref
  46.2 1.6 %shard_map.46.x_ref = bf16[6,576,1152]{2,1,0:T(8,128)(2,1)S(1)} custom-call(bf16[6,512,384]{2,1,0:T(8,128)(2,1)S(1)} %pad_maximum_fusion.x_ref), custom_call_target="tpu_custom_call" | custom-call | bytes 12000000 | tf_op jit(solution)/shard_map/pallas_call | solution.py:40
  47.9 3.1 %copy-done = bf16[6,576,1152]{2,1,0:T(8,128)(2,1)} copy-done((bf16[6,576,1152]{2,1,0:T(8,128)(2,1)}, bf16[6,576,1152]{2,1,0:T(8,128)(2,1)S(1)}, u32[]{:S(2)}) %copy-start) | copy-done | bytes 7962648
  50.9 25.8 %all-gather.2.cloned.1.call-done = bf16[27,192,384]{2,1,0:T(8,128)(2,1)} async-done(((bf16[27,24,384]{2,1,0:T(8,128)(2,1)}), bf16[27,192,384]{2,1,0:T(8,128)(2,1)}) %all-gather.2.cloned.1.call-update) | async-done | bytes 3981328 | tf_op jit(solution)/shard_map/all_gather | solution.py:175
  76.7 3.3 %copy-done.1 = bf16[6,576,1152]{2,1,0:T(8,128)(2,1)S(1)} copy-done((bf16[6,576,1152]{2,1,0:T(8,128)(2,1)S(1)}, bf16[6,576,1152]{2,1,0:T(8,128)(2,1)}, u32[]{:S(2)}) %copy-start.1) | copy-done | bytes 7962648
  80.0 2.1 %copy-done.2 = bf16[27,192,384]{2,1,0:T(8,128)(2,1)S(1)} copy-done((bf16[27,192,384]{2,1,0:T(8,128)(2,1)S(1)}, bf16[27,192,384]{2,1,0:T(8,128)(2,1)}, u32[]{:S(2)}) %copy-start.2) | copy-done | bytes 3981336
  82.1 14.7 %shard_map.47 = (f32[2,512,192]{2,1,0:T(8,128)S(1)}, f32[2,512,192]{2,1,0:T(8,128)S(1)}, f32[8,192]{1,0:T(8,128)S(1)}) custom-call(s32[1]{0:T(128)} %bitcast.core_ref, bf16[6,576,1152]{2,1,0:T(8,128)(2,1)S(1)} %copy-done.1, bf16[3,9,192,384]{3,2,1,0:T(8,128)(2,1)S(1)} %bitcast.8), custom_call_target="tpu_custom_call" | custom-call | flops 8000000000 | bytes 16000000 | tf_op jit(solution)/shard_map/pallas_call | solution.py:102
  96.8 0.3 copy.12
  97.2 0.8 collective-permute-start.4
  98.0 0.6 broadcast_in_dim.8
  98.6 5.3 %all-to-all-start = ((f32[16,1,384]{2,1,0:T(1,128)}), f32[16,1,384]{2,1,0:T(1,128)S(1)}, u32[]{:S(2)}, u32[]{:S(2)}) async-start(f32[16,1,384]{2,1,0:T(1,128)} %broadcast_in_dim.8), calls=%async_computation | async-start | bytes 49152 | tf_op jit(solution)/shard_map/all_to_all | solution.py:184
  104.1 5.6 %all-to-all-done = f32[16,1,384]{2,1,0:T(1,128)S(1)} async-done(((f32[16,1,384]{2,1,0:T(1,128)}), f32[16,1,384]{2,1,0:T(1,128)S(1)}, u32[]{:S(2)}, u32[]{:S(2)}) %all-to-all-start) | async-done | bytes 24608 | tf_op jit(solution)/shard_map/all_to_all | solution.py:184
  109.9 1.5 %copy.14.recv_ref = f32[2,512,192]{2,1,0:T(8,128)S(1)} copy(f32[2,512,192]{1,2,0:T(8,128)} %collective-permute-done.4) | data formatting | bytes 1572864 | tf_op jit(solution)/shard_map/ppermute | solution.py:181
  111.4 1.9 %shard_map.48 = bf16[2,512,384]{2,1,0:T(8,128)(2,1)} custom-call(s32[1]{0:T(128)} %bitcast.core_ref, f32[2,512,192]{2,1,0:T(8,128)S(1)} %get-tuple-element.8.keep_ref, f32[2,512,192]{2,1,0:T(8,128)S(1)} %copy.14.recv_ref, f32[2,2,192]{2,1,0:T(2,128)S(1)} %reduce_sum.9.sums_ref, f32[2,1,192]{2,1,0:T(1,128)S(1)} %reshape.35.gain_ref, ...), custom_call_target="tpu_custom_call" | custom-call | flops 4000000 | bytes 3000000 | tf_op jit(solution)/shard_map/pallas_call | solution.py:140
  (20 shorter events, 0.5 us)
Async XLA Ops:
  6.5 14.6 %copy-start.3 = (bf16[1,2,16,32,384]{4,3,2,1,0:T(8,128)(2,1)S(1)}, bf16[1,2,16,32,384]{4,3,2,1,0:T(8,128)(2,1)}, u32[]{:S(2)}) copy-start(bf16[1,2,16,32,384]{4,3,2,1,0:T(8,128)(2,1)} %param.4) | copy-start | bytes 2359300
  6.5 70.2 %all-gather.2.cloned.1.call-start = ((), (), s32[]{:S(2)}) async-start(), calls=%async_computation.1 | async-start | bytes 4478976 | tf_op jit(solution)/shard_map/all_gather | solution.py:175
  6.5 12.7 %collective-permute-start.3 = (bf16[27,24,384]{2,1,0:T(8,128)(2,1)}, bf16[27,24,384]{2,1,0:T(8,128)(2,1)S(1)}, u32[]{:S(2)}, u32[]{:S(2)}) collective-permute-start(bf16[27,24,384]{2,1,0:T(8,128)(2,1)} %bitcast.11), channel_id=1, source_target_pairs={{1,130},{130,1},{3,128},{128,3},{5,134},{134,5},{7,132},{132,7},{9... | collective-permute-start | bytes 1493000 | tf_op jit(solution)/shard_map/ppermute | solution.py:163
  21.1 2.4 %collective-permute-start = (bf16[2,512,384]{2,1,0:T(8,128)(2,1)S(1)}, bf16[2,512,384]{2,1,0:T(8,128)(2,1)S(1)}, u32[]{:S(2)}, u32[]{:S(2)}) collective-permute-start(bf16[2,512,384]{2,1,0:T(8,128)(2,1)S(1)} %bitcast.9), channel_id=1, source_target_pairs={{0,1},{1,0},{2,3},{3,2},{4,5},{5,4},{6,7},{7,6},{8,9},{9,8},{10,11... | collective-permute-start | bytes 2359304 | tf_op jit(solution)/shard_map/ppermute | solution.py:150
  23.9 10.2 %collective-permute-start.1 = (bf16[1,512,384]{2,1,0:T(8,128)(2,1)S(1)}, bf16[1,512,384]{2,1,0:T(8,128)(2,1)S(1)}, u32[]{:S(2)}, u32[]{:S(2)}) collective-permute-start(bf16[1,512,384]{2,1,0:T(8,128)(2,1)S(1)} %get-tuple-element.11), channel_id=1, source_target_pairs={{0,2},{2,4},{4,6},{6,8},{8,10},{10,12},{12,14},{1,3},{3,5},{5,7},{... | collective-permute-start | bytes 1179656 | tf_op jit(solution)/shard_map/ppermute | solution.py:153
  25.8 20.1 %collective-permute-start.2 = (bf16[1,512,384]{2,1,0:T(8,128)(2,1)S(1)}, bf16[1,512,384]{2,1,0:T(8,128)(2,1)S(1)}, u32[]{:S(2)}, u32[]{:S(2)}) collective-permute-start(bf16[1,512,384]{2,1,0:T(8,128)(2,1)S(1)} %get-tuple-element.12), channel_id=1, source_target_pairs={{2,0},{4,2},{6,4},{8,6},{10,8},{12,10},{14,12},{3,1},{5,3},{7,5},{... | collective-permute-start | bytes 1179656 | tf_op jit(solution)/shard_map/ppermute | solution.py:154
  47.9 3.1 %copy-start = (bf16[6,576,1152]{2,1,0:T(8,128)(2,1)}, bf16[6,576,1152]{2,1,0:T(8,128)(2,1)S(1)}, u32[]{:S(2)}) copy-start(bf16[6,576,1152]{2,1,0:T(8,128)(2,1)S(1)} %shard_map.46.x_ref) | copy-start | bytes 23887876
  76.7 3.3 %copy-start.1 = (bf16[6,576,1152]{2,1,0:T(8,128)(2,1)S(1)}, bf16[6,576,1152]{2,1,0:T(8,128)(2,1)}, u32[]{:S(2)}) copy-start(bf16[6,576,1152]{2,1,0:T(8,128)(2,1)} %copy-done) | copy-start | bytes 23887876
  80.0 2.1 %copy-start.2 = (bf16[27,192,384]{2,1,0:T(8,128)(2,1)S(1)}, bf16[27,192,384]{2,1,0:T(8,128)(2,1)}, u32[]{:S(2)}) copy-start(bf16[27,192,384]{2,1,0:T(8,128)(2,1)} %all-gather.2.cloned.1.call-done) | copy-start | bytes 11943940
  96.8 7.1 %copy-start.4 = (f32[384]{0:T(512)S(1)}, f32[384]{0:T(512)}, u32[]{:S(2)}) copy-start(f32[384]{0:T(512)} %param.6) | copy-start | bytes 4612
  96.8 7.2 %copy-start.5 = (f32[384]{0:T(512)S(1)}, f32[384]{0:T(512)}, u32[]{:S(2)}) copy-start(f32[384]{0:T(512)} %param.7) | copy-start | bytes 4612
  97.2 12.8 %collective-permute-start.4 = (f32[2,512,192]{1,2,0:T(8,128)S(1)}, f32[2,512,192]{1,2,0:T(8,128)}, u32[]{:S(2)}, u32[]{:S(2)}) collective-permute-start(f32[2,512,192]{1,2,0:T(8,128)S(1)} %copy.12), channel_id=1, source_target_pairs={{0,1},{1,0},{2,3},{3,2},{4,5},{5,4},{6,7},{7,6},{8,9},{9,8},{10,11... | collective-permute-start | bytes 2359304 | tf_op jit(solution)/shard_map/ppermute | solution.py:181
  98.6 11.1 %all-to-all-start = ((f32[16,1,384]{2,1,0:T(1,128)}), f32[16,1,384]{2,1,0:T(1,128)S(1)}, u32[]{:S(2)}, u32[]{:S(2)}) async-start(f32[16,1,384]{2,1,0:T(1,128)} %broadcast_in_dim.8), calls=%async_computation | async-start | bytes 49152 | tf_op jit(solution)/shard_map/all_to_all | solution.py:184
Sparse Core Ops, SparseCore 0:
  21.2 55.4 all-gather.1

commit v2 on v1

v2 whole, which is shorter than its diff:
```python
import functools
import math

import jax
import jax.numpy as jnp
from jax import lax
from jax.experimental import pallas as pl
from jax.experimental.pallas import tpu as pltpu
from jax.sharding import Mesh, PartitionSpec as P

AXES = ("xh", "z", "y", "xl", "c")
SIZES = (2, 8, 4, 2, 2)
CHIPS = ("y", "xl")
DEPTH = ("y", "xl", "c")
SWAP = [(0, 1), (1, 0)]
EPS = 1e-05
PADDED = 256
QUARTER_START = (0, 7, 14, 20)


def quarter_of(tap):
    return min(tap // 7, 3)


def shift_rows(plane, by, width):
    rows = plane.shape[0]
    moved = pltpu.roll(plane, by % rows, 0)
    w = lax.broadcasted_iota(jnp.int32, plane.shape, 0) % width
    edge = 0 if by == 1 else width - 1
    return jnp.where(w == edge, 0.0, moved)


def widen_kernel(x_ref, o_ref, *, width):
    x = x_ref[0]
    rows, chans = x.shape
    zero = jnp.zeros((width, 3 * chans), o_ref.dtype)
    o_ref[0, 0:width, :] = zero
    o_ref[0, width + rows : 2 * width + rows, :] = zero
    wide = x.astype(jnp.float32)
    o_ref[0, width : width + rows, 0:chans] = shift_rows(wide, 1, width).astype(o_ref.dtype)
    o_ref[0, width : width + rows, chans : 2 * chans] = x
    o_ref[0, width : width + rows, 2 * chans : 3 * chans] = shift_rows(wide, -1, width).astype(o_ref.dtype)


def widen(planes, width):
    count, rows, chans = planes.shape
    return pl.pallas_call(
        functools.partial(widen_kernel, width=width),
        grid=(count,),
        in_specs=[pl.BlockSpec((1, rows, chans), lambda i: (i, 0, 0))],
        out_specs=pl.BlockSpec((1, rows + 2 * width, 3 * chans), lambda i: (i, 0, 0)),
        out_shape=jax.ShapeDtypeStruct((count, rows + 2 * width, 3 * chans), planes.dtype),
        compiler_params=pltpu.CompilerParams(vmem_limit_bytes=32 << 20),
        cost_estimate=pl.CostEstimate(flops=0, bytes_accessed=12_000_000, transcendentals=0),
    )(planes)


def conv_kernel(ids_ref, x_ref, *refs, rows, width):
    pieces, (send_ref, keep_ref, stats_ref, w_ref, sum_ref, sems) = refs[:8], refs[8:]
    core, colour = ids_ref[0], ids_ref[1]
    j = pl.program_id(0)
    outs = keep_ref.shape[2]

    @pl.when(j == 0)
    def _():
        copies = []
        for s in range(4):
            for h in range(2):
                dst = w_ref.at[s, :, h * outs // 2 : (h + 1) * outs // 2, :]
                copies.append(pltpu.make_async_copy(pieces[2 * s + h], dst, sems.at[2 * s + h]))
        for copy in copies:
            copy.start()
        for copy in copies:
            copy.wait()
        sum_ref[...] = jnp.zeros_like(sum_ref)

    plane = (j + 2 * (1 - core)) % 4
    total = None
    for a in range(3):
        taps = [(quarter_of(t), t - QUARTER_START[quarter_of(t)]) for t in range(9 * a, 9 * a + 9)]
        rhs = jnp.concatenate([w_ref[jnp.bitwise_xor(colour, q), i] for q, i in taps], axis=1)
        lhs = jnp.concatenate([x_ref[plane + a, b * width : b * width + rows, :] for b in range(3)], axis=1)
        part = lax.dot_general(lhs, rhs, (((1,), (1,)), ((), ())), preferred_element_type=jnp.float32)
        total = part if total is None else total + part
    sum_ref[0:1, :] += jnp.sum(total, axis=0, keepdims=True)
    sum_ref[1:2, :] += jnp.sum(total * total, axis=0, keepdims=True)

    @pl.when(j < 2)
    def _():
        send_ref[0, :, 0:outs] = total
        send_ref[0, :, outs:] = jnp.zeros((rows, send_ref.shape[2] - outs), jnp.float32)

    @pl.when(j >= 2)
    def _():
        keep_ref[0] = total

    @pl.when(j == 3)
    def _():
        row = jnp.concatenate([sum_ref[0:1, :], sum_ref[1:2, :]], axis=1)
        stats_ref[...] = jnp.broadcast_to(row, stats_ref.shape)


def conv(ids, wide, pieces, rows, width, group):
    taps, half, chans = pieces[0].shape
    outs = 2 * half
    spec = pltpu.PrefetchScalarGridSpec(
        num_scalar_prefetch=1,
        grid=(4,),
        in_specs=[pl.BlockSpec(memory_space=pltpu.VMEM)] + [pl.BlockSpec(memory_space=pl.ANY)] * 8,
        out_specs=[
            pl.BlockSpec((1, rows, PADDED), lambda j, ids: (jnp.minimum(j, 1), 0, 0)),
            pl.BlockSpec((1, rows, outs), lambda j, ids: (jnp.maximum(j - 2, 0), 0, 0)),
            pl.BlockSpec((group, 2 * outs), lambda j, ids: (0, 0)),
        ],
        scratch_shapes=[
            pltpu.VMEM((4, taps, outs, chans), jnp.bfloat16),
            pltpu.VMEM((8, outs), jnp.float32),
            pltpu.SemaphoreType.DMA((8,)),
        ],
    )
    return pl.pallas_call(
        functools.partial(conv_kernel, rows=rows, width=width),
        grid_spec=spec,
        out_shape=[
            jax.ShapeDtypeStruct((2, rows, PADDED), jnp.float32),
            jax.ShapeDtypeStruct((2, rows, outs), jnp.float32),
            jax.ShapeDtypeStruct((group, 2 * outs), jnp.float32),
        ],
        compiler_params=pltpu.CompilerParams(vmem_limit_bytes=40 << 20),
        cost_estimate=pl.CostEstimate(flops=8 * 10**9, bytes_accessed=16_000_000, transcendentals=0),
    )(ids, wide, *pieces)


def norm_kernel(ids_ref, keep_ref, recv_ref, stats_ref, gain_ref, shift_ref, o_ref, *, cells):
    first = ids_ref[0] == 0
    outs = keep_ref.shape[2]
    keep, recv = keep_ref[0], recv_ref[0, :, 0:outs]
    for half in range(2):
        sums = stats_ref[half : half + 1, :]
        for chip in range(1, stats_ref.shape[0] // 2):
            sums = sums + stats_ref[2 * chip + half : 2 * chip + half + 1, :]
        mean = sums[:, 0:outs] / cells
        variance = sums[:, outs : 2 * outs] / cells - mean * mean
        scale = gain_ref[half] / jnp.sqrt(variance + EPS)
        conv_out = jnp.where(first, keep, recv) if half == 0 else jnp.where(first, recv, keep)
        normed = (conv_out - mean) * scale + shift_ref[half]
        active = jnp.where(normed >= 0, normed, 0.01 * normed).astype(o_ref.dtype)
        o_ref[0, :, half * outs : (half + 1) * outs] = active


def normalize(ids, keep, recv, stats, gain, shift, cells):
    planes, rows, outs = keep.shape
    tile = 256
    spec = pltpu.PrefetchScalarGridSpec(
        num_scalar_prefetch=1,
        grid=(planes, rows // tile),
        in_specs=[
            pl.BlockSpec((1, tile, outs), lambda i, j, ids: (i, j, 0)),
            pl.BlockSpec((1, tile, PADDED), lambda i, j, ids: (i, j, 0)),
            pl.BlockSpec(stats.shape, lambda i, j, ids: (0, 0)),
            pl.BlockSpec((2, 1, outs), lambda i, j, ids: (0, 0, 0)),
            pl.BlockSpec((2, 1, outs), lambda i, j, ids: (0, 0, 0)),
        ],
        out_specs=pl.BlockSpec((1, tile, 2 * outs), lambda i, j, ids: (i, j, 0)),
    )
    return pl.pallas_call(
        functools.partial(norm_kernel, cells=cells),
        grid_spec=spec,
        out_shape=jax.ShapeDtypeStruct((planes, rows, 2 * outs), jnp.bfloat16),
        compiler_params=pltpu.CompilerParams(vmem_limit_bytes=32 << 20),
        cost_estimate=pl.CostEstimate(flops=4_000_000, bytes_accessed=3_000_000, transcendentals=0),
    )(ids, keep, recv, stats, gain, shift)


def join_kernel(ids_ref, *refs):
    pieces, (low_ref, high_ref, sems) = refs[:8], refs[8:]
    step = pieces[0].shape[1]
    z = ids_ref[2]
    for r in range(8):
        where = jnp.remainder(z - r + 8, 8)
        rows = pl.ds(pl.multiple_of(jnp.remainder(where, 4) * step, 8), step)

        @pl.when(where < 4)
        def _():
            pltpu.make_async_copy(pieces[r], low_ref.at[:, rows, :], sems.at[r]).start()

        @pl.when(where >= 4)
        def _():
            pltpu.make_async_copy(pieces[r], high_ref.at[:, rows, :], sems.at[r]).start()

    for r in range(8):
        pltpu.make_async_copy(pieces[r], low_ref.at[:, pl.ds(0, step), :], sems.at[r]).wait()


def join(ids, pieces):
    taps, step, chans = pieces[0].shape
    part = jax.ShapeDtypeStruct((taps, 4 * step, chans), jnp.bfloat16)
    spec = pltpu.PrefetchScalarGridSpec(
        num_scalar_prefetch=1,
        grid=(),
        in_specs=[pl.BlockSpec(memory_space=pl.ANY)] * 8,
        out_specs=[pl.BlockSpec(memory_space=pl.ANY)] * 2,
        scratch_shapes=[pltpu.SemaphoreType.DMA((8,))],
    )
    return pl.pallas_call(
        join_kernel,
        grid_spec=spec,
        out_shape=[part, part],
        cost_estimate=pl.CostEstimate(flops=0, bytes_accessed=2_000_000, transcendentals=0),
    )(ids, *pieces)


def chip_planes(slab, core):
    other = lax.ppermute(slab, "c", SWAP)
    inner = jnp.where(core == 0, jnp.concatenate([slab, other]), jnp.concatenate([other, slab]))
    chips = SIZES[2] * SIZES[3]
    before = lax.ppermute(inner[3:], CHIPS, [(i, i + 1) for i in range(chips - 1)])
    after = lax.ppermute(inner[:1], CHIPS, [(i + 1, i) for i in range(chips - 1)])
    return jnp.concatenate([before, inner, after])


def gather_quarter(shard, core, ids):
    xh, z, y, xl = (lax.axis_index(n) for n in ("xh", "z", "y", "xl"))
    to_xl = jnp.where(core == xh, xl, 1 - xl)
    parts = []
    for odd in range(2):
        colour = 2 * ((y + to_xl) % 2) + (z + odd + to_xl) % 2
        parts.append(lax.dynamic_slice_in_dim(shard, jnp.minimum(7 * colour, 20), 7, axis=0))
    pieces = []
    for r in range(8):
        perm = []
        for here_z in range(8):
            there_z = (here_z + r) % 8
            for h in range(2):
                for x_low in range(2):
                    for c in range(2):
                        src = ((h * 8 + here_z) * 2 + x_low) * 2 + c
                        if c == h:
                            dst = ((h * 8 + there_z) * 2 + x_low) * 2 + c
                        else:
                            dst = (((1 - h) * 8 + there_z) * 2 + 1 - x_low) * 2 + h
                        perm.append((src, dst))
        pieces.append(lax.ppermute(parts[r % 2], ("xh", "z", "xl", "c"), perm))
    return join(ids, pieces)


def ring(array, axes, by):
    count = math.prod(SIZES[AXES.index(n)] for n in axes)
    return lax.ppermute(array, axes, [(i, (i + by) % count) for i in range(count)])


def gather_weights(shard, core, ids):
    low, high = gather_quarter(shard, core, ids)
    pieces = [low, high]
    for axes in (("z",), ("y",), ("xh", "xl")):
        pieces += [ring(low, axes, 1), ring(high, axes, -1)]
    return pieces


def local(slabs, kernel, gain, shift):
    core = lax.axis_index("c")
    z, y, xl = (lax.axis_index(n) for n in ("z", "y", "xl"))
    colour = 2 * ((y + xl) % 2) + (z + xl) % 2
    ids = jnp.stack([core, colour, z]).astype(jnp.int32)
    _, planes, height, width, chans = slabs.shape
    rows = height * width
    outs = chans // 2
    group = SIZES[2] * SIZES[3] * SIZES[4]

    shard = jnp.transpose(kernel, (0, 1, 2, 4, 3)).reshape(27, kernel.shape[4], chans)
    pieces = gather_weights(shard, core, ids)
    wide = widen(chip_planes(slabs[0].reshape(planes, rows, chans), core), width)
    send, keep, stats = conv(ids, wide, pieces, rows, width, group)

    recv = lax.ppermute(send, "c", SWAP)
    everyone = lax.all_to_all(stats, DEPTH, 0, 0, tiled=True)
    cells = planes * rows * group
    out = normalize(
        ids, keep, recv, everyone, gain.reshape(2, 1, outs), shift.reshape(2, 1, outs), cells
    )
    return out.reshape(slabs.shape)


def solution(mesh):
    fine = Mesh(mesh.devices.reshape(SIZES), AXES)
    x_spec = P(("xh", "z"), DEPTH, None, None, None)
    in_specs = (x_spec, P(None, None, None, None, ("xh", "z")), P(), P())
    return jax.shard_map(local, mesh=fine, in_specs=in_specs, out_specs=x_spec, check_vma=False)
```

time: 121 us -> 140 us (1.16)
  Pallas kernels: 18.2 us -> 50.8 us
  starting transfers between devices: 15.2 us -> 47 us
  waiting for transfers between devices: 59.3 us -> 37.5 us
  between operations: 13.5 us -> 0.19 us
  local copies, waits for them, and re-layouts: 11.3 us -> 2.59 us
    pallas_call x0 -> x1, Pallas kernels: none -> 33.1 us  [join(): pl.pallas_call(join_kernel, grid_spec=spec, out_shape=[part, part], cost_...]
    all_gather x1 -> x0, waiting for transfers between devices: 25.8 us -> none  [local(): half = lax.all_gather(x_exchange(shard, core), 'z', axis=1, tiled=True)]
    ppermute x1 -> x14, waiting for transfers between devices: 6.77 us -> 31.8 us  [the longest x6 16.6 us: ring(): lax.ppermute(array, axes, [(i, (i + by) % count) for i in range(count)])]
    ppermute x1 -> x14, starting transfers between devices: 5.9 us -> 30.8 us  [the longest x8 21 us: gather_quarter(): pieces.append(lax.ppermute(parts[r % 2], ('xh', 'z', 'xl', 'c'), perm))]
    ppermute x1, waiting for transfers between devices: 11.8 us -> 0.01 us  [chip_planes(): lax.ppermute(inner[:1], CHIPS, [(i + 1, i) for i in range(chips - 1)])]
    unnamed x12 -> x29, local copies, waits for them, and re-layouts: 8.47 us -> 0.7 us
    ppermute x1, waiting for transfers between devices: 7.03 us -> 0.01 us  [chip_planes(): lax.ppermute(inner[3:], CHIPS, [(i, i + 1) for i in range(chips - 1)])]
    ppermute x1, starting transfers between devices: 0.09 us -> 3.24 us  [chip_planes(): other = lax.ppermute(slab, 'c', SWAP)]
  transfers between devices with their start and end apart: 7 -> 19, of which waited for: 6 -> 11; matrix products, arithmetic and copies ran while one was open for 1% -> 2% of each run, Pallas kernels for 1% -> 25%
where the time goes in v2:
time: 140 us; the launch traced here: 139 us
  Pallas kernels  50.8 us (36%)
  starting transfers between devices  47 us (34%)
  waiting for transfers between devices  37.5 us (27%)
  local copies, waits for them, and re-layouts  2.59 us (2%)
    pallas_call x1, Pallas kernels, join(): pl.pallas_call(join_kernel, grid_spec=spec, out_shape=[part, part], cost_...  33.1 us
    ppermute x8, starting transfers between devices, gather_quarter(): pieces.append(lax.ppermute(parts[r % 2], ('xh', 'z', 'xl', 'c'), perm))  21 us
    ppermute x6, waiting for transfers between devices, ring(): lax.ppermute(array, axes, [(i, (i + by) % count) for i in range(count)])  16.6 us
    ppermute x8, waiting for transfers between devices, gather_quarter(): pieces.append(lax.ppermute(parts[r % 2], ('xh', 'z', 'xl', 'c'), perm))  15.2 us
    pallas_call x1, Pallas kernels, conv(): pl.pallas_call(functools.partial(conv_kernel, rows=rows, width=width), gr...  13.5 us
    ppermute x6, starting transfers between devices, ring(): lax.ppermute(array, axes, [(i, (i + by) % count) for i in range(count)])  9.78 us
    all_to_all x1, starting transfers between devices, local(): everyone = lax.all_to_all(stats, DEPTH, 0, 0, tiled=True)  6.79 us
    all_to_all x1, waiting for transfers between devices, local(): everyone = lax.all_to_all(stats, DEPTH, 0, 0, tiled=True)  5.62 us
  transfers between devices with their start and end apart: 19, of which 11 were waited for; matrix products, arithmetic and copies ran while one was open for 2% of the time, Pallas kernels for 25%

profile of v2, /device:TPU:1, one launch (start us, length us, event | category | flops | bytes accessed | tf_op | source)
XLA Modules:
  0.0 139.3 jit_solution(3391365253430718087)
XLA Ops:
  0.0 3.2 %collective-permute-start = (bf16[2,512,384]{2,1,0:T(8,128)(2,1)}, bf16[2,512,384]{2,1,0:T(8,128)(2,1)S(1)}, u32[]{:S(2)}, u32[]{:S(2)}) collective-permute-start(bf16[2,512,384]{2,1,0:T(8,128)(2,1)} %bitcast.14), channel_id=1, source_target_pairs={{0,1},{1,0},{2,3},{3,2},{4,5},{5,4},{6,7},{7,6},{8,9},{9,8},{10,11... | collective-permute-start | bytes 2359304 | tf_op jit(solution)/shard_map/ppermute | solution.py:214
  4.3 2.6 %collective-permute-start.3 = (bf16[7,24,384]{2,1,0:T(8,128)(2,1)S(1)}, bf16[7,24,384]{2,1,0:T(8,128)(2,1)S(1)}, u32[]{:S(2)}, u32[]{:S(2)}) collective-permute-start(bf16[7,24,384]{2,1,0:T(8,128)(2,1)S(1)} %get-tuple-element.18), channel_id=1, source_target_pairs={{0,0},{1,130},{2,2},{3,128},{128,3},{129,129},{130,1},{131,131},{1... | collective-permute-start | bytes 387080 | tf_op jit(solution)/shard_map/ppermute | solution.py:243
  6.9 2.0 %collective-permute-start.4 = (bf16[7,24,384]{2,1,0:T(8,128)(2,1)S(1)}, bf16[7,24,384]{2,1,0:T(8,128)(2,1)S(1)}, u32[]{:S(2)}, u32[]{:S(2)}) collective-permute-start(bf16[7,24,384]{2,1,0:T(8,128)(2,1)S(1)} %get-tuple-element.17), channel_id=1, source_target_pairs={{0,16},{1,146},{2,18},{3,144},{128,19},{129,145},{130,17},{131,147... | collective-permute-start | bytes 387080 | tf_op jit(solution)/shard_map/ppermute | solution.py:243
  8.8 5.1 %collective-permute-start.5 = (bf16[7,24,384]{2,1,0:T(8,128)(2,1)S(1)}, bf16[7,24,384]{2,1,0:T(8,128)(2,1)S(1)}, u32[]{:S(2)}, u32[]{:S(2)}) collective-permute-start(bf16[7,24,384]{2,1,0:T(8,128)(2,1)S(1)} %get-tuple-element.18), channel_id=1, source_target_pairs={{0,32},{1,162},{2,34},{3,160},{128,35},{129,161},{130,33},{131,163... | collective-permute-start | bytes 387080 | tf_op jit(solution)/shard_map/ppermute | solution.py:243
  14.0 4.0 %collective-permute-start.6 = (bf16[7,24,384]{2,1,0:T(8,128)(2,1)S(1)}, bf16[7,24,384]{2,1,0:T(8,128)(2,1)S(1)}, u32[]{:S(2)}, u32[]{:S(2)}) collective-permute-start(bf16[7,24,384]{2,1,0:T(8,128)(2,1)S(1)} %get-tuple-element.17), channel_id=1, source_target_pairs={{0,48},{1,178},{2,50},{3,176},{128,51},{129,177},{130,49},{131,179... | collective-permute-start | bytes 387080 | tf_op jit(solution)/shard_map/ppermute | solution.py:243
  18.0 2.4 %collective-permute-start.7 = (bf16[7,24,384]{2,1,0:T(8,128)(2,1)S(1)}, bf16[7,24,384]{2,1,0:T(8,128)(2,1)S(1)}, u32[]{:S(2)}, u32[]{:S(2)}) collective-permute-start(bf16[7,24,384]{2,1,0:T(8,128)(2,1)S(1)} %get-tuple-element.18), channel_id=1, source_target_pairs={{0,64},{1,194},{2,66},{3,192},{128,67},{129,193},{130,65},{131,195... | collective-permute-start | bytes 387080 | tf_op jit(solution)/shard_map/ppermute | solution.py:243
  20.4 4.9 %collective-permute-start.8 = (bf16[7,24,384]{2,1,0:T(8,128)(2,1)S(1)}, bf16[7,24,384]{2,1,0:T(8,128)(2,1)S(1)}, u32[]{:S(2)}, u32[]{:S(2)}) collective-permute-start(bf16[7,24,384]{2,1,0:T(8,128)(2,1)S(1)} %get-tuple-element.17), channel_id=1, source_target_pairs={{0,80},{1,210},{2,82},{3,208},{128,83},{129,209},{130,81},{131,211... | collective-permute-start | bytes 387080 | tf_op jit(solution)/shard_map/ppermute | solution.py:243
  25.3 5.1 %collective-permute-done.5.refs_2_ = bf16[7,24,384]{2,1,0:T(8,128)(2,1)S(1)} collective-permute-done((bf16[7,24,384]{2,1,0:T(8,128)(2,1)S(1)}, bf16[7,24,384]{2,1,0:T(8,128)(2,1)S(1)}, u32[]{:S(2)}, u32[]{:S(2)}) %collective-permute-start.5) | collective-permute-done | bytes 129056 | tf_op jit(solution)/shard_map/ppermute | solution.py:243
  30.4 3.8 %collective-permute-done.6.refs_3_ = bf16[7,24,384]{2,1,0:T(8,128)(2,1)S(1)} collective-permute-done((bf16[7,24,384]{2,1,0:T(8,128)(2,1)S(1)}, bf16[7,24,384]{2,1,0:T(8,128)(2,1)S(1)}, u32[]{:S(2)}, u32[]{:S(2)}) %collective-permute-start.6) | collective-permute-done | bytes 129056 | tf_op jit(solution)/shard_map/ppermute | solution.py:243
  34.7 3.4 %collective-permute-done.8.refs_5_ = bf16[7,24,384]{2,1,0:T(8,128)(2,1)S(1)} collective-permute-done((bf16[7,24,384]{2,1,0:T(8,128)(2,1)S(1)}, bf16[7,24,384]{2,1,0:T(8,128)(2,1)S(1)}, u32[]{:S(2)}, u32[]{:S(2)}) %collective-permute-start.8) | collective-permute-done | bytes 129056 | tf_op jit(solution)/shard_map/ppermute | solution.py:243
  38.1 2.3 %collective-permute-done.9.refs_6_ = bf16[7,24,384]{2,1,0:T(8,128)(2,1)S(1)} collective-permute-done((bf16[7,24,384]{2,1,0:T(8,128)(2,1)S(1)}, bf16[7,24,384]{2,1,0:T(8,128)(2,1)S(1)}, u32[]{:S(2)}, u32[]{:S(2)}) %collective-permute-start.9) | collective-permute-done | bytes 129056 | tf_op jit(solution)/shard_map/ppermute | solution.py:243
  41.8 33.1 %shard_map.47 = (bf16[7,96,384]{2,1,0:T(8,128)(2,1)}, bf16[7,96,384]{2,1,0:T(8,128)(2,1)}) custom-call(s32[3]{0:T(128)} %pad_add_fusion.ids_ref, bf16[7,24,384]{2,1,0:T(8,128)(2,1)} %copy-done.4, bf16[7,24,384]{2,1,0:T(8,128)(2,1)} %copy-done.5, bf16[7,24,384]{2,1,0:T(8,128)(2,1)} %copy-done.6, bf16[7,24,384]{2,1,0:T(8,128)(2,1)} %copy-done.7, ...), custom_call_target="tpu_custom_call" | custom-call | bytes 2000000 | tf_op jit(solution)/shard_map/pallas_call | solution.py:205
  77.9 4.0 %collective-permute-start.1 = (bf16[1,512,384]{2,1,0:T(8,128)(2,1)S(1)}, bf16[1,512,384]{2,1,0:T(8,128)(2,1)S(1)}, u32[]{:S(2)}, u32[]{:S(2)}) collective-permute-start(bf16[1,512,384]{2,1,0:T(8,128)(2,1)S(1)} %get-tuple-element.15), channel_id=1, source_target_pairs={{0,2},{2,4},{4,6},{6,8},{8,10},{10,12},{12,14},{1,3},{3,5},{5,7},{... | collective-permute-start | bytes 1179656 | tf_op jit(solution)/shard_map/ppermute | solution.py:217
  83.3 1.6 %collective-permute-start.12 = (bf16[7,96,384]{2,1,0:T(8,128)(2,1)S(1)}, bf16[7,96,384]{2,1,0:T(8,128)(2,1)S(1)}, u32[]{:S(2)}, u32[]{:S(2)}) collective-permute-start(bf16[7,96,384]{2,1,0:T(8,128)(2,1)S(1)} %copy-done.2), channel_id=1, source_target_pairs={{0,112},{16,0},{32,16},{48,32},{64,48},{80,64},{96,80},{112,96},{1... | collective-permute-start | bytes 1548296 | tf_op jit(solution)/shard_map/ppermute | solution.py:249
  84.9 3.0 %collective-permute-done.11.refs_2_ = bf16[7,96,384]{2,1,0:T(8,128)(2,1)S(1)} collective-permute-done((bf16[7,96,384]{2,1,0:T(8,128)(2,1)}, bf16[7,96,384]{2,1,0:T(8,128)(2,1)S(1)}, u32[]{:S(2)}, u32[]{:S(2)}) %collective-permute-start.11) | collective-permute-done | bytes 516128 | tf_op jit(solution)/shard_map/ppermute | solution.py:249
  87.9 2.4 %collective-permute-start.14 = (bf16[7,96,384]{2,1,0:T(8,128)(2,1)S(1)}, bf16[7,96,384]{2,1,0:T(8,128)(2,1)S(1)}, u32[]{:S(2)}, u32[]{:S(2)}) collective-permute-start(bf16[7,96,384]{2,1,0:T(8,128)(2,1)S(1)} %copy-done.2), channel_id=1, source_target_pairs={{0,12},{4,0},{8,4},{12,8},{1,13},{5,1},{9,5},{13,9},{2,14},{6,2},{... | collective-permute-start | bytes 1548296 | tf_op jit(solution)/shard_map/ppermute | solution.py:249
  90.3 1.7 %collective-permute-start.15 = (bf16[7,96,384]{2,1,0:T(8,128)(2,1)S(1)}, bf16[7,96,384]{2,1,0:T(8,128)(2,1)S(1)}, u32[]{:S(2)}, u32[]{:S(2)}) collective-permute-start(bf16[7,96,384]{2,1,0:T(8,128)(2,1)S(1)} %copy-done.1), channel_id=1, source_target_pairs={{0,2},{2,128},{128,130},{130,0},{1,3},{3,129},{129,131},{131,1},{4... | collective-permute-start | bytes 1548296 | tf_op jit(solution)/shard_map/ppermute | solution.py:249
  93.9 1.6 %shard_map.46.x_ref = bf16[6,576,1152]{2,1,0:T(8,128)(2,1)S(1)} custom-call(bf16[6,512,384]{2,1,0:T(8,128)(2,1)S(1)} %pad_maximum_fusion.x_ref), custom_call_target="tpu_custom_call" | custom-call | bytes 12000000 | tf_op jit(solution)/shard_map/pallas_call | solution.py:47
  96.4 6.5 %collective-permute-done.13.refs_4_ = bf16[7,96,384]{2,1,0:T(8,128)(2,1)S(1)} collective-permute-done((bf16[7,96,384]{2,1,0:T(8,128)(2,1)S(1)}, bf16[7,96,384]{2,1,0:T(8,128)(2,1)S(1)}, u32[]{:S(2)}, u32[]{:S(2)}) %collective-permute-start.13) | collective-permute-done | bytes 516128 | tf_op jit(solution)/shard_map/ppermute | solution.py:249
  104.1 5.1 %collective-permute-done.16.refs_7_ = bf16[7,96,384]{2,1,0:T(8,128)(2,1)S(1)} collective-permute-done((bf16[7,96,384]{2,1,0:T(8,128)(2,1)S(1)}, bf16[7,96,384]{2,1,0:T(8,128)(2,1)S(1)}, u32[]{:S(2)}, u32[]{:S(2)}) %collective-permute-start.16) | collective-permute-done | bytes 516128 | tf_op jit(solution)/shard_map/ppermute | solution.py:249
  109.2 13.5 %shard_map.48 = (f32[2,512,256]{2,1,0:T(8,128)S(1)}, f32[2,512,192]{2,1,0:T(8,128)S(1)}, f32[16,384]{1,0:T(8,128)S(1)}) custom-call(s32[3]{0:T(128)S(1)} %copy-done, bf16[6,576,1152]{2,1,0:T(8,128)(2,1)S(1)} %shard_map.46.x_ref, bf16[7,96,384]{2,1,0:T(8,128)(2,1)S(1)} %copy-done.1, bf16[7,96,384]{2,1,0:T(8,128)(2,1)S(1)} %copy-done.2, ...), custom_call_target="tpu_custom_call" | custom-call | flops 8000000000 | bytes 16000000 | tf_op jit(solution)/shard_map/pallas_call | solution.py:121
  124.1 6.8 %all-to-all-start = ((f32[16,1,384]{2,1,0:T(1,128)}), f32[16,1,384]{2,1,0:T(1,128)S(1)}, u32[]{:S(2)}, u32[]{:S(2)}) async-start(f32[16,1,384]{2,1,0:T(1,128)} %copy.5), calls=%async_computation | async-start | bytes 49152 | tf_op jit(solution)/shard_map/all_to_all | solution.py:276
  131.1 5.6 %all-to-all-done = f32[16,1,384]{2,1,0:T(1,128)S(1)} async-done(((f32[16,1,384]{2,1,0:T(1,128)}), f32[16,1,384]{2,1,0:T(1,128)S(1)}, u32[]{:S(2)}, u32[]{:S(2)}) %all-to-all-start) | async-done | bytes 24608 | tf_op jit(solution)/shard_map/all_to_all | solution.py:276
  136.7 2.6 %shard_map.49 = bf16[2,512,384]{2,1,0:T(8,128)(2,1)} custom-call(s32[3]{0:T(128)S(1)} %copy-done, f32[2,512,192]{2,1,0:T(8,128)S(1)} %get-tuple-element.12.keep_ref, f32[2,512,256]{2,1,0:T(8,128)S(1)} %collective-permute-done.17.recv_ref, f32[16,384]{1,0:T(8,128)S(1)} %bitcast.12, f32[2,1,192]{2,1,0:T(1,128)S(1)} %reshape.15.gain_ref, ...), custom_call_target="tpu_custom_call" | custom-call | flops 4000000 | bytes 3000000 | tf_op jit(solution)/shard_map/pallas_call | solution.py:166
  (55 shorter events, 12.6 us)
Async XLA Ops:
  0.0 76.1 %copy-start.3 = (bf16[1,2,16,32,384]{4,3,2,1,0:T(8,128)(2,1)S(1)}, bf16[1,2,16,32,384]{4,3,2,1,0:T(8,128)(2,1)}, u32[]{:S(2)}) copy-start(bf16[1,2,16,32,384]{4,3,2,1,0:T(8,128)(2,1)} %param.4) | copy-start | bytes 2359300
  0.0 76.1 %collective-permute-start = (bf16[2,512,384]{2,1,0:T(8,128)(2,1)}, bf16[2,512,384]{2,1,0:T(8,128)(2,1)S(1)}, u32[]{:S(2)}, u32[]{:S(2)}) collective-permute-start(bf16[2,512,384]{2,1,0:T(8,128)(2,1)} %bitcast.14), channel_id=1, source_target_pairs={{0,1},{1,0},{2,3},{3,2},{4,5},{5,4},{6,7},{7,6},{8,9},{9,8},{10,11... | collective-permute-start | bytes 2359304 | tf_op jit(solution)/shard_map/ppermute | solution.py:214
  4.3 13.7 %collective-permute-start.3 = (bf16[7,24,384]{2,1,0:T(8,128)(2,1)S(1)}, bf16[7,24,384]{2,1,0:T(8,128)(2,1)S(1)}, u32[]{:S(2)}, u32[]{:S(2)}) collective-permute-start(bf16[7,24,384]{2,1,0:T(8,128)(2,1)S(1)} %get-tuple-element.18), channel_id=1, source_target_pairs={{0,0},{1,130},{2,2},{3,128},{128,3},{129,129},{130,1},{131,131},{1... | collective-permute-start | bytes 387080 | tf_op jit(solution)/shard_map/ppermute | solution.py:243
  6.9 13.5 %collective-permute-start.4 = (bf16[7,24,384]{2,1,0:T(8,128)(2,1)S(1)}, bf16[7,24,384]{2,1,0:T(8,128)(2,1)S(1)}, u32[]{:S(2)}, u32[]{:S(2)}) collective-permute-start(bf16[7,24,384]{2,1,0:T(8,128)(2,1)S(1)} %get-tuple-element.17), channel_id=1, source_target_pairs={{0,16},{1,146},{2,18},{3,144},{128,19},{129,145},{130,17},{131,147... | collective-permute-start | bytes 387080 | tf_op jit(solution)/shard_map/ppermute | solution.py:243
  8.8 21.5 %collective-permute-start.5 = (bf16[7,24,384]{2,1,0:T(8,128)(2,1)S(1)}, bf16[7,24,384]{2,1,0:T(8,128)(2,1)S(1)}, u32[]{:S(2)}, u32[]{:S(2)}) collective-permute-start(bf16[7,24,384]{2,1,0:T(8,128)(2,1)S(1)} %get-tuple-element.18), channel_id=1, source_target_pairs={{0,32},{1,162},{2,34},{3,160},{128,35},{129,161},{130,33},{131,163... | collective-permute-start | bytes 387080 | tf_op jit(solution)/shard_map/ppermute | solution.py:243
  14.0 20.2 %collective-permute-start.6 = (bf16[7,24,384]{2,1,0:T(8,128)(2,1)S(1)}, bf16[7,24,384]{2,1,0:T(8,128)(2,1)S(1)}, u32[]{:S(2)}, u32[]{:S(2)}) collective-permute-start(bf16[7,24,384]{2,1,0:T(8,128)(2,1)S(1)} %get-tuple-element.17), channel_id=1, source_target_pairs={{0,48},{1,178},{2,50},{3,176},{128,51},{129,177},{130,49},{131,179... | collective-permute-start | bytes 387080 | tf_op jit(solution)/shard_map/ppermute | solution.py:243
  18.0 23.1 %copy-start.4 = (bf16[7,24,384]{2,1,0:T(8,128)(2,1)}, bf16[7,24,384]{2,1,0:T(8,128)(2,1)S(1)}, u32[]{:S(2)}) copy-start(bf16[7,24,384]{2,1,0:T(8,128)(2,1)S(1)} %collective-permute-done.3.refs_0_) | copy-start | bytes 387076
  18.0 16.8 %collective-permute-start.7 = (bf16[7,24,384]{2,1,0:T(8,128)(2,1)S(1)}, bf16[7,24,384]{2,1,0:T(8,128)(2,1)S(1)}, u32[]{:S(2)}, u32[]{:S(2)}) collective-permute-start(bf16[7,24,384]{2,1,0:T(8,128)(2,1)S(1)} %get-tuple-element.18), channel_id=1, source_target_pairs={{0,64},{1,194},{2,66},{3,192},{128,67},{129,193},{130,65},{131,195... | collective-permute-start | bytes 387080 | tf_op jit(solution)/shard_map/ppermute | solution.py:243
  20.4 20.7 %copy-start.5 = (bf16[7,24,384]{2,1,0:T(8,128)(2,1)}, bf16[7,24,384]{2,1,0:T(8,128)(2,1)S(1)}, u32[]{:S(2)}) copy-start(bf16[7,24,384]{2,1,0:T(8,128)(2,1)S(1)} %collective-permute-done.4.refs_1_) | copy-start | bytes 387076
  20.4 17.8 %collective-permute-start.8 = (bf16[7,24,384]{2,1,0:T(8,128)(2,1)S(1)}, bf16[7,24,384]{2,1,0:T(8,128)(2,1)S(1)}, u32[]{:S(2)}, u32[]{:S(2)}) collective-permute-start(bf16[7,24,384]{2,1,0:T(8,128)(2,1)S(1)} %get-tuple-element.17), channel_id=1, source_target_pairs={{0,80},{1,210},{2,82},{3,208},{128,83},{129,209},{130,81},{131,211... | collective-permute-start | bytes 387080 | tf_op jit(solution)/shard_map/ppermute | solution.py:243
  30.4 10.1 %collective-permute-start.9 = (bf16[7,24,384]{2,1,0:T(8,128)(2,1)S(1)}, bf16[7,24,384]{2,1,0:T(8,128)(2,1)S(1)}, u32[]{:S(2)}, u32[]{:S(2)}) collective-permute-start(bf16[7,24,384]{2,1,0:T(8,128)(2,1)S(1)} %get-tuple-element.18), channel_id=1, source_target_pairs={{0,96},{1,226},{2,98},{3,224},{128,99},{129,225},{130,97},{131,227... | collective-permute-start | bytes 387080 | tf_op jit(solution)/shard_map/ppermute | solution.py:243
  34.1 7.0 %collective-permute-start.10 = (bf16[7,24,384]{2,1,0:T(8,128)(2,1)S(1)}, bf16[7,24,384]{2,1,0:T(8,128)(2,1)S(1)}, u32[]{:S(2)}, u32[]{:S(2)}) collective-permute-start(bf16[7,24,384]{2,1,0:T(8,128)(2,1)S(1)} %get-tuple-element.17), channel_id=1, source_target_pairs={{0,112},{1,242},{2,114},{3,240},{128,115},{129,241},{130,113},{131... | collective-permute-start | bytes 387080 | tf_op jit(solution)/shard_map/ppermute | solution.py:243
  74.9 12.9 %collective-permute-start.11 = (bf16[7,96,384]{2,1,0:T(8,128)(2,1)}, bf16[7,96,384]{2,1,0:T(8,128)(2,1)S(1)}, u32[]{:S(2)}, u32[]{:S(2)}) collective-permute-start(bf16[7,96,384]{2,1,0:T(8,128)(2,1)} %get-tuple-element.10.refs_0_), channel_id=1, source_target_pairs={{0,16},{16,32},{32,48},{48,64},{64,80},{80,96},{96,112},{112,0},{1... | collective-permute-start | bytes 1548296 | tf_op jit(solution)/shard_map/ppermute | solution.py:249
  76.5 13.8 %collective-permute-start.2 = (bf16[1,512,384]{2,1,0:T(8,128)(2,1)S(1)}, bf16[1,512,384]{2,1,0:T(8,128)(2,1)S(1)}, u32[]{:S(2)}, u32[]{:S(2)}) collective-permute-start(bf16[1,512,384]{2,1,0:T(8,128)(2,1)S(1)} %get-tuple-element.16), channel_id=1, source_target_pairs={{2,0},{4,2},{6,4},{8,6},{10,8},{12,10},{14,12},{3,1},{5,3},{7,5},{... | collective-permute-start | bytes 1179656 | tf_op jit(solution)/shard_map/ppermute | solution.py:218
  77.9 14.1 %collective-permute-start.1 = (bf16[1,512,384]{2,1,0:T(8,128)(2,1)S(1)}, bf16[1,512,384]{2,1,0:T(8,128)(2,1)S(1)}, u32[]{:S(2)}, u32[]{:S(2)}) collective-permute-start(bf16[1,512,384]{2,1,0:T(8,128)(2,1)S(1)} %get-tuple-element.15), channel_id=1, source_target_pairs={{0,2},{2,4},{4,6},{6,8},{8,10},{10,12},{12,14},{1,3},{3,5},{5,7},{... | collective-permute-start | bytes 1179656 | tf_op jit(solution)/shard_map/ppermute | solution.py:217
  81.9 21.0 %collective-permute-start.13 = (bf16[7,96,384]{2,1,0:T(8,128)(2,1)S(1)}, bf16[7,96,384]{2,1,0:T(8,128)(2,1)S(1)}, u32[]{:S(2)}, u32[]{:S(2)}) collective-permute-start(bf16[7,96,384]{2,1,0:T(8,128)(2,1)S(1)} %copy-done.1), channel_id=1, source_target_pairs={{0,4},{4,8},{8,12},{12,0},{1,5},{5,9},{9,13},{13,1},{2,6},{6,10},{... | collective-permute-start | bytes 1548296 | tf_op jit(solution)/shard_map/ppermute | solution.py:249
  83.3 13.1 %collective-permute-start.12 = (bf16[7,96,384]{2,1,0:T(8,128)(2,1)S(1)}, bf16[7,96,384]{2,1,0:T(8,128)(2,1)S(1)}, u32[]{:S(2)}, u32[]{:S(2)}) collective-permute-start(bf16[7,96,384]{2,1,0:T(8,128)(2,1)S(1)} %copy-done.2), channel_id=1, source_target_pairs={{0,112},{16,0},{32,16},{48,32},{64,48},{80,64},{96,80},{112,96},{1... | collective-permute-start | bytes 1548296 | tf_op jit(solution)/shard_map/ppermute | solution.py:249
  87.9 15.1 %collective-permute-start.14 = (bf16[7,96,384]{2,1,0:T(8,128)(2,1)S(1)}, bf16[7,96,384]{2,1,0:T(8,128)(2,1)S(1)}, u32[]{:S(2)}, u32[]{:S(2)}) collective-permute-start(bf16[7,96,384]{2,1,0:T(8,128)(2,1)S(1)} %copy-done.2), channel_id=1, source_target_pairs={{0,12},{4,0},{8,4},{12,8},{1,13},{5,1},{9,5},{13,9},{2,14},{6,2},{... | collective-permute-start | bytes 1548296 | tf_op jit(solution)/shard_map/ppermute | solution.py:249
  90.3 13.8 %collective-permute-start.15 = (bf16[7,96,384]{2,1,0:T(8,128)(2,1)S(1)}, bf16[7,96,384]{2,1,0:T(8,128)(2,1)S(1)}, u32[]{:S(2)}, u32[]{:S(2)}) collective-permute-start(bf16[7,96,384]{2,1,0:T(8,128)(2,1)S(1)} %copy-done.1), channel_id=1, source_target_pairs={{0,2},{2,128},{128,130},{130,0},{1,3},{3,129},{129,131},{131,1},{4... | collective-permute-start | bytes 1548296 | tf_op jit(solution)/shard_map/ppermute | solution.py:249
  92.0 17.2 %collective-permute-start.16 = (bf16[7,96,384]{2,1,0:T(8,128)(2,1)S(1)}, bf16[7,96,384]{2,1,0:T(8,128)(2,1)S(1)}, u32[]{:S(2)}, u32[]{:S(2)}) collective-permute-start(bf16[7,96,384]{2,1,0:T(8,128)(2,1)S(1)} %copy-done.2), channel_id=1, source_target_pairs={{0,130},{2,0},{128,2},{130,128},{1,131},{3,1},{129,3},{131,129},{4... | collective-permute-start | bytes 1548296 | tf_op jit(solution)/shard_map/ppermute | solution.py:249
  95.6 35.3 %copy-start.12 = (f32[384]{0:T(512)S(1)}, f32[384]{0:T(512)}, u32[]{:S(2)}) copy-start(f32[384]{0:T(512)} %param.6) | copy-start | bytes 4612
  95.6 35.4 %copy-start.13 = (f32[384]{0:T(512)S(1)}, f32[384]{0:T(512)}, u32[]{:S(2)}) copy-start(f32[384]{0:T(512)} %param.7) | copy-start | bytes 4612
  122.7 14.0 %collective-permute-start.17 = (f32[2,512,256]{2,1,0:T(8,128)S(1)}, f32[2,512,256]{2,1,0:T(8,128)S(1)}, u32[]{:S(2)}, u32[]{:S(2)}) collective-permute-start(f32[2,512,256]{2,1,0:T(8,128)S(1)} %get-tuple-element.13), channel_id=1, source_target_pairs={{0,1},{1,0},{2,3},{3,2},{4,5},{5,4},{6,7},{7,6},{8,9},{9,8},{10,11... | collective-permute-start | bytes 3145736 | tf_op jit(solution)/shard_map/ppermute | solution.py:275
  124.1 12.6 %all-to-all-start = ((f32[16,1,384]{2,1,0:T(1,128)}), f32[16,1,384]{2,1,0:T(1,128)S(1)}, u32[]{:S(2)}, u32[]{:S(2)}) async-start(f32[16,1,384]{2,1,0:T(1,128)} %copy.5), calls=%async_computation | async-start | bytes 49152 | tf_op jit(solution)/shard_map/all_to_all | solution.py:276
  (9 other events, 56.2 us)

commit v3 on v1

v3 whole, which is shorter than its diff:
```python
import functools
import math

import jax
import jax.numpy as jnp
from jax import lax
from jax.experimental import pallas as pl
from jax.experimental.pallas import tpu as pltpu
from jax.sharding import Mesh, PartitionSpec as P

AXES = ("xh", "z", "y", "xl", "c")
SIZES = (2, 8, 4, 2, 2)
CHIPS = ("y", "xl")
DEPTH = ("y", "xl", "c")
SWAP = [(0, 1), (1, 0)]
EPS = 1e-05
PADDED = 256

def shift_rows(plane, by, width):
    rows = plane.shape[0]
    moved = pltpu.roll(plane, by % rows, 0)
    w = lax.broadcasted_iota(jnp.int32, plane.shape, 0) % width
    edge = 0 if by == 1 else width - 1
    return jnp.where(w == edge, 0.0, moved)


def widen_kernel(x_ref, o_ref, *, width):
    x = x_ref[0]
    rows, chans = x.shape
    zero = jnp.zeros((width, 3 * chans), o_ref.dtype)
    o_ref[0, 0:width, :] = zero
    o_ref[0, width + rows : 2 * width + rows, :] = zero
    wide = x.astype(jnp.float32)
    o_ref[0, width : width + rows, 0:chans] = shift_rows(wide, 1, width).astype(o_ref.dtype)
    o_ref[0, width : width + rows, chans : 2 * chans] = x
    o_ref[0, width : width + rows, 2 * chans : 3 * chans] = shift_rows(wide, -1, width).astype(o_ref.dtype)


def widen(planes, width):
    count, rows, chans = planes.shape
    return pl.pallas_call(
        functools.partial(widen_kernel, width=width),
        grid=(count,),
        in_specs=[pl.BlockSpec((1, rows, chans), lambda i: (i, 0, 0))],
        out_specs=pl.BlockSpec((1, rows + 2 * width, 3 * chans), lambda i: (i, 0, 0)),
        out_shape=jax.ShapeDtypeStruct((count, rows + 2 * width, 3 * chans), planes.dtype),
        compiler_params=pltpu.CompilerParams(vmem_limit_bytes=32 << 20),
        cost_estimate=pl.CostEstimate(flops=0, bytes_accessed=12_000_000, transcendentals=0),
    )(planes)


def half_conv(x_ref, w_ref, plane, taps, rows, width):
    chans = w_ref.shape[2]
    lhs, rhs = [], []
    for i, t in taps:
        a, b, e = t // 9, t // 3 % 3, t % 3
        lhs.append(x_ref[plane + a, b * width : b * width + rows, e * chans : (e + 1) * chans])
        rhs.append(w_ref[i])
    lhs, rhs = jnp.concatenate(lhs, axis=1), jnp.concatenate(rhs, axis=1)
    return lax.dot_general(lhs, rhs, (((1,), (1,)), ((), ())), preferred_element_type=jnp.float32)


LOW_TAPS = [(t, t) for t in range(14)]
HIGH_TAPS = [(t - 13, t) for t in range(14, 27)]


def first_kernel(ids_ref, x_ref, w_ref, acc_ref, *, rows, width):
    core, colour = ids_ref[0], ids_ref[1]
    j = pl.program_id(0)
    plane = (j + 2 * (1 - core)) % 4

    @pl.when(colour == 0)
    def _():
        acc_ref[0] = half_conv(x_ref, w_ref, plane, LOW_TAPS, rows, width)

    @pl.when(colour != 0)
    def _():
        acc_ref[0] = half_conv(x_ref, w_ref, plane, HIGH_TAPS, rows, width)


def second_kernel(ids_ref, x_ref, w_ref, acc_ref, before_ref, out_ref, stats_ref, total_ref, sum_ref, *, rows, width, keep):
    core, colour = ids_ref[0], ids_ref[1]
    j = pl.program_id(0)
    outs = total_ref.shape[1]

    @pl.when(j == 0)
    def _():
        sum_ref[...] = before_ref[...] if keep else jnp.zeros_like(sum_ref)

    plane = (j + 2 * keep + 2 * (1 - core)) % 4

    @pl.when(colour == 0)
    def _():
        total_ref[...] = acc_ref[0] + half_conv(x_ref, w_ref, plane, HIGH_TAPS, rows, width)

    @pl.when(colour != 0)
    def _():
        total_ref[...] = acc_ref[0] + half_conv(x_ref, w_ref, plane, LOW_TAPS, rows, width)

    total = total_ref[...]
    sum_ref[0:1, :] += jnp.sum(total, axis=0, keepdims=True)
    sum_ref[1:2, :] += jnp.sum(total * total, axis=0, keepdims=True)
    out_ref[0, :, 0:outs] = total
    if not keep:
        out_ref[0, :, outs:] = jnp.zeros((rows, out_ref.shape[2] - outs), jnp.float32)

    @pl.when(j == 1)
    def _():
        if keep:
            row = jnp.concatenate([sum_ref[0:1, :], sum_ref[1:2, :]], axis=1)
            stats_ref[...] = jnp.broadcast_to(row[None], stats_ref.shape)
        else:
            stats_ref[...] = sum_ref[...]


def first_conv(ids, wide, own, rows, width):
    outs = own.shape[1]
    whole = pl.BlockSpec(memory_space=pltpu.VMEM)
    return pl.pallas_call(
        functools.partial(first_kernel, rows=rows, width=width),
        grid_spec=pltpu.PrefetchScalarGridSpec(
            num_scalar_prefetch=1,
            grid=(4,),
            in_specs=[whole, whole],
            out_specs=pl.BlockSpec((1, rows, outs), lambda j, ids: (j, 0, 0)),
        ),
        out_shape=jax.ShapeDtypeStruct((4, rows, outs), jnp.float32),
        compiler_params=pltpu.CompilerParams(vmem_limit_bytes=40 << 20),
        cost_estimate=pl.CostEstimate(flops=5 * 10**9, bytes_accessed=12_000_000, transcendentals=0),
    )(ids, wide, own)


def second_conv(ids, wide, other, acc, before, rows, width, group, keep):
    outs = other.shape[1]
    lanes = outs if keep else PADDED
    stats = (group, 1, 2 * outs) if keep else (8, outs)
    whole = pl.BlockSpec(memory_space=pltpu.VMEM)
    return pl.pallas_call(
        functools.partial(second_kernel, rows=rows, width=width, keep=keep),
        grid_spec=pltpu.PrefetchScalarGridSpec(
            num_scalar_prefetch=1,
            grid=(2,),
            in_specs=[whole, whole, pl.BlockSpec((1, rows, outs), lambda j, ids: (j + 2 * keep, 0, 0)), whole],
            out_specs=[
                pl.BlockSpec((1, rows, lanes), lambda j, ids: (j, 0, 0)),
                pl.BlockSpec(stats, lambda j, ids: (0,) * len(stats)),
            ],
            scratch_shapes=[pltpu.VMEM((rows, outs), jnp.float32), pltpu.VMEM((8, outs), jnp.float32)],
        ),
        out_shape=[jax.ShapeDtypeStruct((2, rows, lanes), jnp.float32), jax.ShapeDtypeStruct(stats, jnp.float32)],
        compiler_params=pltpu.CompilerParams(vmem_limit_bytes=40 << 20),
        cost_estimate=pl.CostEstimate(flops=2 * 10**9, bytes_accessed=8_000_000, transcendentals=0),
    )(ids, wide, other, acc, before)


def norm_kernel(ids_ref, keep_ref, recv_ref, stats_ref, gain_ref, shift_ref, o_ref, *, cells):
    first = ids_ref[0] == 0
    outs = keep_ref.shape[2]
    keep, recv = keep_ref[0], recv_ref[0, :, 0:outs]
    for half in range(2):
        sums = stats_ref[half]
        for chip in range(1, stats_ref.shape[0] // 2):
            sums = sums + stats_ref[2 * chip + half]
        mean = sums[:, 0:outs] / cells
        variance = sums[:, outs : 2 * outs] / cells - mean * mean
        scale = gain_ref[half] / jnp.sqrt(variance + EPS)
        conv_out = jnp.where(first, keep, recv) if half == 0 else jnp.where(first, recv, keep)
        normed = (conv_out - mean) * scale + shift_ref[half]
        active = jnp.where(normed >= 0, normed, 0.01 * normed).astype(o_ref.dtype)
        o_ref[0, :, half * outs : (half + 1) * outs] = active


def normalize(ids, keep, recv, stats, gain, shift, cells):
    planes, rows, outs = keep.shape
    tile = 256
    spec = pltpu.PrefetchScalarGridSpec(
        num_scalar_prefetch=1,
        grid=(planes, rows // tile),
        in_specs=[
            pl.BlockSpec((1, tile, outs), lambda i, j, ids: (i, j, 0)),
            pl.BlockSpec((1, tile, PADDED), lambda i, j, ids: (i, j, 0)),
            pl.BlockSpec(stats.shape, lambda i, j, ids: (0, 0, 0)),
            pl.BlockSpec((2, 1, outs), lambda i, j, ids: (0, 0, 0)),
            pl.BlockSpec((2, 1, outs), lambda i, j, ids: (0, 0, 0)),
        ],
        out_specs=pl.BlockSpec((1, tile, 2 * outs), lambda i, j, ids: (i, j, 0)),
    )
    return pl.pallas_call(
        functools.partial(norm_kernel, cells=cells),
        grid_spec=spec,
        out_shape=jax.ShapeDtypeStruct((planes, rows, 2 * outs), jnp.bfloat16),
        compiler_params=pltpu.CompilerParams(vmem_limit_bytes=32 << 20),
        cost_estimate=pl.CostEstimate(flops=4_000_000, bytes_accessed=3_000_000, transcendentals=0),
    )(ids, keep, recv, stats, gain, shift)


def chip_planes(slab, core):
    count = SIZES[2] * SIZES[3] * SIZES[4]
    pairs = []
    for d in range(count):
        to = d + 1 if d % 2 else d - 1
        if 0 <= to < count:
            pairs.append((d, to))
    edge = lax.dynamic_slice_in_dim(slab, core, 1, axis=0)
    halo = lax.ppermute(edge, DEPTH, pairs)
    mine = jnp.concatenate([halo, slab])
    other = lax.ppermute(mine, "c", SWAP)
    low = jnp.concatenate([mine, other[1:], other[:1]])
    high = jnp.concatenate([other, slab, halo])
    return jnp.where(core == 0, low, high)


def from_z(array, r):
    perm = []
    for here in range(8):
        there = (here + r) % 8
        for h in range(2):
            for xl in range(2):
                for c in range(2):
                    src = ((h * 8 + here) * 2 + xl) * 2 + c
                    if c == h:
                        dst = ((h * 8 + there) * 2 + xl) * 2 + c
                    else:
                        dst = (((1 - h) * 8 + there) * 2 + 1 - xl) * 2 + h
                    perm.append((src, dst))
    return lax.ppermute(array, ("xh", "z", "xl", "c"), perm)


def ring(array, axes, by):
    count = math.prod(SIZES[AXES.index(n)] for n in axes)
    return lax.ppermute(array, axes, [(i, (i + by) % count) for i in range(count)])


def put(buffer, piece, z, r, tap=0):
    where = jnp.remainder(z - r + 8, 8)
    return lax.dynamic_update_slice(buffer, piece[:, None], (tap, where, 0, 0))


def gather_weights(shard, core):
    xh, zi, y, xl = (lax.axis_index(n) for n in ("xh", "z", "y", "xl"))
    to_xl = jnp.where(core == xh, xl, 1 - xl)
    part = lax.dynamic_slice_in_dim(shard, 13 * ((y + to_xl) % 2), 14, axis=0)
    xs, ys, zs = ("xh", "xl"), ("y",), ("z",)
    up, down, here = from_z(part, 1), from_z(part, -1), from_z(part, 0)
    up2, down2 = ring(up, zs, 1), ring(down, zs, -1)
    far_up, far_down = ring(jnp.stack([here, up, up2]), xs, 1), ring(jnp.stack([down, down2]), xs, -1)
    up3, down3 = ring(up2, zs, 1), ring(down2, zs, -1)
    top, bottom = ring(up3[:7], zs, 1), ring(down3[7:], zs, -1)
    far_top = ring(jnp.concatenate([up3, top]), ys, 1)
    far_bottom = ring(jnp.concatenate([down3, bottom]), ys, -1)

    own = jnp.zeros((14, 8) + shard.shape[1:], shard.dtype)
    for r, piece in ((0, here), (1, up), (-1, down), (2, up2), (-2, down2), (3, up3), (-3, down3)):
        own = put(own, piece, zi, r)
    own = put(put(own, top, zi, 4), bottom, zi, 4, 7)
    other = jnp.zeros_like(own)
    for n in range(3):
        other = put(other, far_up[n], zi, n)
    for n in range(2):
        other = put(other, far_down[n], zi, -n - 1)
    merged = (14, 8 * shard.shape[1], shard.shape[2])

    def finish(gate):
        low, high, _ = lax.optimization_barrier((far_top, far_bottom, gate))
        full = put(put(other, low[:14], zi, 3), high[:14], zi, -3)
        full = put(put(full, low[14:], zi, 4), high[14:], zi, 4, 7)
        return full.reshape(merged)

    return own.reshape(merged), finish, up


def local(slabs, kernel, gain, shift):
    core = lax.axis_index("c")
    z, y, xl = (lax.axis_index(n) for n in ("z", "y", "xl"))
    colour = (y + xl) % 2
    ids = jnp.stack([core, colour, z]).astype(jnp.int32)
    _, planes, height, width, chans = slabs.shape
    rows = height * width
    outs = chans // 2
    group = SIZES[2] * SIZES[3] * SIZES[4]

    shard = jnp.transpose(kernel, (0, 1, 2, 4, 3)).reshape(27, kernel.shape[4], chans)
    own, finish, first = gather_weights(shard, core)
    slab, _ = lax.optimization_barrier((slabs[0].reshape(planes, rows, chans), first))
    wide = widen(chip_planes(slab, core), width)
    acc = first_conv(ids, wide, own, rows, width)
    other = finish(acc)
    send, sums = second_conv(ids, wide, other, acc, jnp.zeros((8, outs), jnp.float32), rows, width, group, 0)
    recv = lax.ppermute(send, "c", SWAP)
    keep, stats = second_conv(ids, wide, other, acc, sums, rows, width, group, 1)
    everyone = lax.all_to_all(stats, DEPTH, 0, 0, tiled=True)
    cells = planes * rows * group
    out = normalize(
        ids, keep, recv, everyone, gain.reshape(2, 1, outs), shift.reshape(2, 1, outs), cells
    )
    return out.reshape(slabs.shape)


def solution(mesh):
    fine = Mesh(mesh.devices.reshape(SIZES), AXES)
    x_spec = P(("xh", "z"), DEPTH, None, None, None)
    in_specs = (x_spec, P(None, None, None, None, ("xh", "z")), P(), P())
    return jax.shard_map(local, mesh=fine, in_specs=in_specs, out_specs=x_spec, check_vma=False)
```

time: 121 us -> 84.6 us (0.70)
  waiting for transfers between devices: 59.3 us -> 21.1 us
  starting transfers between devices: 15.2 us -> 37.1 us
  between operations: 13.5 us -> 0.5 us
  local copies, waits for them, and re-layouts: 11.3 us -> 3.77 us
  Pallas kernels: 18.2 us -> 20.7 us
  other arithmetic: 2.57 us -> 1.16 us
    all_gather x1 -> x0, waiting for transfers between devices: 25.8 us -> none  [local(): half = lax.all_gather(x_exchange(shard, core), 'z', axis=1, tiled=True)]
    ppermute x4 -> x15, starting transfers between devices: 9.15 us -> 31 us  [the longest x10 16.7 us: ring(): lax.ppermute(array, axes, [(i, (i + by) % count) for i in range(count)])]
    ppermute x4 -> x15, waiting for transfers between devices: 27.9 us -> 15.5 us  [the longest x10 11 us: ring(): lax.ppermute(array, axes, [(i, (i + by) % count) for i in range(count)])]
    unnamed x12 -> x8, local copies, waits for them, and re-layouts: 8.47 us -> 1.05 us
    all_to_all x1, starting transfers between devices: 5.31 us -> 3.39 us  [local(): everyone = lax.all_to_all(stats, DEPTH, 0, 0, tiled=True)]
    ppermute x1, starting transfers between devices: 0.77 us -> 2.67 us  [local(): recv = lax.ppermute(send, 'c', SWAP)]
    pallas_call x1 -> x3, Pallas kernels: 14.7 us -> 16.4 us  [the longest x2 9.38 us: second_conv(): pl.pallas_call(functools.partial(second_kernel, rows=rows, width=width, k...]
    select_n x2 -> x1, other arithmetic: 2.15 us -> 0.67 us  [chip_planes(): return jnp.where(core == 0, low, high)]
  transfers between devices with their start and end apart: 7 -> 17, of which waited for: 6 -> 7; matrix products, arithmetic and copies ran while one was open for 1% -> 4% of each run, Pallas kernels for 1% -> 16%
where the time goes in v3:
time: 84.6 us; the launch traced here: 84.3 us
  starting transfers between devices  37.1 us (44%)
  waiting for transfers between devices  21.1 us (25%)
  Pallas kernels  20.7 us (24%)
  local copies, waits for them, and re-layouts  3.77 us (4%)
  other arithmetic  1.16 us (1%)
    ppermute x10, starting transfers between devices, ring(): lax.ppermute(array, axes, [(i, (i + by) % count) for i in range(count)])  16.7 us
    ppermute x3, starting transfers between devices, from_z(): return lax.ppermute(array, ('xh', 'z', 'xl', 'c'), perm)  11.2 us
    ppermute x10, waiting for transfers between devices, ring(): lax.ppermute(array, axes, [(i, (i + by) % count) for i in range(count)])  11 us
    pallas_call x2, Pallas kernels, second_conv(): pl.pallas_call(functools.partial(second_kernel, rows=rows, width=width, k...  9.38 us
    pallas_call x1, Pallas kernels, first_conv(): pl.pallas_call(functools.partial(first_kernel, rows=rows, width=width), g...  7.03 us
    all_to_all x1, waiting for transfers between devices, local(): everyone = lax.all_to_all(stats, DEPTH, 0, 0, tiled=True)  5.56 us
    ppermute x3, waiting for transfers between devices, from_z(): return lax.ppermute(array, ('xh', 'z', 'xl', 'c'), perm)  4.54 us
    all_to_all x1, starting transfers between devices, local(): everyone = lax.all_to_all(stats, DEPTH, 0, 0, tiled=True)  3.39 us
  transfers between devices with their start and end apart: 17, of which 7 were waited for; matrix products, arithmetic and copies ran while one was open for 4% of the time, Pallas kernels for 16%

profile of v3, /device:TPU:1, one launch (start us, length us, event | category | flops | bytes accessed | tf_op | source)
XLA Modules:
  0.0 84.3 jit_solution(17719735612936628646)
XLA Ops:
  1.1 5.3 %collective-permute-start = (bf16[14,24,384]{2,1,0:T(8,128)(2,1)S(1)}, bf16[14,24,384]{2,1,0:T(8,128)(2,1)S(1)}, u32[]{:S(2)}, u32[]{:S(2)}) collective-permute-start(bf16[14,24,384]{2,1,0:T(8,128)(2,1)S(1)} %constant_dynamic-slice_fusion.1), channel_id=1, source_target_pairs={{0,16},{1,146},{2,18},{3,144},{128,19},{129,145},{130,17},{131,147... | collective-permute-start | bytes 774152 | tf_op jit(solution)/shard_map/ppermute | solution.py:226
  6.4 4.0 %collective-permute-start.6 = (bf16[14,24,384]{2,1,0:T(8,128)(2,1)S(1)}, bf16[14,24,384]{2,1,0:T(8,128)(2,1)S(1)}, u32[]{:S(2)}, u32[]{:S(2)}) collective-permute-start(bf16[14,24,384]{2,1,0:T(8,128)(2,1)S(1)} %constant_dynamic-slice_fusion.1), channel_id=1, source_target_pairs={{0,112},{1,242},{2,114},{3,240},{128,115},{129,241},{130,113},{131... | collective-permute-start | bytes 774152 | tf_op jit(solution)/shard_map/ppermute | solution.py:226
  10.4 1.9 %collective-permute-start.3 = (bf16[14,24,384]{2,1,0:T(8,128)(2,1)S(1)}, bf16[14,24,384]{2,1,0:T(8,128)(2,1)S(1)}, u32[]{:S(2)}, u32[]{:S(2)}) collective-permute-start(bf16[14,24,384]{2,1,0:T(8,128)(2,1)S(1)} %constant_dynamic-slice_fusion.1), channel_id=1, source_target_pairs={{0,0},{1,130},{2,2},{3,128},{128,3},{129,129},{130,1},{131,131},{1... | collective-permute-start | bytes 774152 | tf_op jit(solution)/shard_map/ppermute | solution.py:226
  12.5 4.5 %collective-permute-done = bf16[14,24,384]{2,1,0:T(8,128)(2,1)S(1)} collective-permute-done((bf16[14,24,384]{2,1,0:T(8,128)(2,1)S(1)}, bf16[14,24,384]{2,1,0:T(8,128)(2,1)S(1)}, u32[]{:S(2)}, u32[]{:S(2)}) %collective-permute-start) | collective-permute-done | bytes 258080 | tf_op jit(solution)/shard_map/ppermute | solution.py:226
  17.0 1.0 %constant_dynamic-slice_fusion = bf16[1,512,384]{2,1,0:T(8,128)(2,1)S(1)} fusion(bf16[2,512,384]{2,1,0:T(8,128)(2,1)} %bitcast.99, s32[]{:T(128)S(6)} %select_n.119), kind=kLoop, calls=%fused_computation.29 | loop fusion | bytes 786436 | tf_op jit(solution)/shard_map/dynamic_slice | solution.py:204
  18.1 1.9 %collective-permute-start.1 = (bf16[1,512,384]{2,1,0:T(8,128)(2,1)S(1)}, bf16[1,512,384]{2,1,0:T(8,128)(2,1)S(1)}, u32[]{:S(2)}, u32[]{:S(2)}) collective-permute-start(bf16[1,512,384]{2,1,0:T(8,128)(2,1)S(1)} %constant_dynamic-slice_fusion), channel_id=1, source_target_pairs={{1,2},{2,1},{3,4},{4,3},{5,6},{6,5},{7,8},{8,7},{9,10},{10,9},{11,... | collective-permute-start | bytes 1179656 | tf_op jit(solution)/shard_map/ppermute | solution.py:205
  20.1 2.7 %collective-permute-start.7 = (bf16[14,24,384]{2,1,0:T(8,128)(2,1)S(1)}, bf16[14,24,384]{2,1,0:T(8,128)(2,1)S(1)}, u32[]{:S(2)}, u32[]{:S(2)}) collective-permute-start(bf16[14,24,384]{2,1,0:T(8,128)(2,1)S(1)} %collective-permute-done.6), channel_id=1, source_target_pairs={{0,112},{16,0},{32,16},{48,32},{64,48},{80,64},{96,80},{112,96},{1... | collective-permute-start | bytes 774152 | tf_op jit(solution)/shard_map/ppermute | solution.py:231
  23.3 2.8 %collective-permute-done.7 = bf16[14,24,384]{2,1,0:T(8,128)(2,1)S(1)} collective-permute-done((bf16[14,24,384]{2,1,0:T(8,128)(2,1)S(1)}, bf16[14,24,384]{2,1,0:T(8,128)(2,1)S(1)}, u32[]{:S(2)}, u32[]{:S(2)}) %collective-permute-start.7) | collective-permute-done | bytes 258080 | tf_op jit(solution)/shard_map/ppermute | solution.py:231
  26.1 4.6 %collective-permute-start.8 = (bf16[2,14,24,384]{3,2,1,0:T(8,128)(2,1)S(1)}, bf16[2,14,24,384]{3,2,1,0:T(8,128)(2,1)S(1)}, u32[]{:S(2)}, u32[]{:S(2)}) collective-permute-start(bf16[2,14,24,384]{3,2,1,0:T(8,128)(2,1)S(1)} %pad_maximum_fusion.2), channel_id=1, source_target_pairs={{0,130},{2,0},{128,2},{130,128},{1,131},{3,1},{129,3},{131,129},{4... | collective-permute-start | bytes 1548296 | tf_op jit(solution)/shard_map/ppermute | solution.py:231
  30.9 3.5 %collective-permute-start.12 = (bf16[14,24,384]{2,1,0:T(8,128)(2,1)S(1)}, bf16[14,24,384]{2,1,0:T(8,128)(2,1)S(1)}, u32[]{:S(2)}, u32[]{:S(2)}) collective-permute-start(bf16[14,24,384]{2,1,0:T(8,128)(2,1)S(1)} %collective-permute-done.7), channel_id=1, source_target_pairs={{0,112},{16,0},{32,16},{48,32},{64,48},{80,64},{96,80},{112,96},{1... | collective-permute-start | bytes 774152 | tf_op jit(solution)/shard_map/ppermute | solution.py:231
  34.7 1.1 %collective-permute-start.2 = (bf16[3,512,384]{2,1,0:T(8,128)(2,1)S(1)}, bf16[3,512,384]{2,1,0:T(8,128)(2,1)S(1)}, u32[]{:S(2)}, u32[]{:S(2)}) collective-permute-start(bf16[3,512,384]{2,1,0:T(8,128)(2,1)S(1)} %pad_maximum_fusion), channel_id=1, source_target_pairs={{0,1},{1,0},{2,3},{3,2},{4,5},{5,4},{6,7},{7,6},{8,9},{9,8},{10,11... | collective-permute-start | bytes 3538952 | tf_op jit(solution)/shard_map/ppermute | solution.py:207
  35.8 3.4 %collective-permute-done.12 = bf16[14,24,384]{2,1,0:T(8,128)(2,1)S(1)} collective-permute-done((bf16[14,24,384]{2,1,0:T(8,128)(2,1)S(1)}, bf16[14,24,384]{2,1,0:T(8,128)(2,1)S(1)}, u32[]{:S(2)}, u32[]{:S(2)}) %collective-permute-start.12) | collective-permute-done | bytes 258080 | tf_op jit(solution)/shard_map/ppermute | solution.py:231
  39.2 3.5 %collective-permute-start.13 = (bf16[7,24,384]{2,1,0:T(8,128)(2,1)S(1)}, bf16[7,24,384]{2,1,0:T(8,128)(2,1)S(1)}, u32[]{:S(2)}, u32[]{:S(2)}) collective-permute-start(bf16[7,24,384]{2,1,0:T(8,128)(2,1)S(1)} %slice.60), channel_id=1, source_target_pairs={{0,112},{16,0},{32,16},{48,32},{64,48},{80,64},{96,80},{112,96},{1... | collective-permute-start | bytes 387080 | tf_op jit(solution)/shard_map/ppermute | solution.py:231
  42.9 1.7 %collective-permute-done.13 = bf16[7,24,384]{2,1,0:T(8,128)(2,1)S(1)} collective-permute-done((bf16[7,24,384]{2,1,0:T(8,128)(2,1)S(1)}, bf16[7,24,384]{2,1,0:T(8,128)(2,1)S(1)}, u32[]{:S(2)}, u32[]{:S(2)}) %collective-permute-start.13) | collective-permute-done | bytes 129056 | tf_op jit(solution)/shard_map/ppermute | solution.py:231
  45.4 2.7 %collective-permute-done.10 = bf16[7,24,384]{2,1,0:T(8,128)(2,1)S(1)} collective-permute-done((bf16[7,24,384]{2,1,0:T(8,128)(2,1)S(1)}, bf16[7,24,384]{2,1,0:T(8,128)(2,1)S(1)}, u32[]{:S(2)}, u32[]{:S(2)}) %collective-permute-start.10) | collective-permute-done | bytes 129056 | tf_op jit(solution)/shard_map/ppermute | solution.py:231
  48.2 1.6 %collective-permute-start.11 = (bf16[21,24,384]{2,1,0:T(8,128)(2,1)S(1)}, bf16[21,24,384]{2,1,0:T(8,128)(2,1)S(1)}, u32[]{:S(2)}, u32[]{:S(2)}) collective-permute-start(bf16[21,24,384]{2,1,0:T(8,128)(2,1)S(1)} %pad_maximum_fusion.3), channel_id=1, source_target_pairs={{0,4},{4,8},{8,12},{12,0},{1,5},{5,9},{9,13},{13,1},{2,6},{6,10},{... | collective-permute-start | bytes 1161224 | tf_op jit(solution)/shard_map/ppermute | solution.py:231
  51.6 1.6 %shard_map.46.x_ref = bf16[6,576,1152]{2,1,0:T(8,128)(2,1)S(1)} custom-call(bf16[6,512,384]{2,1,0:T(8,128)(2,1)S(1)} %maximum_select_fusion.x_ref), custom_call_target="tpu_custom_call" | custom-call | bytes 12000000 | tf_op jit(solution)/shard_map/pallas_call | solution.py:41
  53.2 7.0 %shard_map.47.acc_ref = f32[4,512,192]{2,1,0:T(8,128)S(1)} custom-call(s32[3]{0:T(128)S(1)} %pad_add_fusion.ids_ref, bf16[6,576,1152]{2,1,0:T(8,128)(2,1)S(1)} %shard_map.46.x_ref, bf16[14,192,384]{2,1,0:T(8,128)(2,1)S(1)} %bitcast.98), custom_call_target="tpu_custom_call" | custom-call | flops 5000000000 | bytes 12000000 | tf_op jit(solution)/shard_map/pallas_call | solution.py:119
  60.5 4.7 %shard_map.48 = (f32[2,512,256]{2,1,0:T(8,128)}, f32[8,192]{1,0:T(8,128)S(1)}) custom-call(s32[3]{0:T(128)S(1)} %pad_add_fusion.ids_ref, bf16[6,576,1152]{2,1,0:T(8,128)(2,1)S(1)} %shard_map.46.x_ref, bf16[14,192,384]{2,1,0:T(8,128)(2,1)S(1)} %bitcast.96, f32[4,512,192]{2,1,0:T(8,128)S(1)} %shard_map.47.acc_ref, f32[8,192]{1,0:T(8,128)S(1)} %broadcast_in_dim.55.before_ref), custom_call_target="tpu_custom_call" | custom-call | flops 2000000000 | bytes 8000000 | tf_op jit(solution)/shard_map/pallas_call | solution.py:138
  65.2 2.7 %collective-permute-start.15 = (f32[2,512,256]{2,1,0:T(8,128)}, f32[2,512,256]{2,1,0:T(8,128)S(1)}, u32[]{:S(2)}, u32[]{:S(2)}) collective-permute-start(f32[2,512,256]{2,1,0:T(8,128)} %get-tuple-element.17), channel_id=1, source_target_pairs={{0,1},{1,0},{2,3},{3,2},{4,5},{5,4},{6,7},{7,6},{8,9},{9,8},{10,11... | collective-permute-start | bytes 3145736 | tf_op jit(solution)/shard_map/ppermute | solution.py:289
  67.9 4.6 %shard_map.49 = (f32[2,512,192]{2,1,0:T(8,128)S(1)}, f32[16,1,384]{2,1,0:T(1,128)}) custom-call(s32[3]{0:T(128)S(1)} %pad_add_fusion.ids_ref, bf16[6,576,1152]{2,1,0:T(8,128)(2,1)S(1)} %shard_map.46.x_ref, bf16[14,192,384]{2,1,0:T(8,128)(2,1)S(1)} %bitcast.97, f32[4,512,192]{2,1,0:T(8,128)S(1)} %shard_map.47.acc_ref, f32[8,192]{1,0:T(8,128)S(1)} %get-tuple-element.15.before_ref), custom_call_target="tpu_custom_call" | custom-call | flops 2000000000 | bytes 8000000 | tf_op jit(solution)/shard_map/pallas_call | solution.py:138
  72.5 3.4 %all-to-all-start = ((f32[16,1,384]{2,1,0:T(1,128)}), f32[16,1,384]{2,1,0:T(1,128)S(1)}, u32[]{:S(2)}, u32[]{:S(2)}) async-start(f32[16,1,384]{2,1,0:T(1,128)} %get-tuple-element.18), calls=%async_computation | async-start | bytes 49152 | tf_op jit(solution)/shard_map/all_to_all | solution.py:291
  76.1 5.6 %all-to-all-done.stats_ref = f32[16,1,384]{2,1,0:T(1,128)S(1)} async-done(((f32[16,1,384]{2,1,0:T(1,128)}), f32[16,1,384]{2,1,0:T(1,128)S(1)}, u32[]{:S(2)}, u32[]{:S(2)}) %all-to-all-start) | async-done | bytes 24608 | tf_op jit(solution)/shard_map/all_to_all | solution.py:291
  81.7 2.6 %shard_map.50 = bf16[2,512,384]{2,1,0:T(8,128)(2,1)} custom-call(s32[3]{0:T(128)S(1)} %pad_add_fusion.ids_ref, f32[2,512,192]{2,1,0:T(8,128)S(1)} %get-tuple-element.16.keep_ref, f32[2,512,256]{2,1,0:T(8,128)S(1)} %collective-permute-done.15.recv_ref, f32[16,1,384]{2,1,0:T(1,128)S(1)} %all-to-all-done.stats_ref, f32[2,1,192]{2,1,0:T(1,128)S(1)} %reshape.21.gain_ref, ...), custom_call_target="tpu_custom_call" | custom-call | flops 4000000 | bytes 3000000 | tf_op jit(solution)/shard_map/pallas_call | solution.py:188
  (59 shorter events, 5.3 us)
Async XLA Ops:
  0.0 1.0 %copy-start = (bf16[3,3,3,384,24]{3,4,2,1,0:T(8,128)(2,1)S(1)}, bf16[3,3,3,384,24]{3,4,2,1,0:T(8,128)(2,1)}, u32[]{:S(2)}) copy-start(bf16[3,3,3,384,24]{3,4,2,1,0:T(8,128)(2,1)} %param.5) | copy-start | bytes 1492996
  1.1 16.0 %collective-permute-start = (bf16[14,24,384]{2,1,0:T(8,128)(2,1)S(1)}, bf16[14,24,384]{2,1,0:T(8,128)(2,1)S(1)}, u32[]{:S(2)}, u32[]{:S(2)}) collective-permute-start(bf16[14,24,384]{2,1,0:T(8,128)(2,1)S(1)} %constant_dynamic-slice_fusion.1), channel_id=1, source_target_pairs={{0,16},{1,146},{2,18},{3,144},{128,19},{129,145},{130,17},{131,147... | collective-permute-start | bytes 774152 | tf_op jit(solution)/shard_map/ppermute | solution.py:226
  6.4 13.7 %collective-permute-start.6 = (bf16[14,24,384]{2,1,0:T(8,128)(2,1)S(1)}, bf16[14,24,384]{2,1,0:T(8,128)(2,1)S(1)}, u32[]{:S(2)}, u32[]{:S(2)}) collective-permute-start(bf16[14,24,384]{2,1,0:T(8,128)(2,1)S(1)} %constant_dynamic-slice_fusion.1), channel_id=1, source_target_pairs={{0,112},{1,242},{2,114},{3,240},{128,115},{129,241},{130,113},{131... | collective-permute-start | bytes 774152 | tf_op jit(solution)/shard_map/ppermute | solution.py:226
  10.4 12.4 %collective-permute-start.3 = (bf16[14,24,384]{2,1,0:T(8,128)(2,1)S(1)}, bf16[14,24,384]{2,1,0:T(8,128)(2,1)S(1)}, u32[]{:S(2)}, u32[]{:S(2)}) collective-permute-start(bf16[14,24,384]{2,1,0:T(8,128)(2,1)S(1)} %constant_dynamic-slice_fusion.1), channel_id=1, source_target_pairs={{0,0},{1,130},{2,2},{3,128},{128,3},{129,129},{130,1},{131,131},{1... | collective-permute-start | bytes 774152 | tf_op jit(solution)/shard_map/ppermute | solution.py:226
  18.1 16.4 %collective-permute-start.1 = (bf16[1,512,384]{2,1,0:T(8,128)(2,1)S(1)}, bf16[1,512,384]{2,1,0:T(8,128)(2,1)S(1)}, u32[]{:S(2)}, u32[]{:S(2)}) collective-permute-start(bf16[1,512,384]{2,1,0:T(8,128)(2,1)S(1)} %constant_dynamic-slice_fusion), channel_id=1, source_target_pairs={{1,2},{2,1},{3,4},{4,3},{5,6},{6,5},{7,8},{8,7},{9,10},{10,9},{11,... | collective-permute-start | bytes 1179656 | tf_op jit(solution)/shard_map/ppermute | solution.py:205
  20.0 10.7 %collective-permute-start.4 = (bf16[14,24,384]{2,1,0:T(8,128)(2,1)S(1)}, bf16[14,24,384]{2,1,0:T(8,128)(2,1)S(1)}, u32[]{:S(2)}, u32[]{:S(2)}) collective-permute-start(bf16[14,24,384]{2,1,0:T(8,128)(2,1)S(1)} %collective-permute-done), channel_id=1, source_target_pairs={{0,16},{16,32},{32,48},{48,64},{64,80},{80,96},{96,112},{112,0},{1... | collective-permute-start | bytes 774152 | tf_op jit(solution)/shard_map/ppermute | solution.py:231
  20.1 5.9 %collective-permute-start.7 = (bf16[14,24,384]{2,1,0:T(8,128)(2,1)S(1)}, bf16[14,24,384]{2,1,0:T(8,128)(2,1)S(1)}, u32[]{:S(2)}, u32[]{:S(2)}) collective-permute-start(bf16[14,24,384]{2,1,0:T(8,128)(2,1)S(1)} %collective-permute-done.6), channel_id=1, source_target_pairs={{0,112},{16,0},{32,16},{48,32},{64,48},{80,64},{96,80},{112,96},{1... | collective-permute-start | bytes 774152 | tf_op jit(solution)/shard_map/ppermute | solution.py:231
  23.2 11.3 %copy-start.1 = (bf16[1,2,16,32,384]{4,3,2,1,0:T(8,128)(2,1)S(1)}, bf16[1,2,16,32,384]{4,3,2,1,0:T(8,128)(2,1)}, u32[]{:S(2)}) copy-start(bf16[1,2,16,32,384]{4,3,2,1,0:T(8,128)(2,1)} %param.4) | copy-start | bytes 2359300
  26.1 24.5 %collective-permute-start.8 = (bf16[2,14,24,384]{3,2,1,0:T(8,128)(2,1)S(1)}, bf16[2,14,24,384]{3,2,1,0:T(8,128)(2,1)S(1)}, u32[]{:S(2)}, u32[]{:S(2)}) collective-permute-start(bf16[2,14,24,384]{3,2,1,0:T(8,128)(2,1)S(1)} %pad_maximum_fusion.2), channel_id=1, source_target_pairs={{0,130},{2,0},{128,2},{130,128},{1,131},{3,1},{129,3},{131,129},{4... | collective-permute-start | bytes 1548296 | tf_op jit(solution)/shard_map/ppermute | solution.py:231
  30.8 19.3 %collective-permute-start.5 = (bf16[3,14,24,384]{3,2,1,0:T(8,128)(2,1)S(1)}, bf16[3,14,24,384]{3,2,1,0:T(8,128)(2,1)S(1)}, u32[]{:S(2)}, u32[]{:S(2)}) collective-permute-start(bf16[3,14,24,384]{3,2,1,0:T(8,128)(2,1)S(1)} %pad_maximum_fusion.1), channel_id=1, source_target_pairs={{0,2},{2,128},{128,130},{130,0},{1,3},{3,129},{129,131},{131,1},{4... | collective-permute-start | bytes 2322440 | tf_op jit(solution)/shard_map/ppermute | solution.py:231
  30.9 8.3 %collective-permute-start.12 = (bf16[14,24,384]{2,1,0:T(8,128)(2,1)S(1)}, bf16[14,24,384]{2,1,0:T(8,128)(2,1)S(1)}, u32[]{:S(2)}, u32[]{:S(2)}) collective-permute-start(bf16[14,24,384]{2,1,0:T(8,128)(2,1)S(1)} %collective-permute-done.7), channel_id=1, source_target_pairs={{0,112},{16,0},{32,16},{48,32},{64,48},{80,64},{96,80},{112,96},{1... | collective-permute-start | bytes 774152 | tf_op jit(solution)/shard_map/ppermute | solution.py:231
  34.4 8.3 %collective-permute-start.9 = (bf16[14,24,384]{2,1,0:T(8,128)(2,1)S(1)}, bf16[14,24,384]{2,1,0:T(8,128)(2,1)S(1)}, u32[]{:S(2)}, u32[]{:S(2)}) collective-permute-start(bf16[14,24,384]{2,1,0:T(8,128)(2,1)S(1)} %collective-permute-done.4), channel_id=1, source_target_pairs={{0,16},{16,32},{32,48},{48,64},{64,80},{80,96},{96,112},{112,0},{1... | collective-permute-start | bytes 774152 | tf_op jit(solution)/shard_map/ppermute | solution.py:231
  34.7 16.1 %collective-permute-start.2 = (bf16[3,512,384]{2,1,0:T(8,128)(2,1)S(1)}, bf16[3,512,384]{2,1,0:T(8,128)(2,1)S(1)}, u32[]{:S(2)}, u32[]{:S(2)}) collective-permute-start(bf16[3,512,384]{2,1,0:T(8,128)(2,1)S(1)} %pad_maximum_fusion), channel_id=1, source_target_pairs={{0,1},{1,0},{2,3},{3,2},{4,5},{5,4},{6,7},{7,6},{8,9},{9,8},{10,11... | collective-permute-start | bytes 3538952 | tf_op jit(solution)/shard_map/ppermute | solution.py:207
  39.2 5.4 %collective-permute-start.13 = (bf16[7,24,384]{2,1,0:T(8,128)(2,1)S(1)}, bf16[7,24,384]{2,1,0:T(8,128)(2,1)S(1)}, u32[]{:S(2)}, u32[]{:S(2)}) collective-permute-start(bf16[7,24,384]{2,1,0:T(8,128)(2,1)S(1)} %slice.60), channel_id=1, source_target_pairs={{0,112},{16,0},{32,16},{48,32},{64,48},{80,64},{96,80},{112,96},{1... | collective-permute-start | bytes 387080 | tf_op jit(solution)/shard_map/ppermute | solution.py:231
  42.7 5.4 %collective-permute-start.10 = (bf16[7,24,384]{2,1,0:T(8,128)(2,1)S(1)}, bf16[7,24,384]{2,1,0:T(8,128)(2,1)S(1)}, u32[]{:S(2)}, u32[]{:S(2)}) collective-permute-start(bf16[7,24,384]{2,1,0:T(8,128)(2,1)S(1)} %slice.59), channel_id=1, source_target_pairs={{0,16},{16,32},{32,48},{48,64},{64,80},{80,96},{96,112},{112,0},{1... | collective-permute-start | bytes 387080 | tf_op jit(solution)/shard_map/ppermute | solution.py:231
  44.7 15.6 %collective-permute-start.14 = (bf16[21,24,384]{2,1,0:T(8,128)(2,1)S(1)}, bf16[21,24,384]{2,1,0:T(8,128)(2,1)S(1)}, u32[]{:S(2)}, u32[]{:S(2)}) collective-permute-start(bf16[21,24,384]{2,1,0:T(8,128)(2,1)S(1)} %pad_maximum_fusion.4), channel_id=1, source_target_pairs={{0,12},{4,0},{8,4},{12,8},{1,13},{5,1},{9,5},{13,9},{2,14},{6,2},{... | collective-permute-start | bytes 1161224 | tf_op jit(solution)/shard_map/ppermute | solution.py:231
  48.2 12.1 %collective-permute-start.11 = (bf16[21,24,384]{2,1,0:T(8,128)(2,1)S(1)}, bf16[21,24,384]{2,1,0:T(8,128)(2,1)S(1)}, u32[]{:S(2)}, u32[]{:S(2)}) collective-permute-start(bf16[21,24,384]{2,1,0:T(8,128)(2,1)S(1)} %pad_maximum_fusion.3), channel_id=1, source_target_pairs={{0,4},{4,8},{8,12},{12,0},{1,5},{5,9},{9,13},{13,1},{2,6},{6,10},{... | collective-permute-start | bytes 1161224 | tf_op jit(solution)/shard_map/ppermute | solution.py:231
  65.2 16.5 %collective-permute-start.15 = (f32[2,512,256]{2,1,0:T(8,128)}, f32[2,512,256]{2,1,0:T(8,128)S(1)}, u32[]{:S(2)}, u32[]{:S(2)}) collective-permute-start(f32[2,512,256]{2,1,0:T(8,128)} %get-tuple-element.17), channel_id=1, source_target_pairs={{0,1},{1,0},{2,3},{3,2},{4,5},{5,4},{6,7},{7,6},{8,9},{9,8},{10,11... | collective-permute-start | bytes 3145736 | tf_op jit(solution)/shard_map/ppermute | solution.py:289
  67.9 8.1 %copy-start.2 = (f32[384]{0:T(512)S(1)}, f32[384]{0:T(512)}, u32[]{:S(2)}) copy-start(f32[384]{0:T(512)} %param.6) | copy-start | bytes 4612
  67.9 8.1 %copy-start.3 = (f32[384]{0:T(512)S(1)}, f32[384]{0:T(512)}, u32[]{:S(2)}) copy-start(f32[384]{0:T(512)} %param.7) | copy-start | bytes 4612
  72.5 9.1 %all-to-all-start = ((f32[16,1,384]{2,1,0:T(1,128)}), f32[16,1,384]{2,1,0:T(1,128)S(1)}, u32[]{:S(2)}, u32[]{:S(2)}) async-start(f32[16,1,384]{2,1,0:T(1,128)} %get-tuple-element.18), calls=%async_computation | async-start | bytes 49152 | tf_op jit(solution)/shard_map/all_to_all | solution.py:291

commit v4 on v3

--- a/solution.py
+++ b/solution.py
@@ -66,106 +66,91 @@
 
 def first_kernel(ids_ref, x_ref, w_ref, acc_ref, *, rows, width):
     core, colour = ids_ref[0], ids_ref[1]
-    j = pl.program_id(0)
-    plane = (j + 2 * (1 - core)) % 4
-
-    @pl.when(colour == 0)
-    def _():
-        acc_ref[0] = half_conv(x_ref, w_ref, plane, LOW_TAPS, rows, width)
-
-    @pl.when(colour != 0)
-    def _():
-        acc_ref[0] = half_conv(x_ref, w_ref, plane, HIGH_TAPS, rows, width)
-
-
-def second_kernel(ids_ref, x_ref, w_ref, acc_ref, before_ref, out_ref, stats_ref, total_ref, sum_ref, *, rows, width, keep):
+
+    def run(taps):
+        for j in range(4):
+            plane = (j + 2 * (1 - core)) % 4
+            acc_ref[j] = half_conv(x_ref, w_ref, plane, taps, rows, width)
+
+    pl.when(colour == 0)(lambda: run(LOW_TAPS))
+    pl.when(colour != 0)(lambda: run(HIGH_TAPS))
+
+
+def second_kernel(ids_ref, x_ref, w_ref, acc_ref, before_ref, out_ref, stats_ref, sum_ref, *, rows, width, keep):
     core, colour = ids_ref[0], ids_ref[1]
-    j = pl.program_id(0)
-    outs = total_ref.shape[1]
-
-    @pl.when(j == 0)
-    def _():
-        sum_ref[...] = before_ref[...] if keep else jnp.zeros_like(sum_ref)
-
-    plane = (j + 2 * keep + 2 * (1 - core)) % 4
-
-    @pl.when(colour == 0)
-    def _():
-        total_ref[...] = acc_ref[0] + half_conv(x_ref, w_ref, plane, HIGH_TAPS, rows, width)
-
-    @pl.when(colour != 0)
-    def _():
-        total_ref[...] = acc_ref[0] + half_conv(x_ref, w_ref, plane, LOW_TAPS, rows, width)
-
-    total = total_ref[...]
-    sum_ref[0:1, :] += jnp.sum(total, axis=0, keepdims=True)
-    sum_ref[1:2, :] += jnp.sum(total * total, axis=0, keepdims=True)
-    out_ref[0, :, 0:outs] = total
-    if not keep:
-        out_ref[0, :, outs:] = jnp.zeros((rows, out_ref.shape[2] - outs), jnp.float32)
-
-    @pl.when(j == 1)
-    def _():
-        if keep:
-            row = jnp.concatenate([sum_ref[0:1, :], sum_ref[1:2, :]], axis=1)
-            stats_ref[...] = jnp.broadcast_to(row[None], stats_ref.shape)
-        else:
-            stats_ref[...] = sum_ref[...]
+    outs = acc_ref.shape[2]
+    sum_ref[...] = before_ref[...] if keep else jnp.zeros_like(sum_ref)
+
+    def run(taps):
+        for j in range(2):
+            plane = (j + 2 * keep + 2 * (1 - core)) % 4
+            total = acc_ref[j + 2 * keep] + half_conv(x_ref, w_ref, plane, taps, rows, width)
+            sum_ref[0:1, :] += jnp.sum(total, axis=0, keepdims=True)
+            sum_ref[1:2, :] += jnp.sum(total * total, axis=0, keepdims=True)
+            out_ref[j, :, 0:outs] = total
+            if not keep:
+                out_ref[j, :, outs:] = jnp.zeros((rows, out_ref.shape[2] - outs), jnp.float32)
+
+    pl.when(colour == 0)(lambda: run(HIGH_TAPS))
+    pl.when(colour != 0)(lambda: run(LOW_TAPS))
+    if keep:
+        row = jnp.concatenate([sum_ref[0:1, :], sum_ref[1:2, :]], axis=1)
+        stats_ref[...] = jnp.broadcast_to(row[None], stats_ref.shape)
+    else:
+        stats_ref[...] = sum_ref[...]
+
+
+def in_vmem(kernel, count, out_shape, scratch, flops, limit):
+    whole = pl.BlockSpec(memory_space=pltpu.VMEM)
+    outs = [whole] * len(out_shape)
+    return pl.pallas_call(
+        kernel,
+        grid_spec=pltpu.PrefetchScalarGridSpec(
+            num_scalar_prefetch=1, grid=(), in_specs=[whole] * count, out_specs=outs, scratch_shapes=scratch
+        ),
+        out_shape=out_shape,
+        compiler_params=pltpu.CompilerParams(vmem_limit_bytes=limit << 20),
+        cost_estimate=pl.CostEstimate(flops=flops, bytes_accessed=8_000_000, transcendentals=0),
+    )
 
 
 def first_conv(ids, wide, own, rows, width):
-    outs = own.shape[1]
-    whole = pl.BlockSpec(memory_space=pltpu.VMEM)
-    return pl.pallas_call(
-        functools.partial(first_kernel, rows=rows, width=width),
-        grid_spec=pltpu.PrefetchScalarGridSpec(
-            num_scalar_prefetch=1,
-            grid=(4,),
-            in_specs=[whole, whole],
-            out_specs=pl.BlockSpec((1, rows, outs), lambda j, ids: (j, 0, 0)),
-        ),
-        out_shape=jax.ShapeDtypeStruct((4, rows, outs), jnp.float32),
-        compiler_params=pltpu.CompilerParams(vmem_limit_bytes=40 << 20),
-        cost_estimate=pl.CostEstimate(flops=5 * 10**9, bytes_accessed=12_000_000, transcendentals=0),
-    )(ids, wide, own)
+    kernel = functools.partial(first_kernel, rows=rows, width=width)
+    out = [jax.ShapeDtypeStruct((4, rows, own.shape[1]), jnp.float32)]
+    return in_vmem(kernel, 2, out, [], 5 * 10**9, 40)(ids, wide, own)[0]
 
 
 def second_conv(ids, wide, other, acc, before, rows, width, group, keep):
     outs = other.shape[1]
     lanes = outs if keep else PADDED
     stats = (group, 1, 2 * outs) if keep else (8, outs)
-    whole = pl.BlockSpec(memory_space=pltpu.VMEM)
-    return pl.pallas_call(
-        functools.partial(second_kernel, rows=rows, width=width, keep=keep),
-        grid_spec=pltpu.PrefetchScalarGridSpec(
-            num_scalar_prefetch=1,
-            grid=(2,),
-            in_specs=[whole, whole, pl.BlockSpec((1, rows, outs), lambda j, ids: (j + 2 * keep, 0, 0)), whole],
-            out_specs=[
-                pl.BlockSpec((1, rows, lanes), lambda j, ids: (j, 0, 0)),
-                pl.BlockSpec(stats, lambda j, ids: (0,) * len(stats)),
-            ],
-            scratch_shapes=[pltpu.VMEM((rows, outs), jnp.float32), pltpu.VMEM((8, outs), jnp.float32)],
-        ),
-        out_shape=[jax.ShapeDtypeStruct((2, rows, lanes), jnp.float32), jax.ShapeDtypeStruct(stats, jnp.float32)],
-        compiler_params=pltpu.CompilerParams(vmem_limit_bytes=40 << 20),
-        cost_estimate=pl.CostEstimate(flops=2 * 10**9, bytes_accessed=8_000_000, transcendentals=0),
-    )(ids, wide, other, acc, before)
-
-
-def norm_kernel(ids_ref, keep_ref, recv_ref, stats_ref, gain_ref, shift_ref, o_ref, *, cells):
+    kernel = functools.partial(second_kernel, rows=rows, width=width, keep=keep)
+    out = [jax.ShapeDtypeStruct((2, rows, lanes), jnp.float32), jax.ShapeDtypeStruct(stats, jnp.float32)]
+    scratch = [pltpu.VMEM((8, outs), jnp.float32)]
+    return in_vmem(kernel, 4, out, scratch, 2 * 10**9, 40)(ids, wide, other, acc, before)
+
+
+def norm_kernel(ids_ref, keep_ref, recv_ref, stats_ref, gain_ref, shift_ref, o_ref, mean_ref, scale_ref, *, cells):
     first = ids_ref[0] == 0
     outs = keep_ref.shape[2]
-    keep, recv = keep_ref[0], recv_ref[0, :, 0:outs]
+    plane, tile = pl.program_id(0), o_ref.shape[1]
+
+    @pl.when((plane == 0) & (pl.program_id(1) == 0))
+    def _():
+        for half in range(2):
+            sums = stats_ref[half]
+            for chip in range(1, stats_ref.shape[0] // 2):
+                sums = sums + stats_ref[2 * chip + half]
+            mean = sums[:, 0:outs] / cells
+            variance = sums[:, outs : 2 * outs] / cells - mean * mean
+            mean_ref[half] = mean
+            scale_ref[half] = gain_ref[half] / jnp.sqrt(variance + EPS)
+
+    where = pl.ds(pl.multiple_of(pl.program_id(1) * tile, tile), tile)
+    keep, recv = keep_ref[plane, where, :], recv_ref[plane, where, 0:outs]
     for half in range(2):
-        sums = stats_ref[half]
-        for chip in range(1, stats_ref.shape[0] // 2):
-            sums = sums + stats_ref[2 * chip + half]
-        mean = sums[:, 0:outs] / cells
-        variance = sums[:, outs : 2 * outs] / cells - mean * mean
-        scale = gain_ref[half] / jnp.sqrt(variance + EPS)
         conv_out = jnp.where(first, keep, recv) if half == 0 else jnp.where(first, recv, keep)
-        normed = (conv_out - mean) * scale + shift_ref[half]
+        normed = (conv_out - mean_ref[half]) * scale_ref[half] + shift_ref[half]
         active = jnp.where(normed >= 0, normed, 0.01 * normed).astype(o_ref.dtype)
         o_ref[0, :, half * outs : (half + 1) * outs] = active
 
@@ -176,14 +161,9 @@
     spec = pltpu.PrefetchScalarGridSpec(
         num_scalar_prefetch=1,
         grid=(planes, rows // tile),
-        in_specs=[
-            pl.BlockSpec((1, tile, outs), lambda i, j, ids: (i, j, 0)),
-            pl.BlockSpec((1, tile, PADDED), lambda i, j, ids: (i, j, 0)),
-            pl.BlockSpec(stats.shape, lambda i, j, ids: (0, 0, 0)),
-            pl.BlockSpec((2, 1, outs), lambda i, j, ids: (0, 0, 0)),
-            pl.BlockSpec((2, 1, outs), lambda i, j, ids: (0, 0, 0)),
-        ],
+        in_specs=[pl.BlockSpec(memory_space=pltpu.VMEM)] * 5,
         out_specs=pl.BlockSpec((1, tile, 2 * outs), lambda i, j, ids: (i, j, 0)),
+        scratch_shapes=[pltpu.VMEM((2, 1, outs), jnp.float32)] * 2,
     )
     return pl.pallas_call(
         functools.partial(norm_kernel, cells=cells),
@@ -236,7 +216,7 @@
     return lax.dynamic_update_slice(buffer, piece[:, None], (tap, where, 0, 0))
 
 
-def gather_weights(shard, core):
+def gather_weights(shard, core, widened):
     xh, zi, y, xl = (lax.axis_index(n) for n in ("xh", "z", "y", "xl"))
     to_xl = jnp.where(core == xh, xl, 1 - xl)
     part = lax.dynamic_slice_in_dim(shard, 13 * ((y + to_xl) % 2), 14, axis=0)
@@ -246,6 +226,8 @@
     far_up, far_down = ring(jnp.stack([here, up, up2]), xs, 1), ring(jnp.stack([down, down2]), xs, -1)
     up3, down3 = ring(up2, zs, 1), ring(down2, zs, -1)
     top, bottom = ring(up3[:7], zs, 1), ring(down3[7:], zs, -1)
+    wide = widened()
+    top, bottom, wide = lax.optimization_barrier((top, bottom, wide))
     far_top = ring(jnp.concatenate([up3, top]), ys, 1)
     far_bottom = ring(jnp.concatenate([down3, bottom]), ys, -1)
 
@@ -253,20 +235,20 @@
     for r, piece in ((0, here), (1, up), (-1, down), (2, up2), (-2, down2), (3, up3), (-3, down3)):
         own = put(own, piece, zi, r)
     own = put(put(own, top, zi, 4), bottom, zi, 4, 7)
-    other = jnp.zeros_like(own)
-    for n in range(3):
-        other = put(other, far_up[n], zi, n)
-    for n in range(2):
-        other = put(other, far_down[n], zi, -n - 1)
     merged = (14, 8 * shard.shape[1], shard.shape[2])
 
     def finish(gate):
-        low, high, _ = lax.optimization_barrier((far_top, far_bottom, gate))
-        full = put(put(other, low[:14], zi, 3), high[:14], zi, -3)
-        full = put(put(full, low[14:], zi, 4), high[14:], zi, 4, 7)
-        return full.reshape(merged)
-
-    return own.reshape(merged), finish, up
+        ups, downs, low, high, _ = lax.optimization_barrier((far_up, far_down, far_top, far_bottom, gate))
+        other = jnp.zeros_like(own)
+        for n in range(3):
+            other = put(other, ups[n], zi, n)
+        for n in range(2):
+            other = put(other, downs[n], zi, -n - 1)
+        other = put(put(other, low[:14], zi, 3), high[:14], zi, -3)
+        other = put(put(other, low[14:], zi, 4), high[14:], zi, 4, 7)
+        return other.reshape(merged)
+
+    return own.reshape(merged), finish, wide
 
 
 def local(slabs, kernel, gain, shift):
@@ -280,9 +262,10 @@
     group = SIZES[2] * SIZES[3] * SIZES[4]
 
     shard = jnp.transpose(kernel, (0, 1, 2, 4, 3)).reshape(27, kernel.shape[4], chans)
-    own, finish, first = gather_weights(shard, core)
-    slab, _ = lax.optimization_barrier((slabs[0].reshape(planes, rows, chans), first))
-    wide = widen(chip_planes(slab, core), width)
+    def widened():
+        return widen(chip_planes(slabs[0].reshape(planes, rows, chans), core), width)
+
+    own, finish, wide = gather_weights(shard, core, widened)
     acc = first_conv(ids, wide, own, rows, width)
     other = finish(acc)
     send, sums = second_conv(ids, wide, other, acc, jnp.zeros((8, outs), jnp.float32), rows, width, group, 0)

time: 84.6 us -> 79.4 us (0.939)
  waiting for transfers between devices: 21.1 us -> 16.8 us
  Pallas kernels: 20.7 us -> 19.4 us
    ppermute x10, waiting for transfers between devices: 11 us -> 5.27 us  [ring(): lax.ppermute(array, axes, [(i, (i + by) % count) for i in range(count)])]
    ppermute x1, waiting for transfers between devices: 0.01 us -> 4.21 us  [chip_planes(): halo = lax.ppermute(edge, DEPTH, pairs)]
    ppermute x3, waiting for transfers between devices: 4.54 us -> 1.68 us  [from_z(): return lax.ppermute(array, ('xh', 'z', 'xl', 'c'), perm)]
    all_to_all x1, starting transfers between devices: 3.39 us -> 6.12 us  [local(): everyone = lax.all_to_all(stats, DEPTH, 0, 0, tiled=True)]
    ppermute x10, starting transfers between devices: 16.7 us -> 14.8 us  [ring(): lax.ppermute(array, axes, [(i, (i + by) % count) for i in range(count)])]
    pallas_call x3, Pallas kernels: 16.4 us -> 15.2 us  [the longest x2 8.64 us: second_conv(): in_vmem(kernel, 4, out, scratch, 2 * 10 ** 9, 40)]
    ppermute x1, starting transfers between devices: 1.12 us -> 0.09 us  [chip_planes(): other = lax.ppermute(mine, 'c', SWAP)]
  transfers between devices with their start and end apart: 17 -> 17, of which waited for: 7 -> 5; matrix products, arithmetic and copies ran while one was open for 4% -> 4% of each run, Pallas kernels for 16% -> 16%
where the time goes in v4:
time: 79.4 us; the launch traced here: 79.2 us
  starting transfers between devices  37.6 us (47%)
  Pallas kernels  19.4 us (24%)
  waiting for transfers between devices  16.8 us (21%)
  local copies, waits for them, and re-layouts  3.77 us (5%)
  other arithmetic  1.19 us (1%)
    ppermute x10, starting transfers between devices, ring(): lax.ppermute(array, axes, [(i, (i + by) % count) for i in range(count)])  14.8 us
    ppermute x3, starting transfers between devices, from_z(): return lax.ppermute(array, ('xh', 'z', 'xl', 'c'), perm)  11.2 us
    pallas_call x2, Pallas kernels, second_conv(): in_vmem(kernel, 4, out, scratch, 2 * 10 ** 9, 40)  8.64 us
    pallas_call x1, Pallas kernels, first_conv(): return in_vmem(kernel, 2, out, [], 5 * 10 ** 9, 40)(ids, wide, own)[0]  6.57 us
    all_to_all x1, starting transfers between devices, local(): everyone = lax.all_to_all(stats, DEPTH, 0, 0, tiled=True)  6.12 us
    all_to_all x1, waiting for transfers between devices, local(): everyone = lax.all_to_all(stats, DEPTH, 0, 0, tiled=True)  5.62 us
    ppermute x10, waiting for transfers between devices, ring(): lax.ppermute(array, axes, [(i, (i + by) % count) for i in range(count)])  5.27 us
    ppermute x1, waiting for transfers between devices, chip_planes(): halo = lax.ppermute(edge, DEPTH, pairs)  4.21 us
  transfers between devices with their start and end apart: 17, of which 5 were waited for; matrix products, arithmetic and copies ran while one was open for 4% of the time, Pallas kernels for 16%

profile of v4, /device:TPU:1, one launch (start us, length us, event | category | flops | bytes accessed | tf_op | source)
XLA Modules:
  0.0 79.2 jit_solution(10838634005681836367)
XLA Ops:
  0.0 1.0 %copy-done = bf16[3,3,3,384,24]{3,4,2,1,0:T(8,128)(2,1)S(1)} copy-done((bf16[3,3,3,384,24]{3,4,2,1,0:T(8,128)(2,1)S(1)}, bf16[3,3,3,384,24]{3,4,2,1,0:T(8,128)(2,1)}, u32[]{:S(2)}) %copy-start) | copy-done | bytes 497688
  1.1 5.3 %collective-permute-start = (bf16[14,24,384]{2,1,0:T(8,128)(2,1)S(1)}, bf16[14,24,384]{2,1,0:T(8,128)(2,1)S(1)}, u32[]{:S(2)}, u32[]{:S(2)}) collective-permute-start(bf16[14,24,384]{2,1,0:T(8,128)(2,1)S(1)} %constant_dynamic-slice_fusion.1), channel_id=1, source_target_pairs={{0,16},{1,146},{2,18},{3,144},{128,19},{129,145},{130,17},{131,147... | collective-permute-start | bytes 774152 | tf_op jit(solution)/shard_map/ppermute | solution.py:206
  6.4 4.0 %collective-permute-start.4 = (bf16[14,24,384]{2,1,0:T(8,128)(2,1)S(1)}, bf16[14,24,384]{2,1,0:T(8,128)(2,1)S(1)}, u32[]{:S(2)}, u32[]{:S(2)}) collective-permute-start(bf16[14,24,384]{2,1,0:T(8,128)(2,1)S(1)} %constant_dynamic-slice_fusion.1), channel_id=1, source_target_pairs={{0,112},{1,242},{2,114},{3,240},{128,115},{129,241},{130,113},{131... | collective-permute-start | bytes 774152 | tf_op jit(solution)/shard_map/ppermute | solution.py:206
  10.4 1.9 %collective-permute-start.10 = (bf16[14,24,384]{2,1,0:T(8,128)(2,1)S(1)}, bf16[14,24,384]{2,1,0:T(8,128)(2,1)S(1)}, u32[]{:S(2)}, u32[]{:S(2)}) collective-permute-start(bf16[14,24,384]{2,1,0:T(8,128)(2,1)S(1)} %constant_dynamic-slice_fusion.1), channel_id=1, source_target_pairs={{0,0},{1,130},{2,2},{3,128},{128,3},{129,129},{130,1},{131,131},{1... | collective-permute-start | bytes 774152 | tf_op jit(solution)/shard_map/ppermute | solution.py:206
  12.3 1.0 %constant_dynamic-slice_fusion = bf16[1,512,384]{2,1,0:T(8,128)(2,1)S(1)} fusion(bf16[2,512,384]{2,1,0:T(8,128)(2,1)} %bitcast.89, s32[]{:T(128)S(6)} %select_n.119), kind=kLoop, calls=%fused_computation.24 | loop fusion | bytes 786436 | tf_op jit(solution)/shard_map/dynamic_slice | solution.py:184
  13.4 2.1 %collective-permute-start.8 = (bf16[1,512,384]{2,1,0:T(8,128)(2,1)S(1)}, bf16[1,512,384]{2,1,0:T(8,128)(2,1)S(1)}, u32[]{:S(2)}, u32[]{:S(2)}) collective-permute-start(bf16[1,512,384]{2,1,0:T(8,128)(2,1)S(1)} %constant_dynamic-slice_fusion), channel_id=1, source_target_pairs={{1,2},{2,1},{3,4},{4,3},{5,6},{6,5},{7,8},{8,7},{9,10},{10,9},{11,... | collective-permute-start | bytes 1179656 | tf_op jit(solution)/shard_map/ppermute | solution.py:185
  15.6 1.4 %collective-permute-done = bf16[14,24,384]{2,1,0:T(8,128)(2,1)S(1)} collective-permute-done((bf16[14,24,384]{2,1,0:T(8,128)(2,1)S(1)}, bf16[14,24,384]{2,1,0:T(8,128)(2,1)S(1)}, u32[]{:S(2)}, u32[]{:S(2)}) %collective-permute-start) | collective-permute-done | bytes 258080 | tf_op jit(solution)/shard_map/ppermute | solution.py:206
  17.1 2.7 %collective-permute-start.5 = (bf16[14,24,384]{2,1,0:T(8,128)(2,1)S(1)}, bf16[14,24,384]{2,1,0:T(8,128)(2,1)S(1)}, u32[]{:S(2)}, u32[]{:S(2)}) collective-permute-start(bf16[14,24,384]{2,1,0:T(8,128)(2,1)S(1)} %collective-permute-done.4), channel_id=1, source_target_pairs={{0,112},{16,0},{32,16},{48,32},{64,48},{80,64},{96,80},{112,96},{1... | collective-permute-start | bytes 774152 | tf_op jit(solution)/shard_map/ppermute | solution.py:211
  20.5 4.2 %collective-permute-done.8 = bf16[1,512,384]{2,1,0:T(8,128)(2,1)S(1)} collective-permute-done((bf16[1,512,384]{2,1,0:T(8,128)(2,1)S(1)}, bf16[1,512,384]{2,1,0:T(8,128)(2,1)S(1)}, u32[]{:S(2)}, u32[]{:S(2)}) %collective-permute-start.8) | collective-permute-done | bytes 393248 | tf_op jit(solution)/shard_map/ppermute | solution.py:185
  25.1 2.6 %collective-permute-start.11 = (bf16[3,14,24,384]{3,2,1,0:T(8,128)(2,1)S(1)}, bf16[3,14,24,384]{3,2,1,0:T(8,128)(2,1)S(1)}, u32[]{:S(2)}, u32[]{:S(2)}) collective-permute-start(bf16[3,14,24,384]{3,2,1,0:T(8,128)(2,1)S(1)} %pad_maximum_fusion.1), channel_id=1, source_target_pairs={{0,2},{2,128},{128,130},{130,0},{1,3},{3,129},{129,131},{131,1},{4... | collective-permute-start | bytes 2322440 | tf_op jit(solution)/shard_map/ppermute | solution.py:211
  27.8 0.7 collective-permute-start.12
  28.5 2.7 %collective-permute-start.6 = (bf16[14,24,384]{2,1,0:T(8,128)(2,1)S(1)}, bf16[14,24,384]{2,1,0:T(8,128)(2,1)S(1)}, u32[]{:S(2)}, u32[]{:S(2)}) collective-permute-start(bf16[14,24,384]{2,1,0:T(8,128)(2,1)S(1)} %collective-permute-done.5), channel_id=1, source_target_pairs={{0,112},{16,0},{32,16},{48,32},{64,48},{80,64},{96,80},{112,96},{1... | collective-permute-start | bytes 774152 | tf_op jit(solution)/shard_map/ppermute | solution.py:211
  31.3 5.2 %collective-permute-done.2 = bf16[14,24,384]{2,1,0:T(8,128)(2,1)S(1)} collective-permute-done((bf16[14,24,384]{2,1,0:T(8,128)(2,1)S(1)}, bf16[14,24,384]{2,1,0:T(8,128)(2,1)S(1)}, u32[]{:S(2)}, u32[]{:S(2)}) %collective-permute-start.2) | collective-permute-done | bytes 258080 | tf_op jit(solution)/shard_map/ppermute | solution.py:211
  36.7 2.7 %collective-permute-start.7 = (bf16[7,24,384]{2,1,0:T(8,128)(2,1)S(1)}, bf16[7,24,384]{2,1,0:T(8,128)(2,1)S(1)}, u32[]{:S(2)}, u32[]{:S(2)}) collective-permute-start(bf16[7,24,384]{2,1,0:T(8,128)(2,1)S(1)} %slice.53), channel_id=1, source_target_pairs={{0,112},{16,0},{32,16},{48,32},{64,48},{80,64},{96,80},{112,96},{1... | collective-permute-start | bytes 387080 | tf_op jit(solution)/shard_map/ppermute | solution.py:211
  40.4 1.6 %shard_map.46.x_ref = bf16[6,576,1152]{2,1,0:T(8,128)(2,1)S(1)} custom-call(bf16[6,512,384]{2,1,0:T(8,128)(2,1)S(1)} %maximum_select_fusion.x_ref), custom_call_target="tpu_custom_call" | custom-call | bytes 12000000 | tf_op jit(solution)/shard_map/pallas_call | solution.py:41
  42.1 1.6 %collective-permute-start.13 = (bf16[21,24,384]{2,1,0:T(8,128)(2,1)S(1)}, bf16[21,24,384]{2,1,0:T(8,128)(2,1)S(1)}, u32[]{:S(2)}, u32[]{:S(2)}) collective-permute-start(bf16[21,24,384]{2,1,0:T(8,128)(2,1)S(1)} %pad_maximum_fusion.3), channel_id=1, source_target_pairs={{0,4},{4,8},{8,12},{12,0},{1,5},{5,9},{9,13},{13,1},{2,6},{6,10},{... | collective-permute-start | bytes 1161224 | tf_op jit(solution)/shard_map/ppermute | solution.py:211
  43.9 1.6 %collective-permute-start.14 = (bf16[21,24,384]{2,1,0:T(8,128)(2,1)S(1)}, bf16[21,24,384]{2,1,0:T(8,128)(2,1)S(1)}, u32[]{:S(2)}, u32[]{:S(2)}) collective-permute-start(bf16[21,24,384]{2,1,0:T(8,128)(2,1)S(1)} %pad_maximum_fusion.4), channel_id=1, source_target_pairs={{0,12},{4,0},{8,4},{12,8},{1,13},{5,1},{9,5},{13,9},{2,14},{6,2},{... | collective-permute-start | bytes 1161224 | tf_op jit(solution)/shard_map/ppermute | solution.py:211
  45.4 6.6 %shard_map.47.acc_ref = f32[4,512,192]{2,1,0:T(8,128)S(1)} custom-call(s32[3]{0:T(128)S(1)} %pad_add_fusion.ids_ref, bf16[6,576,1152]{2,1,0:T(8,128)(2,1)S(1)} %shard_map.46.x_ref, bf16[14,192,384]{2,1,0:T(8,128)(2,1)S(1)} %bitcast.88), custom_call_target="tpu_custom_call" | custom-call | flops 5000000000 | bytes 8000000 | tf_op jit(solution)/shard_map/pallas_call | solution.py:120
  52.8 4.5 %shard_map.48 = (f32[2,512,256]{2,1,0:T(8,128)}, f32[8,192]{1,0:T(8,128)S(1)}) custom-call(s32[3]{0:T(128)S(1)} %pad_add_fusion.ids_ref, bf16[6,576,1152]{2,1,0:T(8,128)(2,1)S(1)} %shard_map.46.x_ref, bf16[14,192,384]{2,1,0:T(8,128)(2,1)S(1)} %bitcast.86, f32[4,512,192]{2,1,0:T(8,128)S(1)} %shard_map.47.acc_ref, f32[8,192]{1,0:T(8,128)S(1)} %broadcast_in_dim.55.before_ref), custom_call_target="tpu_custom_call" | custom-call | flops 2000000000 | bytes 8000000 | tf_op jit(solution)/shard_map/pallas_call | solution.py:130
  57.3 3.3 %collective-permute-start.15 = (f32[2,512,256]{2,1,0:T(8,128)}, f32[2,512,256]{2,1,0:T(8,128)S(1)}, u32[]{:S(2)}, u32[]{:S(2)}) collective-permute-start(f32[2,512,256]{2,1,0:T(8,128)} %get-tuple-element.25), channel_id=1, source_target_pairs={{0,1},{1,0},{2,3},{3,2},{4,5},{5,4},{6,7},{7,6},{8,9},{9,8},{10,11... | collective-permute-start | bytes 3145736 | tf_op jit(solution)/shard_map/ppermute | solution.py:272
  60.6 4.2 %shard_map.49 = (f32[2,512,192]{2,1,0:T(8,128)S(1)}, f32[16,1,384]{2,1,0:T(1,128)}) custom-call(s32[3]{0:T(128)S(1)} %pad_add_fusion.ids_ref, bf16[6,576,1152]{2,1,0:T(8,128)(2,1)S(1)} %shard_map.46.x_ref, bf16[14,192,384]{2,1,0:T(8,128)(2,1)S(1)} %bitcast.87, f32[4,512,192]{2,1,0:T(8,128)S(1)} %shard_map.47.acc_ref, f32[8,192]{1,0:T(8,128)S(1)} %get-tuple-element.23.before_ref), custom_call_target="tpu_custom_call" | custom-call | flops 2000000000 | bytes 8000000 | tf_op jit(solution)/shard_map/pallas_call | solution.py:130
  64.7 6.1 %all-to-all-start = ((f32[16,1,384]{2,1,0:T(1,128)}), f32[16,1,384]{2,1,0:T(1,128)S(1)}, u32[]{:S(2)}, u32[]{:S(2)}) async-start(f32[16,1,384]{2,1,0:T(1,128)} %get-tuple-element.26), calls=%async_computation | async-start | bytes 49152 | tf_op jit(solution)/shard_map/all_to_all | solution.py:274
  71.0 5.6 %all-to-all-done.stats_ref = f32[16,1,384]{2,1,0:T(1,128)S(1)} async-done(((f32[16,1,384]{2,1,0:T(1,128)}), f32[16,1,384]{2,1,0:T(1,128)S(1)}, u32[]{:S(2)}, u32[]{:S(2)}) %all-to-all-start) | async-done | bytes 24608 | tf_op jit(solution)/shard_map/all_to_all | solution.py:274
  76.7 2.5 %shard_map.50 = bf16[2,512,384]{2,1,0:T(8,128)(2,1)} custom-call(s32[3]{0:T(128)S(1)} %pad_add_fusion.ids_ref, f32[2,512,192]{2,1,0:T(8,128)S(1)} %get-tuple-element.24.keep_ref, f32[2,512,256]{2,1,0:T(8,128)S(1)} %collective-permute-done.15.recv_ref, f32[16,1,384]{2,1,0:T(1,128)S(1)} %all-to-all-done.stats_ref, f32[2,1,192]{2,1,0:T(1,128)S(1)} %reshape.21.gain_ref, ...), custom_call_target="tpu_custom_call" | custom-call | flops 4000000 | bytes 3000000 | tf_op jit(solution)/shard_map/pallas_call | solution.py:168
  (59 shorter events, 3.4 us)
Async XLA Ops:
  0.0 1.0 %copy-start = (bf16[3,3,3,384,24]{3,4,2,1,0:T(8,128)(2,1)S(1)}, bf16[3,3,3,384,24]{3,4,2,1,0:T(8,128)(2,1)}, u32[]{:S(2)}) copy-start(bf16[3,3,3,384,24]{3,4,2,1,0:T(8,128)(2,1)} %param.5) | copy-start | bytes 1492996
  1.1 16.0 %collective-permute-start = (bf16[14,24,384]{2,1,0:T(8,128)(2,1)S(1)}, bf16[14,24,384]{2,1,0:T(8,128)(2,1)S(1)}, u32[]{:S(2)}, u32[]{:S(2)}) collective-permute-start(bf16[14,24,384]{2,1,0:T(8,128)(2,1)S(1)} %constant_dynamic-slice_fusion.1), channel_id=1, source_target_pairs={{0,16},{1,146},{2,18},{3,144},{128,19},{129,145},{130,17},{131,147... | collective-permute-start | bytes 774152 | tf_op jit(solution)/shard_map/ppermute | solution.py:206
  6.4 10.7 %collective-permute-start.4 = (bf16[14,24,384]{2,1,0:T(8,128)(2,1)S(1)}, bf16[14,24,384]{2,1,0:T(8,128)(2,1)S(1)}, u32[]{:S(2)}, u32[]{:S(2)}) collective-permute-start(bf16[14,24,384]{2,1,0:T(8,128)(2,1)S(1)} %constant_dynamic-slice_fusion.1), channel_id=1, source_target_pairs={{0,112},{1,242},{2,114},{3,240},{128,115},{129,241},{130,113},{131... | collective-permute-start | bytes 774152 | tf_op jit(solution)/shard_map/ppermute | solution.py:206
  10.4 9.7 %collective-permute-start.10 = (bf16[14,24,384]{2,1,0:T(8,128)(2,1)S(1)}, bf16[14,24,384]{2,1,0:T(8,128)(2,1)S(1)}, u32[]{:S(2)}, u32[]{:S(2)}) collective-permute-start(bf16[14,24,384]{2,1,0:T(8,128)(2,1)S(1)} %constant_dynamic-slice_fusion.1), channel_id=1, source_target_pairs={{0,0},{1,130},{2,2},{3,128},{128,3},{129,129},{130,1},{131,131},{1... | collective-permute-start | bytes 774152 | tf_op jit(solution)/shard_map/ppermute | solution.py:206
  13.4 11.4 %copy-start.1 = (bf16[1,2,16,32,384]{4,3,2,1,0:T(8,128)(2,1)S(1)}, bf16[1,2,16,32,384]{4,3,2,1,0:T(8,128)(2,1)}, u32[]{:S(2)}) copy-start(bf16[1,2,16,32,384]{4,3,2,1,0:T(8,128)(2,1)} %param.4) | copy-start | bytes 2359300
  13.4 11.4 %collective-permute-start.8 = (bf16[1,512,384]{2,1,0:T(8,128)(2,1)S(1)}, bf16[1,512,384]{2,1,0:T(8,128)(2,1)S(1)}, u32[]{:S(2)}, u32[]{:S(2)}) collective-permute-start(bf16[1,512,384]{2,1,0:T(8,128)(2,1)S(1)} %constant_dynamic-slice_fusion), channel_id=1, source_target_pairs={{1,2},{2,1},{3,4},{4,3},{5,6},{6,5},{7,8},{8,7},{9,10},{10,9},{11,... | collective-permute-start | bytes 1179656 | tf_op jit(solution)/shard_map/ppermute | solution.py:185
  17.0 7.9 %collective-permute-start.1 = (bf16[14,24,384]{2,1,0:T(8,128)(2,1)S(1)}, bf16[14,24,384]{2,1,0:T(8,128)(2,1)S(1)}, u32[]{:S(2)}, u32[]{:S(2)}) collective-permute-start(bf16[14,24,384]{2,1,0:T(8,128)(2,1)S(1)} %collective-permute-done), channel_id=1, source_target_pairs={{0,16},{16,32},{32,48},{48,64},{64,80},{80,96},{96,112},{112,0},{1... | collective-permute-start | bytes 774152 | tf_op jit(solution)/shard_map/ppermute | solution.py:211
  17.1 10.6 %collective-permute-start.5 = (bf16[14,24,384]{2,1,0:T(8,128)(2,1)S(1)}, bf16[14,24,384]{2,1,0:T(8,128)(2,1)S(1)}, u32[]{:S(2)}, u32[]{:S(2)}) collective-permute-start(bf16[14,24,384]{2,1,0:T(8,128)(2,1)S(1)} %collective-permute-done.4), channel_id=1, source_target_pairs={{0,112},{16,0},{32,16},{48,32},{64,48},{80,64},{96,80},{112,96},{1... | collective-permute-start | bytes 774152 | tf_op jit(solution)/shard_map/ppermute | solution.py:211
  24.9 14.7 %collective-permute-start.9 = (bf16[3,512,384]{2,1,0:T(8,128)(2,1)S(1)}, bf16[3,512,384]{2,1,0:T(8,128)(2,1)S(1)}, u32[]{:S(2)}, u32[]{:S(2)}) collective-permute-start(bf16[3,512,384]{2,1,0:T(8,128)(2,1)S(1)} %pad_maximum_fusion), channel_id=1, source_target_pairs={{0,1},{1,0},{2,3},{3,2},{4,5},{5,4},{6,7},{7,6},{8,9},{9,8},{10,11... | collective-permute-start | bytes 3538952 | tf_op jit(solution)/shard_map/ppermute | solution.py:187
  25.1 26.9 %collective-permute-start.11 = (bf16[3,14,24,384]{3,2,1,0:T(8,128)(2,1)S(1)}, bf16[3,14,24,384]{3,2,1,0:T(8,128)(2,1)S(1)}, u32[]{:S(2)}, u32[]{:S(2)}) collective-permute-start(bf16[3,14,24,384]{3,2,1,0:T(8,128)(2,1)S(1)} %pad_maximum_fusion.1), channel_id=1, source_target_pairs={{0,2},{2,128},{128,130},{130,0},{1,3},{3,129},{129,131},{131,1},{4... | collective-permute-start | bytes 2322440 | tf_op jit(solution)/shard_map/ppermute | solution.py:211
  27.8 24.2 %collective-permute-start.12 = (bf16[2,14,24,384]{3,2,1,0:T(8,128)(2,1)S(1)}, bf16[2,14,24,384]{3,2,1,0:T(8,128)(2,1)S(1)}, u32[]{:S(2)}, u32[]{:S(2)}) collective-permute-start(bf16[2,14,24,384]{3,2,1,0:T(8,128)(2,1)S(1)} %pad_maximum_fusion.2), channel_id=1, source_target_pairs={{0,130},{2,0},{128,2},{130,128},{1,131},{3,1},{129,3},{131,129},{4... | collective-permute-start | bytes 1548296 | tf_op jit(solution)/shard_map/ppermute | solution.py:211
  28.5 8.0 %collective-permute-start.2 = (bf16[14,24,384]{2,1,0:T(8,128)(2,1)S(1)}, bf16[14,24,384]{2,1,0:T(8,128)(2,1)S(1)}, u32[]{:S(2)}, u32[]{:S(2)}) collective-permute-start(bf16[14,24,384]{2,1,0:T(8,128)(2,1)S(1)} %collective-permute-done.1), channel_id=1, source_target_pairs={{0,16},{16,32},{32,48},{48,64},{64,80},{80,96},{96,112},{112,0},{1... | collective-permute-start | bytes 774152 | tf_op jit(solution)/shard_map/ppermute | solution.py:211
  28.5 8.1 %collective-permute-start.6 = (bf16[14,24,384]{2,1,0:T(8,128)(2,1)S(1)}, bf16[14,24,384]{2,1,0:T(8,128)(2,1)S(1)}, u32[]{:S(2)}, u32[]{:S(2)}) collective-permute-start(bf16[14,24,384]{2,1,0:T(8,128)(2,1)S(1)} %collective-permute-done.5), channel_id=1, source_target_pairs={{0,112},{16,0},{32,16},{48,32},{64,48},{80,64},{96,80},{112,96},{1... | collective-permute-start | bytes 774152 | tf_op jit(solution)/shard_map/ppermute | solution.py:211
  36.6 5.5 %collective-permute-start.3 = (bf16[7,24,384]{2,1,0:T(8,128)(2,1)S(1)}, bf16[7,24,384]{2,1,0:T(8,128)(2,1)S(1)}, u32[]{:S(2)}, u32[]{:S(2)}) collective-permute-start(bf16[7,24,384]{2,1,0:T(8,128)(2,1)S(1)} %slice.52), channel_id=1, source_target_pairs={{0,16},{16,32},{32,48},{48,64},{64,80},{80,96},{96,112},{112,0},{1... | collective-permute-start | bytes 387080 | tf_op jit(solution)/shard_map/ppermute | solution.py:211
  36.7 5.3 %collective-permute-start.7 = (bf16[7,24,384]{2,1,0:T(8,128)(2,1)S(1)}, bf16[7,24,384]{2,1,0:T(8,128)(2,1)S(1)}, u32[]{:S(2)}, u32[]{:S(2)}) collective-permute-start(bf16[7,24,384]{2,1,0:T(8,128)(2,1)S(1)} %slice.53), channel_id=1, source_target_pairs={{0,112},{16,0},{32,16},{48,32},{64,48},{80,64},{96,80},{112,96},{1... | collective-permute-start | bytes 387080 | tf_op jit(solution)/shard_map/ppermute | solution.py:211
  42.1 9.9 %collective-permute-start.13 = (bf16[21,24,384]{2,1,0:T(8,128)(2,1)S(1)}, bf16[21,24,384]{2,1,0:T(8,128)(2,1)S(1)}, u32[]{:S(2)}, u32[]{:S(2)}) collective-permute-start(bf16[21,24,384]{2,1,0:T(8,128)(2,1)S(1)} %pad_maximum_fusion.3), channel_id=1, source_target_pairs={{0,4},{4,8},{8,12},{12,0},{1,5},{5,9},{9,13},{13,1},{2,6},{6,10},{... | collective-permute-start | bytes 1161224 | tf_op jit(solution)/shard_map/ppermute | solution.py:211
  43.9 8.2 %collective-permute-start.14 = (bf16[21,24,384]{2,1,0:T(8,128)(2,1)S(1)}, bf16[21,24,384]{2,1,0:T(8,128)(2,1)S(1)}, u32[]{:S(2)}, u32[]{:S(2)}) collective-permute-start(bf16[21,24,384]{2,1,0:T(8,128)(2,1)S(1)} %pad_maximum_fusion.4), channel_id=1, source_target_pairs={{0,12},{4,0},{8,4},{12,8},{1,13},{5,1},{9,5},{13,9},{2,14},{6,2},{... | collective-permute-start | bytes 1161224 | tf_op jit(solution)/shard_map/ppermute | solution.py:211
  57.3 19.4 %collective-permute-start.15 = (f32[2,512,256]{2,1,0:T(8,128)}, f32[2,512,256]{2,1,0:T(8,128)S(1)}, u32[]{:S(2)}, u32[]{:S(2)}) collective-permute-start(f32[2,512,256]{2,1,0:T(8,128)} %get-tuple-element.25), channel_id=1, source_target_pairs={{0,1},{1,0},{2,3},{3,2},{4,5},{5,4},{6,7},{7,6},{8,9},{9,8},{10,11... | collective-permute-start | bytes 3145736 | tf_op jit(solution)/shard_map/ppermute | solution.py:272
  60.6 10.3 %copy-start.2 = (f32[384]{0:T(512)S(1)}, f32[384]{0:T(512)}, u32[]{:S(2)}) copy-start(f32[384]{0:T(512)} %param.6) | copy-start | bytes 4612
  60.6 10.4 %copy-start.3 = (f32[384]{0:T(512)S(1)}, f32[384]{0:T(512)}, u32[]{:S(2)}) copy-start(f32[384]{0:T(512)} %param.7) | copy-start | bytes 4612
  64.7 11.9 %all-to-all-start = ((f32[16,1,384]{2,1,0:T(1,128)}), f32[16,1,384]{2,1,0:T(1,128)S(1)}, u32[]{:S(2)}, u32[]{:S(2)}) async-start(f32[16,1,384]{2,1,0:T(1,128)} %get-tuple-element.26), calls=%async_computation | async-start | bytes 49152 | tf_op jit(solution)/shard_map/all_to_all | solution.py:274

commit v5 on v4

--- a/solution.py
+++ b/solution.py
@@ -76,28 +76,27 @@
     pl.when(colour != 0)(lambda: run(HIGH_TAPS))
 
 
-def second_kernel(ids_ref, x_ref, w_ref, acc_ref, before_ref, out_ref, stats_ref, sum_ref, *, rows, width, keep):
+def second_kernel(ids_ref, x_ref, w_ref, acc_ref, send_ref, keep_ref, stats_ref, sum_ref, *, rows, width):
     core, colour = ids_ref[0], ids_ref[1]
     outs = acc_ref.shape[2]
-    sum_ref[...] = before_ref[...] if keep else jnp.zeros_like(sum_ref)
+    sum_ref[...] = jnp.zeros_like(sum_ref)
 
     def run(taps):
-        for j in range(2):
-            plane = (j + 2 * keep + 2 * (1 - core)) % 4
-            total = acc_ref[j + 2 * keep] + half_conv(x_ref, w_ref, plane, taps, rows, width)
+        for j in range(4):
+            plane = (j + 2 * (1 - core)) % 4
+            total = acc_ref[j] + half_conv(x_ref, w_ref, plane, taps, rows, width)
             sum_ref[0:1, :] += jnp.sum(total, axis=0, keepdims=True)
             sum_ref[1:2, :] += jnp.sum(total * total, axis=0, keepdims=True)
-            out_ref[j, :, 0:outs] = total
-            if not keep:
-                out_ref[j, :, outs:] = jnp.zeros((rows, out_ref.shape[2] - outs), jnp.float32)
+            if j < 2:
+                send_ref[j, :, 0:outs] = total
+                send_ref[j, :, outs:] = jnp.zeros((rows, send_ref.shape[2] - outs), jnp.float32)
+            else:
+                keep_ref[j - 2] = total
 
     pl.when(colour == 0)(lambda: run(HIGH_TAPS))
     pl.when(colour != 0)(lambda: run(LOW_TAPS))
-    if keep:
-        row = jnp.concatenate([sum_ref[0:1, :], sum_ref[1:2, :]], axis=1)
-        stats_ref[...] = jnp.broadcast_to(row[None], stats_ref.shape)
-    else:
-        stats_ref[...] = sum_ref[...]
+    row = jnp.concatenate([sum_ref[0:1, :], sum_ref[1:2, :]], axis=1)
+    stats_ref[...] = jnp.broadcast_to(row[None], stats_ref.shape)
 
 
 def in_vmem(kernel, count, out_shape, scratch, flops, limit):
@@ -120,14 +119,13 @@
     return in_vmem(kernel, 2, out, [], 5 * 10**9, 40)(ids, wide, own)[0]
 
 
-def second_conv(ids, wide, other, acc, before, rows, width, group, keep):
+def second_conv(ids, wide, other, acc, rows, width, group):
     outs = other.shape[1]
-    lanes = outs if keep else PADDED
-    stats = (group, 1, 2 * outs) if keep else (8, outs)
-    kernel = functools.partial(second_kernel, rows=rows, width=width, keep=keep)
-    out = [jax.ShapeDtypeStruct((2, rows, lanes), jnp.float32), jax.ShapeDtypeStruct(stats, jnp.float32)]
+    kernel = functools.partial(second_kernel, rows=rows, width=width)
+    shapes = ((2, rows, PADDED), (2, rows, outs), (group, 1, 2 * outs))
+    out = [jax.ShapeDtypeStruct(shape, jnp.float32) for shape in shapes]
     scratch = [pltpu.VMEM((8, outs), jnp.float32)]
-    return in_vmem(kernel, 4, out, scratch, 2 * 10**9, 40)(ids, wide, other, acc, before)
+    return in_vmem(kernel, 3, out, scratch, 5 * 10**9, 40)(ids, wide, other, acc)
 
 
 def norm_kernel(ids_ref, keep_ref, recv_ref, stats_ref, gain_ref, shift_ref, o_ref, mean_ref, scale_ref, *, cells):
@@ -157,7 +155,7 @@
 
 def normalize(ids, keep, recv, stats, gain, shift, cells):
     planes, rows, outs = keep.shape
-    tile = 256
+    tile = 512
     spec = pltpu.PrefetchScalarGridSpec(
         num_scalar_prefetch=1,
         grid=(planes, rows // tile),
@@ -268,9 +266,8 @@
     own, finish, wide = gather_weights(shard, core, widened)
     acc = first_conv(ids, wide, own, rows, width)
     other = finish(acc)
-    send, sums = second_conv(ids, wide, other, acc, jnp.zeros((8, outs), jnp.float32), rows, width, group, 0)
+    send, keep, stats = second_conv(ids, wide, other, acc, rows, width, group)
     recv = lax.ppermute(send, "c", SWAP)
-    keep, stats = second_conv(ids, wide, other, acc, sums, rows, width, group, 1)
     everyone = lax.all_to_all(stats, DEPTH, 0, 0, tiled=True)
     cells = planes * rows * group
     out = normalize(

time: 79.4 us -> 77.7 us (0.979)
  Pallas kernels: 19.4 us -> 17.6 us
    pallas_call x2 -> x1, Pallas kernels: 8.64 us -> 7.41 us  [second_conv(): in_vmem(kernel, 3, out, scratch, 5 * 10 ** 9, 40)(ids, wide, other, acc)]
  transfers between devices with their start and end apart: 17 -> 17, of which waited for: 5 -> 5; matrix products, arithmetic and copies ran while one was open for 4% -> 4% of each run, Pallas kernels for 16% -> 11%
where the time goes in v5:
time: 77.7 us; the launch traced here: 77.5 us
  starting transfers between devices  37.6 us (48%)
  Pallas kernels  17.6 us (23%)
  waiting for transfers between devices  16.8 us (22%)
  local copies, waits for them, and re-layouts  3.78 us (5%)
  other arithmetic  1.19 us (2%)
    ppermute x10, starting transfers between devices, ring(): lax.ppermute(array, axes, [(i, (i + by) % count) for i in range(count)])  14.8 us
    ppermute x3, starting transfers between devices, from_z(): return lax.ppermute(array, ('xh', 'z', 'xl', 'c'), perm)  11.2 us
    pallas_call x1, Pallas kernels, second_conv(): in_vmem(kernel, 3, out, scratch, 5 * 10 ** 9, 40)(ids, wide, other, acc)  7.41 us
    pallas_call x1, Pallas kernels, first_conv(): return in_vmem(kernel, 2, out, [], 5 * 10 ** 9, 40)(ids, wide, own)[0]  6.57 us
    all_to_all x1, starting transfers between devices, local(): everyone = lax.all_to_all(stats, DEPTH, 0, 0, tiled=True)  6.1 us
    all_to_all x1, waiting for transfers between devices, local(): everyone = lax.all_to_all(stats, DEPTH, 0, 0, tiled=True)  5.62 us
    ppermute x10, waiting for transfers between devices, ring(): lax.ppermute(array, axes, [(i, (i + by) % count) for i in range(count)])  5.27 us
    ppermute x1, waiting for transfers between devices, chip_planes(): halo = lax.ppermute(edge, DEPTH, pairs)  4.21 us
  transfers between devices with their start and end apart: 17, of which 5 were waited for; matrix products, arithmetic and copies ran while one was open for 4% of the time, Pallas kernels for 11%

profile of v5, /device:TPU:1, one launch (start us, length us, event | category | flops | bytes accessed | tf_op | source)
XLA Modules:
  0.0 77.5 jit_solution(14671567214418366352)
XLA Ops:
  0.0 1.0 %copy-done = bf16[3,3,3,384,24]{3,4,2,1,0:T(8,128)(2,1)S(1)} copy-done((bf16[3,3,3,384,24]{3,4,2,1,0:T(8,128)(2,1)S(1)}, bf16[3,3,3,384,24]{3,4,2,1,0:T(8,128)(2,1)}, u32[]{:S(2)}) %copy-start) | copy-done | bytes 497688
  1.1 5.3 %collective-permute-start = (bf16[14,24,384]{2,1,0:T(8,128)(2,1)S(1)}, bf16[14,24,384]{2,1,0:T(8,128)(2,1)S(1)}, u32[]{:S(2)}, u32[]{:S(2)}) collective-permute-start(bf16[14,24,384]{2,1,0:T(8,128)(2,1)S(1)} %constant_dynamic-slice_fusion.1), channel_id=1, source_target_pairs={{0,16},{1,146},{2,18},{3,144},{128,19},{129,145},{130,17},{131,147... | collective-permute-start | bytes 774152 | tf_op jit(solution)/shard_map/ppermute | solution.py:204
  6.4 4.0 %collective-permute-start.4 = (bf16[14,24,384]{2,1,0:T(8,128)(2,1)S(1)}, bf16[14,24,384]{2,1,0:T(8,128)(2,1)S(1)}, u32[]{:S(2)}, u32[]{:S(2)}) collective-permute-start(bf16[14,24,384]{2,1,0:T(8,128)(2,1)S(1)} %constant_dynamic-slice_fusion.1), channel_id=1, source_target_pairs={{0,112},{1,242},{2,114},{3,240},{128,115},{129,241},{130,113},{131... | collective-permute-start | bytes 774152 | tf_op jit(solution)/shard_map/ppermute | solution.py:204
  10.4 1.9 %collective-permute-start.10 = (bf16[14,24,384]{2,1,0:T(8,128)(2,1)S(1)}, bf16[14,24,384]{2,1,0:T(8,128)(2,1)S(1)}, u32[]{:S(2)}, u32[]{:S(2)}) collective-permute-start(bf16[14,24,384]{2,1,0:T(8,128)(2,1)S(1)} %constant_dynamic-slice_fusion.1), channel_id=1, source_target_pairs={{0,0},{1,130},{2,2},{3,128},{128,3},{129,129},{130,1},{131,131},{1... | collective-permute-start | bytes 774152 | tf_op jit(solution)/shard_map/ppermute | solution.py:204
  12.3 1.0 %constant_dynamic-slice_fusion = bf16[1,512,384]{2,1,0:T(8,128)(2,1)S(1)} fusion(bf16[2,512,384]{2,1,0:T(8,128)(2,1)} %bitcast.88, s32[]{:T(128)S(6)} %select_n.119), kind=kLoop, calls=%fused_computation.24 | loop fusion | bytes 786436 | tf_op jit(solution)/shard_map/dynamic_slice | solution.py:182
  13.4 2.1 %collective-permute-start.8 = (bf16[1,512,384]{2,1,0:T(8,128)(2,1)S(1)}, bf16[1,512,384]{2,1,0:T(8,128)(2,1)S(1)}, u32[]{:S(2)}, u32[]{:S(2)}) collective-permute-start(bf16[1,512,384]{2,1,0:T(8,128)(2,1)S(1)} %constant_dynamic-slice_fusion), channel_id=1, source_target_pairs={{1,2},{2,1},{3,4},{4,3},{5,6},{6,5},{7,8},{8,7},{9,10},{10,9},{11,... | collective-permute-start | bytes 1179656 | tf_op jit(solution)/shard_map/ppermute | solution.py:183
  15.6 1.4 %collective-permute-done = bf16[14,24,384]{2,1,0:T(8,128)(2,1)S(1)} collective-permute-done((bf16[14,24,384]{2,1,0:T(8,128)(2,1)S(1)}, bf16[14,24,384]{2,1,0:T(8,128)(2,1)S(1)}, u32[]{:S(2)}, u32[]{:S(2)}) %collective-permute-start) | collective-permute-done | bytes 258080 | tf_op jit(solution)/shard_map/ppermute | solution.py:204
  17.1 2.7 %collective-permute-start.5 = (bf16[14,24,384]{2,1,0:T(8,128)(2,1)S(1)}, bf16[14,24,384]{2,1,0:T(8,128)(2,1)S(1)}, u32[]{:S(2)}, u32[]{:S(2)}) collective-permute-start(bf16[14,24,384]{2,1,0:T(8,128)(2,1)S(1)} %collective-permute-done.4), channel_id=1, source_target_pairs={{0,112},{16,0},{32,16},{48,32},{64,48},{80,64},{96,80},{112,96},{1... | collective-permute-start | bytes 774152 | tf_op jit(solution)/shard_map/ppermute | solution.py:209
  20.5 4.2 %collective-permute-done.8 = bf16[1,512,384]{2,1,0:T(8,128)(2,1)S(1)} collective-permute-done((bf16[1,512,384]{2,1,0:T(8,128)(2,1)S(1)}, bf16[1,512,384]{2,1,0:T(8,128)(2,1)S(1)}, u32[]{:S(2)}, u32[]{:S(2)}) %collective-permute-start.8) | collective-permute-done | bytes 393248 | tf_op jit(solution)/shard_map/ppermute | solution.py:183
  25.1 2.6 %collective-permute-start.11 = (bf16[3,14,24,384]{3,2,1,0:T(8,128)(2,1)S(1)}, bf16[3,14,24,384]{3,2,1,0:T(8,128)(2,1)S(1)}, u32[]{:S(2)}, u32[]{:S(2)}) collective-permute-start(bf16[3,14,24,384]{3,2,1,0:T(8,128)(2,1)S(1)} %pad_maximum_fusion.1), channel_id=1, source_target_pairs={{0,2},{2,128},{128,130},{130,0},{1,3},{3,129},{129,131},{131,1},{4... | collective-permute-start | bytes 2322440 | tf_op jit(solution)/shard_map/ppermute | solution.py:209
  27.8 0.7 collective-permute-start.12
  28.5 2.7 %collective-permute-start.6 = (bf16[14,24,384]{2,1,0:T(8,128)(2,1)S(1)}, bf16[14,24,384]{2,1,0:T(8,128)(2,1)S(1)}, u32[]{:S(2)}, u32[]{:S(2)}) collective-permute-start(bf16[14,24,384]{2,1,0:T(8,128)(2,1)S(1)} %collective-permute-done.5), channel_id=1, source_target_pairs={{0,112},{16,0},{32,16},{48,32},{64,48},{80,64},{96,80},{112,96},{1... | collective-permute-start | bytes 774152 | tf_op jit(solution)/shard_map/ppermute | solution.py:209
  31.3 5.2 %collective-permute-done.2 = bf16[14,24,384]{2,1,0:T(8,128)(2,1)S(1)} collective-permute-done((bf16[14,24,384]{2,1,0:T(8,128)(2,1)S(1)}, bf16[14,24,384]{2,1,0:T(8,128)(2,1)S(1)}, u32[]{:S(2)}, u32[]{:S(2)}) %collective-permute-start.2) | collective-permute-done | bytes 258080 | tf_op jit(solution)/shard_map/ppermute | solution.py:209
  36.7 2.7 %collective-permute-start.7 = (bf16[7,24,384]{2,1,0:T(8,128)(2,1)S(1)}, bf16[7,24,384]{2,1,0:T(8,128)(2,1)S(1)}, u32[]{:S(2)}, u32[]{:S(2)}) collective-permute-start(bf16[7,24,384]{2,1,0:T(8,128)(2,1)S(1)} %slice.53), channel_id=1, source_target_pairs={{0,112},{16,0},{32,16},{48,32},{64,48},{80,64},{96,80},{112,96},{1... | collective-permute-start | bytes 387080 | tf_op jit(solution)/shard_map/ppermute | solution.py:209
  39.7 0.7 maximum_select_fusion.x_ref
  40.4 1.6 %shard_map.46.x_ref = bf16[6,576,1152]{2,1,0:T(8,128)(2,1)S(1)} custom-call(bf16[6,512,384]{2,1,0:T(8,128)(2,1)S(1)} %maximum_select_fusion.x_ref), custom_call_target="tpu_custom_call" | custom-call | bytes 12000000 | tf_op jit(solution)/shard_map/pallas_call | solution.py:41
  42.1 1.6 %collective-permute-start.13 = (bf16[21,24,384]{2,1,0:T(8,128)(2,1)S(1)}, bf16[21,24,384]{2,1,0:T(8,128)(2,1)S(1)}, u32[]{:S(2)}, u32[]{:S(2)}) collective-permute-start(bf16[21,24,384]{2,1,0:T(8,128)(2,1)S(1)} %pad_maximum_fusion.3), channel_id=1, source_target_pairs={{0,4},{4,8},{8,12},{12,0},{1,5},{5,9},{9,13},{13,1},{2,6},{6,10},{... | collective-permute-start | bytes 1161224 | tf_op jit(solution)/shard_map/ppermute | solution.py:209
  43.9 1.6 %collective-permute-start.14 = (bf16[21,24,384]{2,1,0:T(8,128)(2,1)S(1)}, bf16[21,24,384]{2,1,0:T(8,128)(2,1)S(1)}, u32[]{:S(2)}, u32[]{:S(2)}) collective-permute-start(bf16[21,24,384]{2,1,0:T(8,128)(2,1)S(1)} %pad_maximum_fusion.4), channel_id=1, source_target_pairs={{0,12},{4,0},{8,4},{12,8},{1,13},{5,1},{9,5},{13,9},{2,14},{6,2},{... | collective-permute-start | bytes 1161224 | tf_op jit(solution)/shard_map/ppermute | solution.py:209
  45.4 6.6 %shard_map.47.acc_ref = f32[4,512,192]{2,1,0:T(8,128)S(1)} custom-call(s32[3]{0:T(128)S(1)} %pad_add_fusion.ids_ref, bf16[6,576,1152]{2,1,0:T(8,128)(2,1)S(1)} %shard_map.46.x_ref, bf16[14,192,384]{2,1,0:T(8,128)(2,1)S(1)} %bitcast.87), custom_call_target="tpu_custom_call" | custom-call | flops 5000000000 | bytes 8000000 | tf_op jit(solution)/shard_map/pallas_call | solution.py:119
  52.8 7.4 %shard_map.48 = (f32[2,512,256]{2,1,0:T(8,128)}, f32[2,512,192]{2,1,0:T(8,128)S(1)}, f32[16,1,384]{2,1,0:T(1,128)}) custom-call(s32[3]{0:T(128)S(1)} %pad_add_fusion.ids_ref, bf16[6,576,1152]{2,1,0:T(8,128)(2,1)S(1)} %shard_map.46.x_ref, bf16[14,192,384]{2,1,0:T(8,128)(2,1)S(1)} %bitcast.86, f32[4,512,192]{2,1,0:T(8,128)S(1)} %shard_map.47.acc_ref), custom_call_target="tpu_custom_call" | custom-call | flops 5000000000 | bytes 8000000 | tf_op jit(solution)/shard_map/pallas_call | solution.py:128
  60.2 3.3 %collective-permute-start.15 = (f32[2,512,256]{2,1,0:T(8,128)}, f32[2,512,256]{2,1,0:T(8,128)S(1)}, u32[]{:S(2)}, u32[]{:S(2)}) collective-permute-start(f32[2,512,256]{2,1,0:T(8,128)} %get-tuple-element.23), channel_id=1, source_target_pairs={{0,1},{1,0},{2,3},{3,2},{4,5},{5,4},{6,7},{7,6},{8,9},{9,8},{10,11... | collective-permute-start | bytes 3145736 | tf_op jit(solution)/shard_map/ppermute | solution.py:270
  63.5 6.1 %all-to-all-start = ((f32[16,1,384]{2,1,0:T(1,128)}), f32[16,1,384]{2,1,0:T(1,128)S(1)}, u32[]{:S(2)}, u32[]{:S(2)}) async-start(f32[16,1,384]{2,1,0:T(1,128)} %get-tuple-element.24), calls=%async_computation | async-start | bytes 49152 | tf_op jit(solution)/shard_map/all_to_all | solution.py:271
  69.8 5.6 %all-to-all-done.stats_ref = f32[16,1,384]{2,1,0:T(1,128)S(1)} async-done(((f32[16,1,384]{2,1,0:T(1,128)}), f32[16,1,384]{2,1,0:T(1,128)S(1)}, u32[]{:S(2)}, u32[]{:S(2)}) %all-to-all-start) | async-done | bytes 24608 | tf_op jit(solution)/shard_map/all_to_all | solution.py:271
  75.4 2.0 %shard_map.49 = bf16[2,512,384]{2,1,0:T(8,128)(2,1)} custom-call(s32[3]{0:T(128)S(1)} %pad_add_fusion.ids_ref, f32[2,512,192]{2,1,0:T(8,128)S(1)} %get-tuple-element.22.keep_ref, f32[2,512,256]{2,1,0:T(8,128)S(1)} %collective-permute-done.15.recv_ref, f32[16,1,384]{2,1,0:T(1,128)S(1)} %all-to-all-done.stats_ref, f32[2,1,192]{2,1,0:T(1,128)S(1)} %reshape.21.gain_ref, ...), custom_call_target="tpu_custom_call" | custom-call | flops 4000000 | bytes 3000000 | tf_op jit(solution)/shard_map/pallas_call | solution.py:166
  (57 shorter events, 2.7 us)
Async XLA Ops:
  0.0 1.0 %copy-start = (bf16[3,3,3,384,24]{3,4,2,1,0:T(8,128)(2,1)S(1)}, bf16[3,3,3,384,24]{3,4,2,1,0:T(8,128)(2,1)}, u32[]{:S(2)}) copy-start(bf16[3,3,3,384,24]{3,4,2,1,0:T(8,128)(2,1)} %param.5) | copy-start | bytes 1492996
  1.1 16.0 %collective-permute-start = (bf16[14,24,384]{2,1,0:T(8,128)(2,1)S(1)}, bf16[14,24,384]{2,1,0:T(8,128)(2,1)S(1)}, u32[]{:S(2)}, u32[]{:S(2)}) collective-permute-start(bf16[14,24,384]{2,1,0:T(8,128)(2,1)S(1)} %constant_dynamic-slice_fusion.1), channel_id=1, source_target_pairs={{0,16},{1,146},{2,18},{3,144},{128,19},{129,145},{130,17},{131,147... | collective-permute-start | bytes 774152 | tf_op jit(solution)/shard_map/ppermute | solution.py:204
  6.4 10.7 %collective-permute-start.4 = (bf16[14,24,384]{2,1,0:T(8,128)(2,1)S(1)}, bf16[14,24,384]{2,1,0:T(8,128)(2,1)S(1)}, u32[]{:S(2)}, u32[]{:S(2)}) collective-permute-start(bf16[14,24,384]{2,1,0:T(8,128)(2,1)S(1)} %constant_dynamic-slice_fusion.1), channel_id=1, source_target_pairs={{0,112},{1,242},{2,114},{3,240},{128,115},{129,241},{130,113},{131... | collective-permute-start | bytes 774152 | tf_op jit(solution)/shard_map/ppermute | solution.py:204
  10.4 9.7 %collective-permute-start.10 = (bf16[14,24,384]{2,1,0:T(8,128)(2,1)S(1)}, bf16[14,24,384]{2,1,0:T(8,128)(2,1)S(1)}, u32[]{:S(2)}, u32[]{:S(2)}) collective-permute-start(bf16[14,24,384]{2,1,0:T(8,128)(2,1)S(1)} %constant_dynamic-slice_fusion.1), channel_id=1, source_target_pairs={{0,0},{1,130},{2,2},{3,128},{128,3},{129,129},{130,1},{131,131},{1... | collective-permute-start | bytes 774152 | tf_op jit(solution)/shard_map/ppermute | solution.py:204
  13.4 11.4 %copy-start.1 = (bf16[1,2,16,32,384]{4,3,2,1,0:T(8,128)(2,1)S(1)}, bf16[1,2,16,32,384]{4,3,2,1,0:T(8,128)(2,1)}, u32[]{:S(2)}) copy-start(bf16[1,2,16,32,384]{4,3,2,1,0:T(8,128)(2,1)} %param.4) | copy-start | bytes 2359300
  13.4 11.4 %collective-permute-start.8 = (bf16[1,512,384]{2,1,0:T(8,128)(2,1)S(1)}, bf16[1,512,384]{2,1,0:T(8,128)(2,1)S(1)}, u32[]{:S(2)}, u32[]{:S(2)}) collective-permute-start(bf16[1,512,384]{2,1,0:T(8,128)(2,1)S(1)} %constant_dynamic-slice_fusion), channel_id=1, source_target_pairs={{1,2},{2,1},{3,4},{4,3},{5,6},{6,5},{7,8},{8,7},{9,10},{10,9},{11,... | collective-permute-start | bytes 1179656 | tf_op jit(solution)/shard_map/ppermute | solution.py:183
  17.0 7.9 %collective-permute-start.1 = (bf16[14,24,384]{2,1,0:T(8,128)(2,1)S(1)}, bf16[14,24,384]{2,1,0:T(8,128)(2,1)S(1)}, u32[]{:S(2)}, u32[]{:S(2)}) collective-permute-start(bf16[14,24,384]{2,1,0:T(8,128)(2,1)S(1)} %collective-permute-done), channel_id=1, source_target_pairs={{0,16},{16,32},{32,48},{48,64},{64,80},{80,96},{96,112},{112,0},{1... | collective-permute-start | bytes 774152 | tf_op jit(solution)/shard_map/ppermute | solution.py:209
  17.1 10.6 %collective-permute-start.5 = (bf16[14,24,384]{2,1,0:T(8,128)(2,1)S(1)}, bf16[14,24,384]{2,1,0:T(8,128)(2,1)S(1)}, u32[]{:S(2)}, u32[]{:S(2)}) collective-permute-start(bf16[14,24,384]{2,1,0:T(8,128)(2,1)S(1)} %collective-permute-done.4), channel_id=1, source_target_pairs={{0,112},{16,0},{32,16},{48,32},{64,48},{80,64},{96,80},{112,96},{1... | collective-permute-start | bytes 774152 | tf_op jit(solution)/shard_map/ppermute | solution.py:209
  24.9 14.7 %collective-permute-start.9 = (bf16[3,512,384]{2,1,0:T(8,128)(2,1)S(1)}, bf16[3,512,384]{2,1,0:T(8,128)(2,1)S(1)}, u32[]{:S(2)}, u32[]{:S(2)}) collective-permute-start(bf16[3,512,384]{2,1,0:T(8,128)(2,1)S(1)} %pad_maximum_fusion), channel_id=1, source_target_pairs={{0,1},{1,0},{2,3},{3,2},{4,5},{5,4},{6,7},{7,6},{8,9},{9,8},{10,11... | collective-permute-start | bytes 3538952 | tf_op jit(solution)/shard_map/ppermute | solution.py:185
  25.1 26.9 %collective-permute-start.11 = (bf16[3,14,24,384]{3,2,1,0:T(8,128)(2,1)S(1)}, bf16[3,14,24,384]{3,2,1,0:T(8,128)(2,1)S(1)}, u32[]{:S(2)}, u32[]{:S(2)}) collective-permute-start(bf16[3,14,24,384]{3,2,1,0:T(8,128)(2,1)S(1)} %pad_maximum_fusion.1), channel_id=1, source_target_pairs={{0,2},{2,128},{128,130},{130,0},{1,3},{3,129},{129,131},{131,1},{4... | collective-permute-start | bytes 2322440 | tf_op jit(solution)/shard_map/ppermute | solution.py:209
  27.8 24.2 %collective-permute-start.12 = (bf16[2,14,24,384]{3,2,1,0:T(8,128)(2,1)S(1)}, bf16[2,14,24,384]{3,2,1,0:T(8,128)(2,1)S(1)}, u32[]{:S(2)}, u32[]{:S(2)}) collective-permute-start(bf16[2,14,24,384]{3,2,1,0:T(8,128)(2,1)S(1)} %pad_maximum_fusion.2), channel_id=1, source_target_pairs={{0,130},{2,0},{128,2},{130,128},{1,131},{3,1},{129,3},{131,129},{4... | collective-permute-start | bytes 1548296 | tf_op jit(solution)/shard_map/ppermute | solution.py:209
  28.5 8.0 %collective-permute-start.2 = (bf16[14,24,384]{2,1,0:T(8,128)(2,1)S(1)}, bf16[14,24,384]{2,1,0:T(8,128)(2,1)S(1)}, u32[]{:S(2)}, u32[]{:S(2)}) collective-permute-start(bf16[14,24,384]{2,1,0:T(8,128)(2,1)S(1)} %collective-permute-done.1), channel_id=1, source_target_pairs={{0,16},{16,32},{32,48},{48,64},{64,80},{80,96},{96,112},{112,0},{1... | collective-permute-start | bytes 774152 | tf_op jit(solution)/shard_map/ppermute | solution.py:209
  28.5 8.1 %collective-permute-start.6 = (bf16[14,24,384]{2,1,0:T(8,128)(2,1)S(1)}, bf16[14,24,384]{2,1,0:T(8,128)(2,1)S(1)}, u32[]{:S(2)}, u32[]{:S(2)}) collective-permute-start(bf16[14,24,384]{2,1,0:T(8,128)(2,1)S(1)} %collective-permute-done.5), channel_id=1, source_target_pairs={{0,112},{16,0},{32,16},{48,32},{64,48},{80,64},{96,80},{112,96},{1... | collective-permute-start | bytes 774152 | tf_op jit(solution)/shard_map/ppermute | solution.py:209
  36.6 5.5 %collective-permute-start.3 = (bf16[7,24,384]{2,1,0:T(8,128)(2,1)S(1)}, bf16[7,24,384]{2,1,0:T(8,128)(2,1)S(1)}, u32[]{:S(2)}, u32[]{:S(2)}) collective-permute-start(bf16[7,24,384]{2,1,0:T(8,128)(2,1)S(1)} %slice.52), channel_id=1, source_target_pairs={{0,16},{16,32},{32,48},{48,64},{64,80},{80,96},{96,112},{112,0},{1... | collective-permute-start | bytes 387080 | tf_op jit(solution)/shard_map/ppermute | solution.py:209
  36.7 5.3 %collective-permute-start.7 = (bf16[7,24,384]{2,1,0:T(8,128)(2,1)S(1)}, bf16[7,24,384]{2,1,0:T(8,128)(2,1)S(1)}, u32[]{:S(2)}, u32[]{:S(2)}) collective-permute-start(bf16[7,24,384]{2,1,0:T(8,128)(2,1)S(1)} %slice.53), channel_id=1, source_target_pairs={{0,112},{16,0},{32,16},{48,32},{64,48},{80,64},{96,80},{112,96},{1... | collective-permute-start | bytes 387080 | tf_op jit(solution)/shard_map/ppermute | solution.py:209
  42.1 9.9 %collective-permute-start.13 = (bf16[21,24,384]{2,1,0:T(8,128)(2,1)S(1)}, bf16[21,24,384]{2,1,0:T(8,128)(2,1)S(1)}, u32[]{:S(2)}, u32[]{:S(2)}) collective-permute-start(bf16[21,24,384]{2,1,0:T(8,128)(2,1)S(1)} %pad_maximum_fusion.3), channel_id=1, source_target_pairs={{0,4},{4,8},{8,12},{12,0},{1,5},{5,9},{9,13},{13,1},{2,6},{6,10},{... | collective-permute-start | bytes 1161224 | tf_op jit(solution)/shard_map/ppermute | solution.py:209
  43.9 8.2 %collective-permute-start.14 = (bf16[21,24,384]{2,1,0:T(8,128)(2,1)S(1)}, bf16[21,24,384]{2,1,0:T(8,128)(2,1)S(1)}, u32[]{:S(2)}, u32[]{:S(2)}) collective-permute-start(bf16[21,24,384]{2,1,0:T(8,128)(2,1)S(1)} %pad_maximum_fusion.4), channel_id=1, source_target_pairs={{0,12},{4,0},{8,4},{12,8},{1,13},{5,1},{9,5},{13,9},{2,14},{6,2},{... | collective-permute-start | bytes 1161224 | tf_op jit(solution)/shard_map/ppermute | solution.py:209
  52.8 16.8 %copy-start.2 = (f32[384]{0:T(512)S(1)}, f32[384]{0:T(512)}, u32[]{:S(2)}) copy-start(f32[384]{0:T(512)} %param.6) | copy-start | bytes 4612
  52.8 16.9 %copy-start.3 = (f32[384]{0:T(512)S(1)}, f32[384]{0:T(512)}, u32[]{:S(2)}) copy-start(f32[384]{0:T(512)} %param.7) | copy-start | bytes 4612
  60.2 15.2 %collective-permute-start.15 = (f32[2,512,256]{2,1,0:T(8,128)}, f32[2,512,256]{2,1,0:T(8,128)S(1)}, u32[]{:S(2)}, u32[]{:S(2)}) collective-permute-start(f32[2,512,256]{2,1,0:T(8,128)} %get-tuple-element.23), channel_id=1, source_target_pairs={{0,1},{1,0},{2,3},{3,2},{4,5},{5,4},{6,7},{7,6},{8,9},{9,8},{10,11... | collective-permute-start | bytes 3145736 | tf_op jit(solution)/shard_map/ppermute | solution.py:270
  63.5 11.9 %all-to-all-start = ((f32[16,1,384]{2,1,0:T(1,128)}), f32[16,1,384]{2,1,0:T(1,128)S(1)}, u32[]{:S(2)}, u32[]{:S(2)}) async-start(f32[16,1,384]{2,1,0:T(1,128)} %get-tuple-element.24), calls=%async_computation | async-start | bytes 49152 | tf_op jit(solution)/shard_map/all_to_all | solution.py:271

commit v6 on v5

--- a/solution.py
+++ b/solution.py
@@ -25,24 +25,25 @@
 
 
 def widen_kernel(x_ref, o_ref, *, width):
-    x = x_ref[0]
-    rows, chans = x.shape
-    zero = jnp.zeros((width, 3 * chans), o_ref.dtype)
-    o_ref[0, 0:width, :] = zero
-    o_ref[0, width + rows : 2 * width + rows, :] = zero
-    wide = x.astype(jnp.float32)
-    o_ref[0, width : width + rows, 0:chans] = shift_rows(wide, 1, width).astype(o_ref.dtype)
-    o_ref[0, width : width + rows, chans : 2 * chans] = x
-    o_ref[0, width : width + rows, 2 * chans : 3 * chans] = shift_rows(wide, -1, width).astype(o_ref.dtype)
+    for n in range(x_ref.shape[0]):
+        x = x_ref[n]
+        rows, chans = x.shape
+        zero = jnp.zeros((width, 3 * chans), o_ref.dtype)
+        o_ref[n, 0:width, :] = zero
+        o_ref[n, width + rows : 2 * width + rows, :] = zero
+        wide = x.astype(jnp.float32)
+        o_ref[n, width : width + rows, 0:chans] = shift_rows(wide, 1, width).astype(o_ref.dtype)
+        o_ref[n, width : width + rows, chans : 2 * chans] = x
+        o_ref[n, width : width + rows, 2 * chans : 3 * chans] = shift_rows(wide, -1, width).astype(o_ref.dtype)
 
 
 def widen(planes, width):
     count, rows, chans = planes.shape
     return pl.pallas_call(
         functools.partial(widen_kernel, width=width),
-        grid=(count,),
-        in_specs=[pl.BlockSpec((1, rows, chans), lambda i: (i, 0, 0))],
-        out_specs=pl.BlockSpec((1, rows + 2 * width, 3 * chans), lambda i: (i, 0, 0)),
+        grid=(count // 3,),
+        in_specs=[pl.BlockSpec((3, rows, chans), lambda i: (i, 0, 0))],
+        out_specs=pl.BlockSpec((3, rows + 2 * width, 3 * chans), lambda i: (i, 0, 0)),
         out_shape=jax.ShapeDtypeStruct((count, rows + 2 * width, 3 * chans), planes.dtype),
         compiler_params=pltpu.CompilerParams(vmem_limit_bytes=32 << 20),
         cost_estimate=pl.CostEstimate(flops=0, bytes_accessed=12_000_000, transcendentals=0),

time: 77.7 us -> 77.7 us (level)
  transfers between devices with their start and end apart: 17 -> 17, of which waited for: 5 -> 6; matrix products, arithmetic and copies ran while one was open for 4% -> 4% of each run, Pallas kernels for 11% -> 10%
where the time goes in v6:
time: 77.7 us; the launch traced here: 77.4 us
  starting transfers between devices  37.8 us (49%)
  Pallas kernels  17.2 us (22%)
  waiting for transfers between devices  16.9 us (22%)
  local copies, waits for them, and re-layouts  3.78 us (5%)
  other arithmetic  1.19 us (2%)
    ppermute x10, starting transfers between devices, ring(): lax.ppermute(array, axes, [(i, (i + by) % count) for i in range(count)])  15 us
    ppermute x3, starting transfers between devices, from_z(): return lax.ppermute(array, ('xh', 'z', 'xl', 'c'), perm)  11.2 us
    pallas_call x1, Pallas kernels, second_conv(): in_vmem(kernel, 3, out, scratch, 5 * 10 ** 9, 40)(ids, wide, other, acc)  7.4 us
    pallas_call x1, Pallas kernels, first_conv(): return in_vmem(kernel, 2, out, [], 5 * 10 ** 9, 40)(ids, wide, own)[0]  6.38 us
    all_to_all x1, starting transfers between devices, local(): everyone = lax.all_to_all(stats, DEPTH, 0, 0, tiled=True)  6 us
    all_to_all x1, waiting for transfers between devices, local(): everyone = lax.all_to_all(stats, DEPTH, 0, 0, tiled=True)  5.62 us
    ppermute x10, waiting for transfers between devices, ring(): lax.ppermute(array, axes, [(i, (i + by) % count) for i in range(count)])  5.39 us
    ppermute x1, waiting for transfers between devices, chip_planes(): halo = lax.ppermute(edge, DEPTH, pairs)  4.21 us
  transfers between devices with their start and end apart: 17, of which 6 were waited for; matrix products, arithmetic and copies ran while one was open for 4% of the time, Pallas kernels for 10%

profile of v6, /device:TPU:1, one launch (start us, length us, event | category | flops | bytes accessed | tf_op | source)
XLA Modules:
  0.0 77.4 jit_solution(417944050657028613)
XLA Ops:
  0.0 1.0 %copy-done = bf16[3,3,3,384,24]{3,4,2,1,0:T(8,128)(2,1)S(1)} copy-done((bf16[3,3,3,384,24]{3,4,2,1,0:T(8,128)(2,1)S(1)}, bf16[3,3,3,384,24]{3,4,2,1,0:T(8,128)(2,1)}, u32[]{:S(2)}) %copy-start) | copy-done | bytes 497688
  1.1 5.3 %collective-permute-start = (bf16[14,24,384]{2,1,0:T(8,128)(2,1)S(1)}, bf16[14,24,384]{2,1,0:T(8,128)(2,1)S(1)}, u32[]{:S(2)}, u32[]{:S(2)}) collective-permute-start(bf16[14,24,384]{2,1,0:T(8,128)(2,1)S(1)} %constant_dynamic-slice_fusion.1), channel_id=1, source_target_pairs={{0,16},{1,146},{2,18},{3,144},{128,19},{129,145},{130,17},{131,147... | collective-permute-start | bytes 774152 | tf_op jit(solution)/shard_map/ppermute | solution.py:205
  6.4 4.0 %collective-permute-start.4 = (bf16[14,24,384]{2,1,0:T(8,128)(2,1)S(1)}, bf16[14,24,384]{2,1,0:T(8,128)(2,1)S(1)}, u32[]{:S(2)}, u32[]{:S(2)}) collective-permute-start(bf16[14,24,384]{2,1,0:T(8,128)(2,1)S(1)} %constant_dynamic-slice_fusion.1), channel_id=1, source_target_pairs={{0,112},{1,242},{2,114},{3,240},{128,115},{129,241},{130,113},{131... | collective-permute-start | bytes 774152 | tf_op jit(solution)/shard_map/ppermute | solution.py:205
  10.4 1.9 %collective-permute-start.10 = (bf16[14,24,384]{2,1,0:T(8,128)(2,1)S(1)}, bf16[14,24,384]{2,1,0:T(8,128)(2,1)S(1)}, u32[]{:S(2)}, u32[]{:S(2)}) collective-permute-start(bf16[14,24,384]{2,1,0:T(8,128)(2,1)S(1)} %constant_dynamic-slice_fusion.1), channel_id=1, source_target_pairs={{0,0},{1,130},{2,2},{3,128},{128,3},{129,129},{130,1},{131,131},{1... | collective-permute-start | bytes 774152 | tf_op jit(solution)/shard_map/ppermute | solution.py:205
  12.3 1.0 %constant_dynamic-slice_fusion = bf16[1,512,384]{2,1,0:T(8,128)(2,1)S(1)} fusion(bf16[2,512,384]{2,1,0:T(8,128)(2,1)} %bitcast.88, s32[]{:T(128)S(6)} %select_n.119), kind=kLoop, calls=%fused_computation.24 | loop fusion | bytes 786436 | tf_op jit(solution)/shard_map/dynamic_slice | solution.py:183
  13.4 2.1 %collective-permute-start.8 = (bf16[1,512,384]{2,1,0:T(8,128)(2,1)S(1)}, bf16[1,512,384]{2,1,0:T(8,128)(2,1)S(1)}, u32[]{:S(2)}, u32[]{:S(2)}) collective-permute-start(bf16[1,512,384]{2,1,0:T(8,128)(2,1)S(1)} %constant_dynamic-slice_fusion), channel_id=1, source_target_pairs={{1,2},{2,1},{3,4},{4,3},{5,6},{6,5},{7,8},{8,7},{9,10},{10,9},{11,... | collective-permute-start | bytes 1179656 | tf_op jit(solution)/shard_map/ppermute | solution.py:184
  15.6 1.4 %collective-permute-done = bf16[14,24,384]{2,1,0:T(8,128)(2,1)S(1)} collective-permute-done((bf16[14,24,384]{2,1,0:T(8,128)(2,1)S(1)}, bf16[14,24,384]{2,1,0:T(8,128)(2,1)S(1)}, u32[]{:S(2)}, u32[]{:S(2)}) %collective-permute-start) | collective-permute-done | bytes 258080 | tf_op jit(solution)/shard_map/ppermute | solution.py:205
  17.1 2.7 %collective-permute-start.5 = (bf16[14,24,384]{2,1,0:T(8,128)(2,1)S(1)}, bf16[14,24,384]{2,1,0:T(8,128)(2,1)S(1)}, u32[]{:S(2)}, u32[]{:S(2)}) collective-permute-start(bf16[14,24,384]{2,1,0:T(8,128)(2,1)S(1)} %collective-permute-done.4), channel_id=1, source_target_pairs={{0,112},{16,0},{32,16},{48,32},{64,48},{80,64},{96,80},{112,96},{1... | collective-permute-start | bytes 774152 | tf_op jit(solution)/shard_map/ppermute | solution.py:210
  20.5 4.2 %collective-permute-done.8 = bf16[1,512,384]{2,1,0:T(8,128)(2,1)S(1)} collective-permute-done((bf16[1,512,384]{2,1,0:T(8,128)(2,1)S(1)}, bf16[1,512,384]{2,1,0:T(8,128)(2,1)S(1)}, u32[]{:S(2)}, u32[]{:S(2)}) %collective-permute-start.8) | collective-permute-done | bytes 393248 | tf_op jit(solution)/shard_map/ppermute | solution.py:184
  25.1 2.6 %collective-permute-start.11 = (bf16[3,14,24,384]{3,2,1,0:T(8,128)(2,1)S(1)}, bf16[3,14,24,384]{3,2,1,0:T(8,128)(2,1)S(1)}, u32[]{:S(2)}, u32[]{:S(2)}) collective-permute-start(bf16[3,14,24,384]{3,2,1,0:T(8,128)(2,1)S(1)} %pad_maximum_fusion.1), channel_id=1, source_target_pairs={{0,2},{2,128},{128,130},{130,0},{1,3},{3,129},{129,131},{131,1},{4... | collective-permute-start | bytes 2322440 | tf_op jit(solution)/shard_map/ppermute | solution.py:210
  27.8 0.7 collective-permute-start.12
  28.5 2.7 %collective-permute-start.6 = (bf16[14,24,384]{2,1,0:T(8,128)(2,1)S(1)}, bf16[14,24,384]{2,1,0:T(8,128)(2,1)S(1)}, u32[]{:S(2)}, u32[]{:S(2)}) collective-permute-start(bf16[14,24,384]{2,1,0:T(8,128)(2,1)S(1)} %collective-permute-done.5), channel_id=1, source_target_pairs={{0,112},{16,0},{32,16},{48,32},{64,48},{80,64},{96,80},{112,96},{1... | collective-permute-start | bytes 774152 | tf_op jit(solution)/shard_map/ppermute | solution.py:210
  31.3 5.2 %collective-permute-done.2 = bf16[14,24,384]{2,1,0:T(8,128)(2,1)S(1)} collective-permute-done((bf16[14,24,384]{2,1,0:T(8,128)(2,1)S(1)}, bf16[14,24,384]{2,1,0:T(8,128)(2,1)S(1)}, u32[]{:S(2)}, u32[]{:S(2)}) %collective-permute-start.2) | collective-permute-done | bytes 258080 | tf_op jit(solution)/shard_map/ppermute | solution.py:210
  36.7 2.7 %collective-permute-start.7 = (bf16[7,24,384]{2,1,0:T(8,128)(2,1)S(1)}, bf16[7,24,384]{2,1,0:T(8,128)(2,1)S(1)}, u32[]{:S(2)}, u32[]{:S(2)}) collective-permute-start(bf16[7,24,384]{2,1,0:T(8,128)(2,1)S(1)} %slice.53), channel_id=1, source_target_pairs={{0,112},{16,0},{32,16},{48,32},{64,48},{80,64},{96,80},{112,96},{1... | collective-permute-start | bytes 387080 | tf_op jit(solution)/shard_map/ppermute | solution.py:210
  39.7 0.7 maximum_select_fusion.x_ref
  40.4 1.4 %shard_map.46.x_ref = bf16[6,576,1152]{2,1,0:T(8,128)(2,1)S(1)} custom-call(bf16[6,512,384]{2,1,0:T(8,128)(2,1)S(1)} %maximum_select_fusion.x_ref), custom_call_target="tpu_custom_call" | custom-call | bytes 12000000 | tf_op jit(solution)/shard_map/pallas_call | solution.py:42
  42.0 1.6 %collective-permute-start.13 = (bf16[21,24,384]{2,1,0:T(8,128)(2,1)S(1)}, bf16[21,24,384]{2,1,0:T(8,128)(2,1)S(1)}, u32[]{:S(2)}, u32[]{:S(2)}) collective-permute-start(bf16[21,24,384]{2,1,0:T(8,128)(2,1)S(1)} %pad_maximum_fusion.3), channel_id=1, source_target_pairs={{0,4},{4,8},{8,12},{12,0},{1,5},{5,9},{9,13},{13,1},{2,6},{6,10},{... | collective-permute-start | bytes 1161224 | tf_op jit(solution)/shard_map/ppermute | solution.py:210
  43.8 1.7 %collective-permute-start.14 = (bf16[21,24,384]{2,1,0:T(8,128)(2,1)S(1)}, bf16[21,24,384]{2,1,0:T(8,128)(2,1)S(1)}, u32[]{:S(2)}, u32[]{:S(2)}) collective-permute-start(bf16[21,24,384]{2,1,0:T(8,128)(2,1)S(1)} %pad_maximum_fusion.4), channel_id=1, source_target_pairs={{0,12},{4,0},{8,4},{12,8},{1,13},{5,1},{9,5},{13,9},{2,14},{6,2},{... | collective-permute-start | bytes 1161224 | tf_op jit(solution)/shard_map/ppermute | solution.py:210
  45.5 6.4 %shard_map.47.acc_ref = f32[4,512,192]{2,1,0:T(8,128)S(1)} custom-call(s32[3]{0:T(128)S(1)} %pad_add_fusion.ids_ref, bf16[6,576,1152]{2,1,0:T(8,128)(2,1)S(1)} %shard_map.46.x_ref, bf16[14,192,384]{2,1,0:T(8,128)(2,1)S(1)} %bitcast.87), custom_call_target="tpu_custom_call" | custom-call | flops 5000000000 | bytes 8000000 | tf_op jit(solution)/shard_map/pallas_call | solution.py:120
  52.7 7.4 %shard_map.48 = (f32[2,512,256]{2,1,0:T(8,128)}, f32[2,512,192]{2,1,0:T(8,128)S(1)}, f32[16,1,384]{2,1,0:T(1,128)}) custom-call(s32[3]{0:T(128)S(1)} %pad_add_fusion.ids_ref, bf16[6,576,1152]{2,1,0:T(8,128)(2,1)S(1)} %shard_map.46.x_ref, bf16[14,192,384]{2,1,0:T(8,128)(2,1)S(1)} %bitcast.86, f32[4,512,192]{2,1,0:T(8,128)S(1)} %shard_map.47.acc_ref), custom_call_target="tpu_custom_call" | custom-call | flops 5000000000 | bytes 8000000 | tf_op jit(solution)/shard_map/pallas_call | solution.py:129
  60.1 3.5 %collective-permute-start.15 = (f32[2,512,256]{2,1,0:T(8,128)}, f32[2,512,256]{2,1,0:T(8,128)S(1)}, u32[]{:S(2)}, u32[]{:S(2)}) collective-permute-start(f32[2,512,256]{2,1,0:T(8,128)} %get-tuple-element.23), channel_id=1, source_target_pairs={{0,1},{1,0},{2,3},{3,2},{4,5},{5,4},{6,7},{7,6},{8,9},{9,8},{10,11... | collective-permute-start | bytes 3145736 | tf_op jit(solution)/shard_map/ppermute | solution.py:271
  63.6 6.0 %all-to-all-start = ((f32[16,1,384]{2,1,0:T(1,128)}), f32[16,1,384]{2,1,0:T(1,128)S(1)}, u32[]{:S(2)}, u32[]{:S(2)}) async-start(f32[16,1,384]{2,1,0:T(1,128)} %get-tuple-element.24), calls=%async_computation | async-start | bytes 49152 | tf_op jit(solution)/shard_map/all_to_all | solution.py:272
  69.8 5.6 %all-to-all-done.stats_ref = f32[16,1,384]{2,1,0:T(1,128)S(1)} async-done(((f32[16,1,384]{2,1,0:T(1,128)}), f32[16,1,384]{2,1,0:T(1,128)S(1)}, u32[]{:S(2)}, u32[]{:S(2)}) %all-to-all-start) | async-done | bytes 24608 | tf_op jit(solution)/shard_map/all_to_all | solution.py:272
  75.4 2.0 %shard_map.49 = bf16[2,512,384]{2,1,0:T(8,128)(2,1)} custom-call(s32[3]{0:T(128)S(1)} %pad_add_fusion.ids_ref, f32[2,512,192]{2,1,0:T(8,128)S(1)} %get-tuple-element.22.keep_ref, f32[2,512,256]{2,1,0:T(8,128)S(1)} %collective-permute-done.15.recv_ref, f32[16,1,384]{2,1,0:T(1,128)S(1)} %all-to-all-done.stats_ref, f32[2,1,192]{2,1,0:T(1,128)S(1)} %reshape.21.gain_ref, ...), custom_call_target="tpu_custom_call" | custom-call | flops 4000000 | bytes 3000000 | tf_op jit(solution)/shard_map/pallas_call | solution.py:167
  (57 shorter events, 2.8 us)
Async XLA Ops:
  0.0 1.0 %copy-start = (bf16[3,3,3,384,24]{3,4,2,1,0:T(8,128)(2,1)S(1)}, bf16[3,3,3,384,24]{3,4,2,1,0:T(8,128)(2,1)}, u32[]{:S(2)}) copy-start(bf16[3,3,3,384,24]{3,4,2,1,0:T(8,128)(2,1)} %param.5) | copy-start | bytes 1492996
  1.1 16.0 %collective-permute-start = (bf16[14,24,384]{2,1,0:T(8,128)(2,1)S(1)}, bf16[14,24,384]{2,1,0:T(8,128)(2,1)S(1)}, u32[]{:S(2)}, u32[]{:S(2)}) collective-permute-start(bf16[14,24,384]{2,1,0:T(8,128)(2,1)S(1)} %constant_dynamic-slice_fusion.1), channel_id=1, source_target_pairs={{0,16},{1,146},{2,18},{3,144},{128,19},{129,145},{130,17},{131,147... | collective-permute-start | bytes 774152 | tf_op jit(solution)/shard_map/ppermute | solution.py:205
  6.4 10.7 %collective-permute-start.4 = (bf16[14,24,384]{2,1,0:T(8,128)(2,1)S(1)}, bf16[14,24,384]{2,1,0:T(8,128)(2,1)S(1)}, u32[]{:S(2)}, u32[]{:S(2)}) collective-permute-start(bf16[14,24,384]{2,1,0:T(8,128)(2,1)S(1)} %constant_dynamic-slice_fusion.1), channel_id=1, source_target_pairs={{0,112},{1,242},{2,114},{3,240},{128,115},{129,241},{130,113},{131... | collective-permute-start | bytes 774152 | tf_op jit(solution)/shard_map/ppermute | solution.py:205
  10.4 9.7 %collective-permute-start.10 = (bf16[14,24,384]{2,1,0:T(8,128)(2,1)S(1)}, bf16[14,24,384]{2,1,0:T(8,128)(2,1)S(1)}, u32[]{:S(2)}, u32[]{:S(2)}) collective-permute-start(bf16[14,24,384]{2,1,0:T(8,128)(2,1)S(1)} %constant_dynamic-slice_fusion.1), channel_id=1, source_target_pairs={{0,0},{1,130},{2,2},{3,128},{128,3},{129,129},{130,1},{131,131},{1... | collective-permute-start | bytes 774152 | tf_op jit(solution)/shard_map/ppermute | solution.py:205
  13.4 11.4 %copy-start.1 = (bf16[1,2,16,32,384]{4,3,2,1,0:T(8,128)(2,1)S(1)}, bf16[1,2,16,32,384]{4,3,2,1,0:T(8,128)(2,1)}, u32[]{:S(2)}) copy-start(bf16[1,2,16,32,384]{4,3,2,1,0:T(8,128)(2,1)} %param.4) | copy-start | bytes 2359300
  13.4 11.4 %collective-permute-start.8 = (bf16[1,512,384]{2,1,0:T(8,128)(2,1)S(1)}, bf16[1,512,384]{2,1,0:T(8,128)(2,1)S(1)}, u32[]{:S(2)}, u32[]{:S(2)}) collective-permute-start(bf16[1,512,384]{2,1,0:T(8,128)(2,1)S(1)} %constant_dynamic-slice_fusion), channel_id=1, source_target_pairs={{1,2},{2,1},{3,4},{4,3},{5,6},{6,5},{7,8},{8,7},{9,10},{10,9},{11,... | collective-permute-start | bytes 1179656 | tf_op jit(solution)/shard_map/ppermute | solution.py:184
  17.0 7.9 %collective-permute-start.1 = (bf16[14,24,384]{2,1,0:T(8,128)(2,1)S(1)}, bf16[14,24,384]{2,1,0:T(8,128)(2,1)S(1)}, u32[]{:S(2)}, u32[]{:S(2)}) collective-permute-start(bf16[14,24,384]{2,1,0:T(8,128)(2,1)S(1)} %collective-permute-done), channel_id=1, source_target_pairs={{0,16},{16,32},{32,48},{48,64},{64,80},{80,96},{96,112},{112,0},{1... | collective-permute-start | bytes 774152 | tf_op jit(solution)/shard_map/ppermute | solution.py:210
  17.1 10.6 %collective-permute-start.5 = (bf16[14,24,384]{2,1,0:T(8,128)(2,1)S(1)}, bf16[14,24,384]{2,1,0:T(8,128)(2,1)S(1)}, u32[]{:S(2)}, u32[]{:S(2)}) collective-permute-start(bf16[14,24,384]{2,1,0:T(8,128)(2,1)S(1)} %collective-permute-done.4), channel_id=1, source_target_pairs={{0,112},{16,0},{32,16},{48,32},{64,48},{80,64},{96,80},{112,96},{1... | collective-permute-start | bytes 774152 | tf_op jit(solution)/shard_map/ppermute | solution.py:210
  24.9 14.7 %collective-permute-start.9 = (bf16[3,512,384]{2,1,0:T(8,128)(2,1)S(1)}, bf16[3,512,384]{2,1,0:T(8,128)(2,1)S(1)}, u32[]{:S(2)}, u32[]{:S(2)}) collective-permute-start(bf16[3,512,384]{2,1,0:T(8,128)(2,1)S(1)} %pad_maximum_fusion), channel_id=1, source_target_pairs={{0,1},{1,0},{2,3},{3,2},{4,5},{5,4},{6,7},{7,6},{8,9},{9,8},{10,11... | collective-permute-start | bytes 3538952 | tf_op jit(solution)/shard_map/ppermute | solution.py:186
  25.1 26.8 %collective-permute-start.11 = (bf16[3,14,24,384]{3,2,1,0:T(8,128)(2,1)S(1)}, bf16[3,14,24,384]{3,2,1,0:T(8,128)(2,1)S(1)}, u32[]{:S(2)}, u32[]{:S(2)}) collective-permute-start(bf16[3,14,24,384]{3,2,1,0:T(8,128)(2,1)S(1)} %pad_maximum_fusion.1), channel_id=1, source_target_pairs={{0,2},{2,128},{128,130},{130,0},{1,3},{3,129},{129,131},{131,1},{4... | collective-permute-start | bytes 2322440 | tf_op jit(solution)/shard_map/ppermute | solution.py:210
  27.8 24.1 %collective-permute-start.12 = (bf16[2,14,24,384]{3,2,1,0:T(8,128)(2,1)S(1)}, bf16[2,14,24,384]{3,2,1,0:T(8,128)(2,1)S(1)}, u32[]{:S(2)}, u32[]{:S(2)}) collective-permute-start(bf16[2,14,24,384]{3,2,1,0:T(8,128)(2,1)S(1)} %pad_maximum_fusion.2), channel_id=1, source_target_pairs={{0,130},{2,0},{128,2},{130,128},{1,131},{3,1},{129,3},{131,129},{4... | collective-permute-start | bytes 1548296 | tf_op jit(solution)/shard_map/ppermute | solution.py:210
  28.5 8.0 %collective-permute-start.2 = (bf16[14,24,384]{2,1,0:T(8,128)(2,1)S(1)}, bf16[14,24,384]{2,1,0:T(8,128)(2,1)S(1)}, u32[]{:S(2)}, u32[]{:S(2)}) collective-permute-start(bf16[14,24,384]{2,1,0:T(8,128)(2,1)S(1)} %collective-permute-done.1), channel_id=1, source_target_pairs={{0,16},{16,32},{32,48},{48,64},{64,80},{80,96},{96,112},{112,0},{1... | collective-permute-start | bytes 774152 | tf_op jit(solution)/shard_map/ppermute | solution.py:210
  28.5 8.1 %collective-permute-start.6 = (bf16[14,24,384]{2,1,0:T(8,128)(2,1)S(1)}, bf16[14,24,384]{2,1,0:T(8,128)(2,1)S(1)}, u32[]{:S(2)}, u32[]{:S(2)}) collective-permute-start(bf16[14,24,384]{2,1,0:T(8,128)(2,1)S(1)} %collective-permute-done.5), channel_id=1, source_target_pairs={{0,112},{16,0},{32,16},{48,32},{64,48},{80,64},{96,80},{112,96},{1... | collective-permute-start | bytes 774152 | tf_op jit(solution)/shard_map/ppermute | solution.py:210
  36.6 5.4 %collective-permute-start.3 = (bf16[7,24,384]{2,1,0:T(8,128)(2,1)S(1)}, bf16[7,24,384]{2,1,0:T(8,128)(2,1)S(1)}, u32[]{:S(2)}, u32[]{:S(2)}) collective-permute-start(bf16[7,24,384]{2,1,0:T(8,128)(2,1)S(1)} %slice.52), channel_id=1, source_target_pairs={{0,16},{16,32},{32,48},{48,64},{64,80},{80,96},{96,112},{112,0},{1... | collective-permute-start | bytes 387080 | tf_op jit(solution)/shard_map/ppermute | solution.py:210
  36.7 5.3 %collective-permute-start.7 = (bf16[7,24,384]{2,1,0:T(8,128)(2,1)S(1)}, bf16[7,24,384]{2,1,0:T(8,128)(2,1)S(1)}, u32[]{:S(2)}, u32[]{:S(2)}) collective-permute-start(bf16[7,24,384]{2,1,0:T(8,128)(2,1)S(1)} %slice.53), channel_id=1, source_target_pairs={{0,112},{16,0},{32,16},{48,32},{64,48},{80,64},{96,80},{112,96},{1... | collective-permute-start | bytes 387080 | tf_op jit(solution)/shard_map/ppermute | solution.py:210
  42.0 9.9 %collective-permute-start.13 = (bf16[21,24,384]{2,1,0:T(8,128)(2,1)S(1)}, bf16[21,24,384]{2,1,0:T(8,128)(2,1)S(1)}, u32[]{:S(2)}, u32[]{:S(2)}) collective-permute-start(bf16[21,24,384]{2,1,0:T(8,128)(2,1)S(1)} %pad_maximum_fusion.3), channel_id=1, source_target_pairs={{0,4},{4,8},{8,12},{12,0},{1,5},{5,9},{9,13},{13,1},{2,6},{6,10},{... | collective-permute-start | bytes 1161224 | tf_op jit(solution)/shard_map/ppermute | solution.py:210
  43.8 8.2 %collective-permute-start.14 = (bf16[21,24,384]{2,1,0:T(8,128)(2,1)S(1)}, bf16[21,24,384]{2,1,0:T(8,128)(2,1)S(1)}, u32[]{:S(2)}, u32[]{:S(2)}) collective-permute-start(bf16[21,24,384]{2,1,0:T(8,128)(2,1)S(1)} %pad_maximum_fusion.4), channel_id=1, source_target_pairs={{0,12},{4,0},{8,4},{12,8},{1,13},{5,1},{9,5},{13,9},{2,14},{6,2},{... | collective-permute-start | bytes 1161224 | tf_op jit(solution)/shard_map/ppermute | solution.py:210
  52.7 16.9 %copy-start.2 = (f32[384]{0:T(512)S(1)}, f32[384]{0:T(512)}, u32[]{:S(2)}) copy-start(f32[384]{0:T(512)} %param.6) | copy-start | bytes 4612
  52.7 17.0 %copy-start.3 = (f32[384]{0:T(512)S(1)}, f32[384]{0:T(512)}, u32[]{:S(2)}) copy-start(f32[384]{0:T(512)} %param.7) | copy-start | bytes 4612
  60.1 15.3 %collective-permute-start.15 = (f32[2,512,256]{2,1,0:T(8,128)}, f32[2,512,256]{2,1,0:T(8,128)S(1)}, u32[]{:S(2)}, u32[]{:S(2)}) collective-permute-start(f32[2,512,256]{2,1,0:T(8,128)} %get-tuple-element.23), channel_id=1, source_target_pairs={{0,1},{1,0},{2,3},{3,2},{4,5},{5,4},{6,7},{7,6},{8,9},{9,8},{10,11... | collective-permute-start | bytes 3145736 | tf_op jit(solution)/shard_map/ppermute | solution.py:271
  63.6 11.8 %all-to-all-start = ((f32[16,1,384]{2,1,0:T(1,128)}), f32[16,1,384]{2,1,0:T(1,128)S(1)}, u32[]{:S(2)}, u32[]{:S(2)}) async-start(f32[16,1,384]{2,1,0:T(1,128)} %get-tuple-element.24), calls=%async_computation | async-start | bytes 49152 | tf_op jit(solution)/shard_map/all_to_all | solution.py:272
